TPU v7x, 512 devices: a whole 4x8x8 slice. The times are simulated.
512 devices in a mesh: sub: 32 (over z, y_hi, core), hgt: 16 (over y_lo, x).
Axes of the slice: x: 4, y: 8 (y_hi: 2, y_lo: 4; y = y_hi * 4 + y_lo), z: 8, core: 2. Of those that a mesh axis runs over, the one named last changes fastest.
Arguments:
- polar_beams: bfloat16 [16, 2, 512, 4096], P('hgt', None, 'sub'), may hold values from -6 to 6
- band_start: int32 [3, 2, 2, 16], replicated, may hold values from 0 to 8, as said below
- band_weight: bfloat16 [3, 2, 2, 16, 8], replicated, may hold values from -1.5 to 1.5
- phase_rate: float32 [3, 2, 2, 16], replicated, may hold values from -6 to 6
- layer_wave: float32 [16], P('hgt'), may hold values from 0.5 to 2
- beam_map: int32 [64, 2048], replicated, may hold values from 0 to 126, as said below
- range_map: int32 [64, 2048], replicated, may hold values from 0 to 4094
- pixel_frac: bfloat16 [3, 64, 2048], replicated, may hold values from 0 to 1
Outputs:
- image: float32 [64, 16, 2, 2048], P('sub', 'hgt')
Inputs may be any that keep to these rules, and one draw needn't show every extreme that they name: band_start[l,k,h,j] + t for t < 8 lies within h * 8 - 8 to h * 8 + 16 / 2 + 7. beam_map[y, x] differs from x * 128 // 2048 by at most 2.
All inputs are finite; a program needn't handle non-finite values.
Results may differ from a plain program's by a relative error of at most 0.0041.
Values may be sent and summed in bfloat16 or wider, within the bound.
No kernel may reach another device: no remote copies, remote signals or barrier semaphores. Data moves between devices by JAX's collectives and lax.ppermute only.
A program may use at most 192 MiB of HBM per device.

v0:
```python
import jax
import jax.numpy as jnp
from jax import lax
from jax.sharding import PartitionSpec as P

range_phase = 0.003


def from_partner(value, axis, bit):
    mask = 2**bit
    pairs = [(source, source ^ mask) for source in range(lax.axis_size(axis))]
    return lax.ppermute(value, axis, pairs)


def from_behind(block, axis, distance):
    devices = range(lax.axis_size(axis))
    route = [(i - distance, i) for i in devices if i - distance in devices]
    return lax.ppermute(block, axis, route)


def rotate(real_part, imag_part, angles):
    cosine = jnp.cos(angles)
    sine_part = jnp.sin(angles)
    return (cosine * real_part - sine_part * imag_part, sine_part * real_part + cosine * imag_part)


def band_matrix(starts, weights, first_row, row_total):
    col_ids = jnp.arange(row_total, dtype=jnp.int32) + first_row
    tap_ids = jnp.arange(weights.shape[-1], dtype=jnp.int32)
    matches = (col_ids[None, None, :] == starts[:, None, None] + tap_ids[None, :, None]).astype(
        jnp.float32
    )
    return jnp.einsum("jt,jtc->jc", weights.astype(jnp.float32), matches).astype(jnp.bfloat16)


def contribution(layer_beams, matrix, angles):
    blended = jnp.einsum("jc,zpcr->zpjr", matrix, layer_beams, preferred_element_type=jnp.float32)
    real_part, imag_part = rotate(blended[:, 0], blended[:, 1], angles)
    return jnp.stack([real_part, imag_part], axis=1)


def body(
    polar_beams, band_start, band_weight, phase_rate, layer_wave, beam_map, range_map, pixel_frac
):
    sub_index = lax.axis_index("sub")
    sub_count = lax.axis_size("sub")
    layer_count = polar_beams.shape[0]
    beam_count = polar_beams.shape[2]
    range_count = polar_beams.shape[3]
    levels = band_start.shape[0]
    column_count = beam_map.shape[1]
    range_pos = (jnp.arange(range_count, dtype=jnp.float32) + 0.5) / range_count

    def phase_angles(section, child, my_half):
        return (
            layer_wave[:, None, None]
            * phase_rate[section][child, my_half][None, :, None]
            * range_pos[None, None, :]
        )

    def merge_section(current, section):
        my_half = sub_index >> section & 1
        far_half = 1 - my_half
        own_part = contribution(
            current,
            band_matrix(
                band_start[section][my_half, my_half],
                band_weight[section][my_half, my_half],
                0,
                beam_count,
            ),
            phase_angles(section, my_half, my_half),
        )
        received = from_partner(current, "sub", section)
        first_row = 0
        far_part = contribution(
            received,
            band_matrix(
                band_start[section][far_half, my_half],
                band_weight[section][far_half, my_half],
                first_row,
                beam_count,
            ),
            phase_angles(section, far_half, my_half),
        )
        return own_part + far_part

    current = polar_beams
    for section in range(levels - 1):
        current = merge_section(current, section).astype(jnp.bfloat16)
    final_polar = merge_section(current, levels - 1)
    sector_idx = jnp.int32(0)
    for bit_idx in range(levels):
        sector_idx = sector_idx * 2 + (sub_index >> bit_idx & 1)
    sector_start = sector_idx * beam_count
    flat_polar = final_polar.reshape(layer_count, 2, beam_count * range_count)
    cols_per_beam = column_count // (beam_count * 2**levels)
    window = min(column_count, ((beam_count + 5) * cols_per_beam + 127) // 128 * 128)
    col_start = jnp.clip((sector_start - 3) * cols_per_beam, 0, column_count - window)
    tile_rows = beam_map.shape[0] // sub_count
    pixel_rows = tile_rows * lax.axis_size("sub")
    rows_beam = lax.dynamic_slice(beam_map, (0, col_start), (pixel_rows, window))
    rows_range = lax.dynamic_slice(range_map, (0, col_start), (pixel_rows, window))
    beam_frac = lax.dynamic_slice(pixel_frac[0], (0, col_start), (pixel_rows, window)).astype(
        jnp.float32
    )
    range_frac = lax.dynamic_slice(pixel_frac[1], (0, col_start), (pixel_rows, window)).astype(
        jnp.float32
    )
    summed = jnp.zeros((layer_count, 2, pixel_rows * window), jnp.float32)
    for beam_step in range(2):
        local_beam = rows_beam + beam_step - sector_start
        inside = (local_beam >= 0) & (local_beam < beam_count)
        beam_part = jnp.where(inside, beam_frac if beam_step else 1.0 - beam_frac, 0.0)
        clipped = jnp.clip(local_beam, 0, beam_count - 1)
        for range_step in range(2):
            pair_weight = beam_part * (range_frac if range_step else 1.0 - range_frac)
            flat_index = (clipped * range_count + rows_range + range_step).reshape(-1)
            summed = summed + pair_weight.reshape(-1)[None, None, :] * jnp.take(
                flat_polar, flat_index, axis=2
            )
    angles = (
        layer_wave[:, None]
        * range_phase
        * (rows_range.astype(jnp.float32) + range_frac).reshape(-1)[None, :]
    )
    real_part, imag_part = rotate(summed[:, 0], summed[:, 1], angles)
    stacked = jnp.stack([real_part, imag_part], axis=1).reshape(layer_count, 2, pixel_rows, window)
    placed = jnp.zeros((layer_count, 2, pixel_rows, column_count), jnp.float32)
    placed = lax.dynamic_update_slice(
        placed, stacked, (jnp.int32(0), jnp.int32(0), jnp.int32(0), col_start)
    )
    my_tile = lax.psum_scatter(
        jnp.transpose(placed, (2, 0, 1, 3)), "sub", scatter_dimension=0, tiled=True
    )
    above_layer = from_behind(my_tile, "hgt", -1)
    upper_layers = jnp.concatenate([my_tile[:, 1:], above_layer], axis=1)
    height_frac = lax.dynamic_slice_in_dim(
        pixel_frac[2], sub_index * tile_rows, tile_rows, 0
    ).astype(jnp.float32)[:, None, None, :]
    return (1.0 - height_frac) * my_tile + height_frac * upper_layers


def solution(mesh):
    in_specs = (P("hgt", None, "sub", None), P(), P(), P(), P("hgt"), P(), P(), P())
    out_specs = P("sub", "hgt", None, None)
    return jax.shard_map(body, mesh=mesh, in_specs=in_specs, out_specs=out_specs, check_vma=False)
```

profile of v0, /device:TPU:6, one launch (start us, length us, event | category | flops | bytes accessed | tf_op | source)
XLA Modules:
  0.0 907.3 jit_solution(5051703838200946815)
XLA Ops:
  6.5 1.9 collective-permute-start
  8.5 1.1 broadcast_add_fusion.1
  10.0 0.7 fusion.114
  10.7 0.1 copy.40
  10.8 0.7 fusion.116
  11.6 0.1 copy.38
  11.8 0.2 fusion.61
  12.0 1.2 convolution_bitcast_fusion.5
  13.8 0.7 fusion.115
  14.5 0.1 copy.42
  14.7 0.1 copy.44
  14.8 1.2 fusion.113
  16.0 0.2 fusion.62
  16.2 0.2 fusion.63
  16.4 0.2 fusion.64
  16.7 1.0 fusion.54
  17.8 0.1 copy.46
  17.9 1.4 convert_multiply_fusion.1
  19.3 0.2 convolution_bitcast_fusion.4
  19.5 2.1 fusion.32
  21.7 7.7 collective-permute-start.1
  29.4 0.2 fusion.65
  29.6 0.1 copy.48
  29.7 0.2 convolution_bitcast_fusion.3
  29.9 8.2 collective-permute-done.1
  38.2 0.2 convolution_bitcast_fusion.2
  38.4 2.1 fusion.30
  40.6 4.4 collective-permute-start.2
  45.0 0.2 fusion.66
  45.3 0.1 cos.102
  45.4 0.1 sin.108
  45.5 0.2 convolution_bitcast_fusion.1
  45.7 5.2 collective-permute-done.2
  50.9 0.2 convolution_bitcast_fusion
  51.1 2.1 fusion.28
  53.2 0.3 stack.90
  53.5 0.3 stack.91
  53.9 0.5 pad_maximum_fusion.1
  54.3 15.6 %copy.32 = f32[1,2,65536]{1,2,0:T(8,128)} copy(f32[1,2,65536]{2,1,0:T(2,128)S(1)} %pad_maximum_fusion.1) | data formatting | bytes 1048576 | tf_op jit(solution)/shard_map/stack | solution.py:39
  70.0 0.3 stack.85
  70.3 0.3 stack.86
  70.6 0.5 pad_maximum_fusion
  71.1 15.4 %copy.31 = f32[1,2,65536]{1,2,0:T(8,128)} copy(f32[1,2,65536]{2,1,0:T(2,128)S(1)} %pad_maximum_fusion) | data formatting | bytes 1048576 | tf_op jit(solution)/shard_map/stack | solution.py:39
  86.5 33.3 %add_bitcast_fusion = f32[2,65536]{0,1:T(8,128)} fusion(f32[1,2,65536]{1,2,0:T(8,128)} %copy.31, f32[1,2,65536]{1,2,0:T(8,128)} %copy.32), kind=kLoop, calls=%fused_computation.4 | loop fusion | flops 131072 | bytes 1572864 | tf_op jit(solution)/shard_map/jit(_take)/Arg_0.9 | solution.py:119
  119.9 92.4 %gather_fusion = f32[24576,2]{1,0:T(8,128)} fusion(f32[2,65536]{0,1:T(8,128)} %add_bitcast_fusion, s32[24576]{0:T(1024)S(1)} %fusion.57), kind=kCustom, calls=%fused_computation.clone | custom fusion | bytes 491520 | tf_op jit(solution)/shard_map/jit(_take)/gather | solution.py:119
  212.3 7.5 copy.33
  219.9 92.4 %gather_fusion.1 = f32[24576,2]{1,0:T(8,128)} fusion(f32[2,65536]{0,1:T(8,128)} %add_bitcast_fusion, s32[24576]{0:T(1024)S(1)} %fusion.58), kind=kCustom, calls=%fused_computation.1.clone | custom fusion | bytes 491520 | tf_op jit(solution)/shard_map/jit(_take)/gather | solution.py:119
  312.3 7.5 copy.34
  319.8 92.4 %gather_fusion.2 = f32[24576,2]{1,0:T(8,128)} fusion(f32[2,65536]{0,1:T(8,128)} %add_bitcast_fusion, s32[24576]{0:T(1024)S(1)} %fusion.59), kind=kCustom, calls=%fused_computation.2.clone | custom fusion | bytes 491520 | tf_op jit(solution)/shard_map/jit(_take)/gather | solution.py:119
  412.3 7.5 copy.35
  419.8 92.4 %gather_fusion.3 = f32[24576,2]{1,0:T(8,128)} fusion(f32[2,65536]{0,1:T(8,128)} %add_bitcast_fusion, s32[24576]{0:T(1024)S(1)} %fusion.60), kind=kCustom, calls=%fused_computation.3.clone | custom fusion | bytes 491520 | tf_op jit(solution)/shard_map/jit(_take)/gather | solution.py:119
  512.3 7.5 copy.36
  519.8 0.6 fusion.47
  520.4 0.6 subtract_reduce_fusion
  521.1 0.2 copy.37
  521.3 0.5 broadcast_in_dim.12
  521.8 3.8 dynamic_update_slice.3
  525.6 1.0 copy-done
  526.6 1.3 dynamic-slice.21
  528.6 361.8 %all-reduce.3.cloned.1.call-done = f32[64,1,2,2048]{3,2,1,0:T(2,128)} async-done(((f32[64,1,2,2048]{3,2,1,0:T(2,128)}), f32[64,1,2,2048]{3,2,1,0:T(2,128)}) %all-reduce.3.cloned.1.call-update) | async-done | bytes 1048592
  890.4 0.8 constant_dynamic-slice_fusion.18
  891.2 2.8 collective-permute-start.3
  894.0 5.1 collective-permute-done.3
  899.1 1.4 multiply_add_fusion.2
  (38 shorter events, 1.0 us)
Async XLA Ops:
  6.5 883.9 %all-reduce.3.cloned.1.call-start = ((), (), s32[]{:S(2)}) async-start(), calls=%async_computation | async-start | bytes 2097152
  6.5 12.8 %collective-permute-start = (bf16[1,2,16,4096]{3,2,1,0:T(8,128)(2,1)}, bf16[1,2,16,4096]{3,2,1,0:T(8,128)(2,1)S(1)}, u32[]{:S(2)}, u32[]{:S(2)}) collective-permute-start(bf16[1,2,16,4096]{3,2,1,0:T(8,128)(2,1)} %param.10), channel_id=1, source_target_pairs={{0,16},{16,0},{32,48},{48,32},{64,80},{80,64},{96,112},{112,96},{1... | collective-permute-start | bytes 786440 | tf_op jit(solution)/shard_map/ppermute | solution.py:12
  21.7 16.5 %collective-permute-start.1 = (bf16[1,2,16,4096]{3,2,1,0:T(8,128)(2,1)S(1)}, bf16[1,2,16,4096]{3,2,1,0:T(8,128)(2,1)S(1)}, u32[]{:S(2)}, u32[]{:S(2)}) collective-permute-start(bf16[1,2,16,4096]{3,2,1,0:T(8,128)(2,1)S(1)} %fusion.2), channel_id=1, source_target_pairs={{0,32},{16,48},{32,0},{48,16},{64,96},{80,112},{96,64},{112,80},{1... | collective-permute-start | bytes 786440 | tf_op jit(solution)/shard_map/ppermute | solution.py:12
  40.6 10.3 %collective-permute-start.2 = (bf16[1,2,16,4096]{3,2,1,0:T(8,128)(2,1)S(1)}, bf16[1,2,16,4096]{3,2,1,0:T(8,128)(2,1)S(1)}, u32[]{:S(2)}, u32[]{:S(2)}) collective-permute-start(bf16[1,2,16,4096]{3,2,1,0:T(8,128)(2,1)S(1)} %fusion.3), channel_id=1, source_target_pairs={{0,64},{16,80},{32,96},{48,112},{64,0},{80,16},{96,32},{112,48},{1... | collective-permute-start | bytes 786440 | tf_op jit(solution)/shard_map/ppermute | solution.py:12
  525.6 1.0 copy-start
  891.2 7.9 collective-permute-start.3
Sparse Core Ops, SparseCore 0:
  526.7 363.6 all-reduce.2
where the time goes:
time: 908 us; the launch traced here: 907 us
  local copies, waits for them, and re-layouts  444 us (49%)
  waiting for transfers between devices  380 us (42%)
  other arithmetic  47.6 us (5%)
  starting transfers between devices  16.9 us (2%)
  between operations  15.2 us (2%)
    gather x8, local copies, waits for them, and re-layouts, body(): jnp.take(flat_polar, flat_index, axis=2)  400 us
    unnamed x2, waiting for transfers between devices  362 us
    another operation x1, other arithmetic, body(): jnp.take(flat_polar, flat_index, axis=2)  33.3 us
    another operation x6, local copies, waits for them, and re-layouts, contribution(): return jnp.stack([real_part, imag_part], axis=1)  32.4 us
  transfers between devices with their start and end apart: 5, of which 4 were waited for; matrix products, arithmetic and copies ran while one was open for 1% of the time, Pallas kernels for 0%

commit v1 on v0

v1 whole, which is shorter than its diff:
```python
import functools

import jax
import jax.numpy as jnp
from jax import lax
from jax.experimental import pallas as pl
from jax.experimental.pallas import tpu as pltpu
from jax.sharding import PartitionSpec as P

range_phase = 0.003
LANES = 128
WINDOW = 16
HALO = 4
BLOCK = 256


def merge_kernel(
    place_ref, wave_ref, data_ref, params_ref, out_ref, padded_ref, *, levels, groups, range_count
):
    beams = data_ref.shape[2]
    members = 2**levels
    wave = wave_ref[0]
    params = params_ref[...]
    matrices = levels * 4
    lane = lax.broadcasted_iota(jnp.int32, (1, LANES), 1)
    position = ((place_ref[0] * LANES + lane).astype(jnp.float32) + 0.5) / range_count
    taps = (params.shape[1] - 2 * matrices) // matrices
    cosines, sines, bands = {}, {}, []
    col_ids = lax.broadcasted_iota(jnp.int32, (beams, 2 * beams), 1).astype(jnp.float32)
    for level in range(levels):
        blocks = []
        for half in range(2):
            for child in range(2):
                i = (level * 2 + child) * 2 + half
                angles = (wave * params[:, i : i + 1]) * position
                cosines[level, child, half] = jnp.cos(angles)
                sines[level, child, half] = jnp.sin(angles)
                offsets = col_ids - (params[:, matrices + i : matrices + i + 1] + child * beams)
                block = jnp.zeros((beams, 2 * beams), jnp.float32)
                for tap in range(taps):
                    c = 2 * matrices + i * taps + tap
                    block = jnp.where(offsets == tap, params[:, c : c + 1], block)
                blocks.append(block)
        bands.append(jnp.concatenate(blocks, axis=0).astype(jnp.bfloat16))
    total = [None] * members
    for group in range(groups):
        current = [
            [data_ref[group * members + s, part] for part in range(2)] for s in range(members)
        ]
        for level in range(levels):
            lows = [s for s in range(members) if not s >> level & 1]
            highs = [s | 1 << level for s in lows]
            stacked = jnp.concatenate(
                [
                    jnp.concatenate([current[s][part] for s in rows for part in range(2)], axis=1)
                    for rows in (lows, highs)
                ],
                axis=0,
            )
            product = jnp.dot(bands[level], stacked, preferred_element_type=jnp.float32)
            following = [None] * members
            for pair, s in enumerate(lows):
                for half in range(2):
                    summed = None
                    for child in range(2):
                        row = (half * 2 + child) * beams
                        real = product[row : row + beams, pair * 2 * LANES : (pair * 2 + 1) * LANES]
                        imag = product[
                            row : row + beams, (pair * 2 + 1) * LANES : (pair * 2 + 2) * LANES
                        ]
                        cosine, sine = cosines[level, child, half], sines[level, child, half]
                        term = (cosine * real - sine * imag, sine * real + cosine * imag)
                        summed = term if child == 0 else (summed[0] + term[0], summed[1] + term[1])
                    if level + 1 < levels:
                        summed = tuple(v.astype(jnp.bfloat16) for v in summed)
                    following[s | half << level] = summed
            current = following
        for s in range(members):
            total[s] = (
                current[s]
                if group == 0
                else (total[s][0] + current[s][0], total[s][1] + current[s][1])
            )
    merged = beams * members
    padding = padded_ref.shape[1] - HALO - merged
    for part in range(2):
        padded_ref[part, 0:HALO, :] = jnp.zeros((HALO, LANES), jnp.float32)
        padded_ref[part, HALO + merged :, :] = jnp.zeros((padding, LANES), jnp.float32)
        for s in range(members):
            sector = 0
            for bit in range(levels):
                sector = sector * 2 + (s >> bit & 1)
            start = HALO + sector * beams
            padded_ref[part, start : start + beams, :] = total[s][part]
    for block in range(out_ref.shape[0] // 2):
        low = 4 * (block >> 1) + (block & 1)
        for part in range(2):
            rows = padded_ref[part, 8 * block : 8 * block + WINDOW, :].astype(jnp.bfloat16)
            out_ref[low, part] = rows
            out_ref[low + 2, part] = rows


def sample_kernel(
    place_ref,
    wave_ref,
    table_ref,
    beam_ref,
    range_ref,
    frac_ref,
    out_ref,
    lhs_ref,
    frac_scratch,
    cart_ref,
):
    slices = table_ref.shape[0]
    per_block = BLOCK // LANES
    blocks = slices // per_block
    lane = lax.broadcasted_iota(jnp.int32, (WINDOW, LANES), 1)
    for part in range(2):
        rolled = [
            pltpu.roll(table_ref[i, part].astype(jnp.float32), LANES - 1, 1) for i in range(slices)
        ]
        for i in range(slices):
            shifted = jnp.where(lane < LANES - 1, rolled[i], rolled[(i + 1) % slices])
            row = (i // per_block) * 4 * WINDOW + part * WINDOW
            col = (i % per_block) * LANES
            lhs_ref[row : row + WINDOW, col : col + LANES] = table_ref[i, part]
            row = row + 2 * WINDOW
            lhs_ref[row : row + WINDOW, col : col + LANES] = shifted.astype(jnp.bfloat16)
    frac_scratch[...] = frac_ref[...].astype(jnp.float32)
    column_block = place_ref[1]
    row_half = place_ref[2]
    first_beam = column_block * 8 - HALO
    pixels = 4 * LANES
    rows_iota = lax.broadcasted_iota(jnp.int32, (BLOCK, pixels), 0)
    beam_iota = lax.broadcasted_iota(jnp.int32, (WINDOW, pixels), 0)

    def flat(value):
        return jnp.concatenate([value[i : i + 1, :] for i in range(4)], axis=1)

    def chunk(step, carry):
        start = step * 8 + row_half * 4
        samples = flat(range_ref[pl.ds(start, 4), :])
        beam = flat(beam_ref[pl.ds(start, 4), :]) - first_beam
        frac0 = flat(frac_scratch[0, pl.ds(start, 4), :])
        frac1 = flat(frac_scratch[1, pl.ds(start, 4), :])
        inner = samples & (BLOCK - 1)
        outer = samples >> (BLOCK.bit_length() - 1)
        hot = jnp.where(rows_iota == inner, 1.0, 0.0).astype(jnp.bfloat16)
        product = jnp.dot(lhs_ref[...], hot, preferred_element_type=jnp.float32)
        picked = product[0 : 4 * WINDOW]
        for k in range(1, blocks):
            picked = jnp.where(
                outer == k, product[k * 4 * WINDOW : (k + 1) * 4 * WINDOW], picked
            )
        weights = jnp.where(
            beam_iota == beam, 1.0 - frac0, jnp.where(beam_iota == beam + 1, frac0, 0.0)
        )
        low_weights = weights * (1.0 - frac1)
        high_weights = weights * frac1
        for part in range(2):
            low = picked[part * WINDOW : (part + 1) * WINDOW]
            high = picked[(2 + part) * WINDOW : (3 + part) * WINDOW]
            summed = jnp.sum(low_weights * low + high_weights * high, axis=0, keepdims=True)
            for i in range(4):
                cart_ref[part, pl.ds(step * 4 + i, 1), :] = summed[:, i * LANES : (i + 1) * LANES]
        angle_scale = wave_ref[0] * range_phase
        angles = angle_scale * (samples.astype(jnp.float32) + frac1)
        for i in range(4):
            cart_ref[2, pl.ds(step * 4 + i, 1), :] = angles[:, i * LANES : (i + 1) * LANES]
        return carry

    lax.fori_loop(0, range_ref.shape[0] // 8, chunk, 0)
    real, imag, angles = cart_ref[0], cart_ref[1], cart_ref[2]
    cosine, sine = jnp.cos(angles), jnp.sin(angles)
    cart_ref[0] = cosine * real - sine * imag
    cart_ref[1] = sine * real + cosine * imag
    for row in range(cart_ref.shape[1]):
        for part in range(2):
            out_ref[row // 2, row % 2, part, :] = cart_ref[part, row, :]


def body(
    polar_beams,
    band_start,
    band_weight,
    phase_rate,
    layer_wave,
    beam_map,
    range_map,
    pixel_frac,
    *,
    interpret=False,
):
    sub_index = lax.axis_index("sub")
    sub_count = lax.axis_size("sub")
    beams = polar_beams.shape[2]
    range_count = polar_beams.shape[3]
    levels = band_start.shape[0]
    taps = band_weight.shape[-1]
    row_count, column_count = beam_map.shape
    matrices = levels * 4
    column_block = (sub_index >> 2) * 2 + (sub_index & 1)
    row_half = sub_index >> 1 & 1
    place = jnp.stack([sub_index, column_block, row_half]).astype(jnp.int32)
    params = jnp.concatenate(
        [
            phase_rate.reshape(matrices, beams),
            band_start.reshape(matrices, beams).astype(jnp.float32),
            band_weight.reshape(matrices, beams, taps)
            .transpose(0, 2, 1)
            .reshape(matrices * taps, beams)
            .astype(jnp.float32),
        ],
        axis=0,
    ).T

    slices = polar_beams.reshape(2, beams, sub_count, LANES).transpose(2, 0, 1, 3)
    slices = lax.all_to_all(slices, "sub", 0, 0, tiled=True)
    smem = pl.BlockSpec(memory_space=pltpu.SMEM)
    vmem = pl.BlockSpec(memory_space=pltpu.VMEM)
    windows = pl.pallas_call(
        functools.partial(
            merge_kernel,
            levels=levels,
            groups=sub_count // 2**levels,
            range_count=range_count,
        ),
        out_shape=jax.ShapeDtypeStruct((sub_count, 2, WINDOW, LANES), jnp.bfloat16),
        in_specs=[smem, smem, vmem, vmem],
        out_specs=vmem,
        scratch_shapes=[pltpu.VMEM((2, 144, LANES), jnp.float32)],
        interpret=interpret,
        name="merge",
    )(place, layer_wave, slices, params)
    table = lax.all_to_all(windows, "sub", 0, 0, tiled=True)
    rows = row_count // 2
    cart = pl.pallas_call(
        sample_kernel,
        out_shape=jax.ShapeDtypeStruct((rows // 2, 2, 2, LANES), jnp.float32),
        grid_spec=pltpu.PrefetchScalarGridSpec(
            num_scalar_prefetch=1,
            grid=(1,),
            in_specs=[
                smem,
                pl.BlockSpec(table.shape, lambda i, p: (0, 0, 0, 0)),
                pl.BlockSpec((row_count, LANES), lambda i, p: (0, p[1])),
                pl.BlockSpec((row_count, LANES), lambda i, p: (0, p[1])),
                pl.BlockSpec((3, row_count, LANES), lambda i, p: (0, 0, p[1])),
            ],
            out_specs=pl.BlockSpec((rows // 2, 2, 2, LANES), lambda i, p: (0, 0, 0, 0)),
            scratch_shapes=[
                pltpu.VMEM((range_count // BLOCK * 4 * WINDOW, BLOCK), jnp.bfloat16),
                pltpu.VMEM((3, row_count, LANES), jnp.float32),
                pltpu.VMEM((3, rows, LANES), jnp.float32),
            ],
        ),
        interpret=interpret,
        name="sample",
    )(place, layer_wave, table, beam_map, range_map, pixel_frac)
    halves = [[s for s in range(sub_count) if s >> 1 & 1 == half] for half in range(2)]
    tile = lax.all_to_all(cart, "sub", 0, 0, axis_index_groups=halves, tiled=True)
    layers = lax.axis_size("hgt")
    above = lax.ppermute(tile, "hgt", [(i, i - 1) for i in range(1, layers)])
    tile_rows = row_count // sub_count
    height_frac = lax.dynamic_slice_in_dim(
        pixel_frac[2], sub_index * tile_rows, tile_rows, 0
    ).astype(jnp.float32)
    height_frac = height_frac.reshape(tile_rows, column_count // LANES, LANES).transpose(1, 0, 2)
    height_frac = height_frac[:, :, None, :]
    blended = (1.0 - height_frac) * tile + height_frac * above
    return blended.transpose(1, 2, 0, 3).reshape(tile_rows, 1, 2, column_count)


def solution(mesh):
    in_specs = (P("hgt", None, "sub", None), P(), P(), P(), P("hgt"), P(), P(), P())
    out_specs = P("sub", "hgt", None, None)
    return jax.shard_map(body, mesh=mesh, in_specs=in_specs, out_specs=out_specs, check_vma=False)
```

time: 908 us -> 85.1 us (0.09)
  the two profiles are of different devices: /device:TPU:6 before, /device:TPU:14 now
where the time goes in v1:
time: 85.1 us; the launch traced here: 84.5 us
  waiting for transfers between devices  41.2 us (48%)
  starting transfers between devices  25.3 us (30%)
  Pallas kernels  9.64 us (11%)
  local copies, waits for them, and re-layouts  6.29 us (7%)
  other arithmetic  1.38 us (2%)
    all_to_all x1, starting transfers between devices, body(): slices = lax.all_to_all(slices, 'sub', 0, 0, tiled=True)  15.2 us
    all_to_all x1, waiting for transfers between devices, body(): table = lax.all_to_all(windows, 'sub', 0, 0, tiled=True)  15.1 us
    all_to_all x1, waiting for transfers between devices, body(): slices = lax.all_to_all(slices, 'sub', 0, 0, tiled=True)  13.3 us
    all_to_all x1, waiting for transfers between devices, body(): lax.all_to_all(cart, 'sub', 0, 0, axis_index_groups=halves, tiled=True)  7.63 us
    pallas_call x1, Pallas kernels, body(): pl.pallas_call(sample_kernel, out_shape=jax.ShapeDtypeStruct((rows // 2,...  6.17 us
    ppermute x1, waiting for transfers between devices, body(): above = lax.ppermute(tile, 'hgt', [(i, i - 1) for i in range(1, layers)])  5.16 us
    all_to_all x1, starting transfers between devices, body(): table = lax.all_to_all(windows, 'sub', 0, 0, tiled=True)  3.87 us
    unnamed x11, local copies, waits for them, and re-layouts  3.63 us
  transfers between devices with their start and end apart: 4, of which 4 were waited for; matrix products, arithmetic and copies ran while one was open for 3% of the time, Pallas kernels for 0%

profile of v1, /device:TPU:14, one launch (start us, length us, event | category | flops | bytes accessed | tf_op | source)
XLA Modules:
  0.0 84.5 jit_solution(13828296613709135091)
XLA Ops:
  0.0 1.0 %copy.20 = bf16[4,8,32,128]{3,2,1,0:T(8,128)(2,1)S(1)} copy(bf16[4,8,32,128]{3,1,2,0:T(8,128)(2,1)} %bitcast.35) | data formatting | bytes 524288
  1.0 0.8 copy.22
  1.8 0.0 copy-start.2
  1.8 15.2 %all-to-all-start = ((bf16[32,2,16,128]{3,2,1,0:T(8,128)(2,1)}), bf16[32,2,16,128]{3,2,1,0:T(8,128)(2,1)S(1)}, u32[]{:S(2)}, u32[]{:S(2)}) async-start(bf16[32,2,16,128]{3,2,1,0:T(8,128)(2,1)} %bitcast.33), calls=%async_computation | async-start | bytes 524288 | tf_op jit(solution)/shard_map/all_to_all | solution.py:219
  17.7 0.0 copy-done.2
  17.7 0.0 copy-start.4
  17.7 0.1 copy.17
  17.8 0.6 copy-done.4
  18.4 0.0 copy-start.3
  18.4 0.1 copy.16
  18.5 0.6 copy-done.3
  19.1 0.1 copy.15
  19.2 0.6 pad_add_fusion.place_ref
  19.8 0.7 maximum_bitcast_fusion.params_ref
  20.5 13.3 %all-to-all-done.data_ref = bf16[32,2,16,128]{3,2,1,0:T(8,128)(2,1)S(1)} async-done(((bf16[32,2,16,128]{3,2,1,0:T(8,128)(2,1)}), bf16[32,2,16,128]{3,2,1,0:T(8,128)(2,1)S(1)}, u32[]{:S(2)}, u32[]{:S(2)}) %all-to-all-start) | async-done | bytes 262176 | tf_op jit(solution)/shard_map/all_to_all | solution.py:219
  33.8 0.0 copy-start
  33.8 0.7 copy-done
  34.5 3.5 %merge.1 = bf16[32,2,16,128]{3,2,1,0:T(8,128)(2,1)} custom-call(s32[3]{0:T(128)} %pad_add_fusion.place_ref, f32[1]{0:T(128)S(6)} %copy.23.wave_ref, bf16[32,2,16,128]{3,2,1,0:T(8,128)(2,1)} %copy-done, f32[16,120]{1,0:T(8,128)} %maximum_bitcast_fusion.params_ref), custom_call_target="tpu_custom_call" | custom-call | tf_op jit(solution)/shard_map/merge/pallas_call | solution.py:222
  38.0 3.9 %all-to-all-start.1 = ((bf16[32,2,16,128]{3,2,1,0:T(8,128)(2,1)}), bf16[32,2,16,128]{3,2,1,0:T(8,128)(2,1)S(1)}, u32[]{:S(2)}, u32[]{:S(2)}) async-start(bf16[32,2,16,128]{3,2,1,0:T(8,128)(2,1)} %merge.1), calls=%async_computation.1 | async-start | bytes 524288 | tf_op jit(solution)/shard_map/all_to_all | solution.py:236
  41.8 1.0 %slice.3 = bf16[1,64,2048]{2,1,0:T(8,128)(2,1)S(1)} slice(bf16[3,64,2048]{2,1,0:T(8,128)(2,1)} %frac_ref.1), slice={[2:3], [0:64], [0:2048]} | slice | bytes 524288 | tf_op jit(solution)/shard_map/slice | solution.py:267
  42.8 15.1 %all-to-all-done.1.table_ref = bf16[32,2,16,128]{3,2,1,0:T(8,128)(2,1)S(1)} async-done(((bf16[32,2,16,128]{3,2,1,0:T(8,128)(2,1)}), bf16[32,2,16,128]{3,2,1,0:T(8,128)(2,1)S(1)}, u32[]{:S(2)}, u32[]{:S(2)}) %all-to-all-start.1) | async-done | bytes 262176 | tf_op jit(solution)/shard_map/all_to_all | solution.py:236
  57.9 0.0 copy-start.1
  57.9 0.7 copy-done.1
  58.6 6.2 %sample.1 = f32[16,2,2,128]{3,2,1,0:T(2,128)} custom-call(s32[3]{0:T(128)} %pad_add_fusion.place_ref, f32[1]{0:T(128)S(6)} %copy.23.wave_ref, bf16[32,2,16,128]{3,2,1,0:T(8,128)(2,1)} %copy-done.1, s32[64,2048]{1,0:T(8,128)} %beam_ref.1, s32[64,2048]{1,0:T(8,128)} %range_ref.1, bf16[3,64,2048]{2,1,0:T(8,128)(2,1)} %frac_ref.1), custom_call_target="tpu_custom_call" | custom-call | tf_op jit(solution)/shard_map/sample/pallas_call | solution.py:238
  64.8 3.5 %all-to-all-start.2 = ((f32[16,2,2,128]{3,2,1,0:T(2,128)}), f32[16,2,2,128]{3,2,1,0:T(2,128)S(1)}, u32[]{:S(2)}, u32[]{:S(2)}) async-start(f32[16,2,2,128]{3,2,1,0:T(2,128)} %sample.1), calls=%async_computation.2 | async-start | bytes 65536 | tf_op jit(solution)/shard_map/all_to_all | solution.py:262
  68.3 7.6 %all-to-all-done.2 = f32[16,2,2,128]{3,2,1,0:T(2,128)S(1)} async-done(((f32[16,2,2,128]{3,2,1,0:T(2,128)}), f32[16,2,2,128]{3,2,1,0:T(2,128)S(1)}, u32[]{:S(2)}, u32[]{:S(2)}) %all-to-all-start.2) | async-done | bytes 32800 | tf_op jit(solution)/shard_map/all_to_all | solution.py:262
  75.9 2.7 %collective-permute-start = (f32[16,2,2,128]{3,2,1,0:T(2,128)S(1)}, f32[16,2,2,128]{3,2,1,0:T(2,128)S(1)}, u32[]{:S(2)}, u32[]{:S(2)}) collective-permute-start(f32[16,2,2,128]{3,2,1,0:T(2,128)S(1)} %all-to-all-done.2), channel_id=1, source_target_pairs={{1,0},{2,1},{3,2},{4,3},{5,4},{6,5},{7,6},{8,7},{9,8},{10,9},{11,1... | collective-permute-start | bytes 98312 | tf_op jit(solution)/shard_map/ppermute | solution.py:264
  78.7 5.2 %collective-permute-done = f32[16,2,2,128]{3,2,1,0:T(2,128)S(1)} collective-permute-done((f32[16,2,2,128]{3,2,1,0:T(2,128)S(1)}, f32[16,2,2,128]{3,2,1,0:T(2,128)S(1)}, u32[]{:S(2)}, u32[]{:S(2)}) %collective-permute-start) | collective-permute-done | bytes 32800 | tf_op jit(solution)/shard_map/ppermute | solution.py:264
  83.9 0.6 reshape.27
  (8 shorter events, 0.1 us)
Async XLA Ops:
  1.8 15.9 %copy-start.2 = (bf16[3,2,2,16,8]{3,4,2,1,0:T(8,128)(2,1)S(1)}, bf16[3,2,2,16,8]{3,4,2,1,0:T(8,128)(2,1)}, u32[]{:S(2)}) copy-start(bf16[3,2,2,16,8]{3,4,2,1,0:T(8,128)(2,1)} %param.10) | copy-start | bytes 9220
  1.8 32.0 %all-to-all-start = ((bf16[32,2,16,128]{3,2,1,0:T(8,128)(2,1)}), bf16[32,2,16,128]{3,2,1,0:T(8,128)(2,1)S(1)}, u32[]{:S(2)}, u32[]{:S(2)}) async-start(bf16[32,2,16,128]{3,2,1,0:T(8,128)(2,1)} %bitcast.33), calls=%async_computation | async-start | bytes 524288 | tf_op jit(solution)/shard_map/all_to_all | solution.py:219
  17.7 0.7 copy-start.4
  18.4 0.7 copy-start.3
  33.8 0.7 copy-start
  38.0 19.9 %all-to-all-start.1 = ((bf16[32,2,16,128]{3,2,1,0:T(8,128)(2,1)}), bf16[32,2,16,128]{3,2,1,0:T(8,128)(2,1)S(1)}, u32[]{:S(2)}, u32[]{:S(2)}) async-start(bf16[32,2,16,128]{3,2,1,0:T(8,128)(2,1)} %merge.1), calls=%async_computation.1 | async-start | bytes 524288 | tf_op jit(solution)/shard_map/all_to_all | solution.py:236
  57.9 0.7 copy-start.1
  64.8 11.2 %all-to-all-start.2 = ((f32[16,2,2,128]{3,2,1,0:T(2,128)}), f32[16,2,2,128]{3,2,1,0:T(2,128)S(1)}, u32[]{:S(2)}, u32[]{:S(2)}) async-start(f32[16,2,2,128]{3,2,1,0:T(2,128)} %sample.1), calls=%async_computation.2 | async-start | bytes 65536 | tf_op jit(solution)/shard_map/all_to_all | solution.py:262
  75.9 7.9 %collective-permute-start = (f32[16,2,2,128]{3,2,1,0:T(2,128)S(1)}, f32[16,2,2,128]{3,2,1,0:T(2,128)S(1)}, u32[]{:S(2)}, u32[]{:S(2)}) collective-permute-start(f32[16,2,2,128]{3,2,1,0:T(2,128)S(1)} %all-to-all-done.2), channel_id=1, source_target_pairs={{1,0},{2,1},{3,2},{4,3},{5,4},{6,5},{7,6},{8,7},{9,8},{10,9},{11,1... | collective-permute-start | bytes 98312 | tf_op jit(solution)/shard_map/ppermute | solution.py:264

commit v2 on v1

v2 whole, which is shorter than its diff:
```python
import functools

import jax
import jax.numpy as jnp
from jax import lax
from jax.experimental import pallas as pl
from jax.experimental.pallas import tpu as pltpu
from jax.sharding import PartitionSpec as P

range_phase = 0.003
LANES = 128
WINDOW = 16
HALO = 4
QUARTER = 8
ROWS = 64


def split_kernel(source_ref, out_ref):
    width = out_ref.shape[3]
    for i in range(out_ref.shape[0]):
        for part in range(out_ref.shape[1]):
            out_ref[i, part] = source_ref[0, part, :, i * width : (i + 1) * width]


def swap_quarters(values):
    lane = lax.broadcasted_iota(jnp.int32, values[0].shape, 1)
    values = list(values)
    for bit, width in ((1, 64), (0, 32)):
        keep = lane & width == 0
        for i in range(4):
            if i >> bit & 1:
                continue
            j = i | 1 << bit
            a, b = values[i], values[j]
            values[i] = jnp.where(keep, a, pltpu.roll(b, width, 1))
            values[j] = jnp.where(keep, pltpu.roll(a, LANES - width, 1), b)
    return values


def prepare_kernel(
    place_ref,
    wave_ref,
    params_ref,
    beam_ref,
    range_ref,
    frac_ref,
    trig_ref,
    first_ref,
    second_ref,
    third_ref,
    whole_ref,
    real_ref,
    pixel_ref,
    *,
    range_count,
):
    wave = wave_ref[0]
    params = params_ref[...]
    beams = params.shape[0]
    matrices = 12
    taps = (params.shape[1] - 2 * matrices) // matrices
    width = trig_ref.shape[3]
    lane = lax.broadcasted_iota(jnp.int32, (1, width), 1)
    position = ((place_ref[0] * width + lane).astype(jnp.float32) + 0.5) / range_count
    row_half = place_ref[1]
    upper = row_half == 1

    def column(offset, level, child, half):
        i = offset + (level * 2 + child) * 2 + half
        return params[:, i : i + 1]

    def mine(offset, level, half):
        return jnp.where(upper, column(offset, level, 1, half), column(offset, level, 0, half))

    def weight(tap, level, child, half):
        i = 2 * matrices + ((level * 2 + child) * 2 + half) * taps + tap
        return params[:, i : i + 1]

    rates = [column(0, 0, child, half) for half in range(2) for child in range(2)]
    rates += [mine(0, 1, half) for half in range(2)]
    rates += [column(0, 2, child, half) for half in range(2) for child in range(2)]
    for i, rate in enumerate(rates):
        angles = (wave * rate) * position
        trig_ref[i, 0] = jnp.cos(angles)
        trig_ref[i, 1] = jnp.sin(angles)

    def band(starts, weights):
        ids = lax.broadcasted_iota(jnp.int32, (beams, beams), 1).astype(jnp.float32) - starts
        block = jnp.zeros((beams, beams), jnp.float32)
        for tap in range(taps):
            block = jnp.where(ids == tap, weights[tap], block)
        return block

    def pair_bands(level, copies):
        rows = []
        for half in range(2):
            for child in range(2):
                block = band(
                    column(matrices, level, child, half),
                    [weight(tap, level, child, half) for tap in range(taps)],
                )
                empty = jnp.zeros_like(block)
                rows.append(
                    jnp.concatenate(
                        [block if c == child else empty for c in range(2) for _ in range(copies)],
                        axis=1,
                    )
                )
        return jnp.concatenate(rows, axis=0).astype(jnp.bfloat16)

    first_ref[...] = pair_bands(0, 1)
    third_ref[...] = pair_bands(2, 2)
    rows = []
    for half in range(2):
        block = band(
            mine(matrices, 1, half),
            [
                jnp.where(upper, weight(tap, 1, 1, half), weight(tap, 1, 0, half))
                for tap in range(taps)
            ],
        )
        rows.append(jnp.concatenate([block, block], axis=1))
    second_ref[...] = jnp.concatenate(rows, axis=0).astype(jnp.bfloat16)

    samples = range_ref[...]
    fracs = [frac_ref[i].astype(jnp.float32) for i in range(3)]
    angles = (wave * range_phase) * (samples.astype(jnp.float32) + fracs[1])
    pixel_ref[0] = jnp.cos(angles)
    pixel_ref[1] = jnp.sin(angles)
    pixel_ref[2] = fracs[2]
    first_beam = place_ref[2] * 8 - HALO
    for group in range(ROWS // 32):
        rows = [slice(group * 32 + 8 * j, group * 32 + 8 * j + 8) for j in range(4)]
        sample_parts = swap_quarters([samples[r] for r in rows])
        beam_parts = swap_quarters([beam_ref[r, :] - first_beam for r in rows])
        frac_parts = [swap_quarters([fracs[i][r] for r in rows]) for i in range(2)]
        for quarter in range(4):
            place = slice(quarter * 16 + group * 8, quarter * 16 + group * 8 + 8)
            whole_ref[0, place, :] = sample_parts[quarter] & (width - 1)
            whole_ref[1, place, :] = sample_parts[quarter] >> (width.bit_length() - 1)
            whole_ref[2, place, :] = beam_parts[quarter] - (2 * quarter + 2)
            for i in range(2):
                real_ref[i, place, :] = frac_parts[i][quarter]


def halves_of(value):
    high = value.astype(jnp.bfloat16)
    return high, (value - high.astype(jnp.float32)).astype(jnp.bfloat16)


def merge_kernel(
    data_ref, trig_ref, first_ref, second_ref, third_ref, out_ref, padded_ref, *, groups
):
    beams, width = data_ref.shape[2], data_ref.shape[3]

    def turn(i, product, row, col):
        real = product[row : row + beams, col : col + width]
        imag = product[row : row + beams, col + width : col + 2 * width]
        cosine, sine = trig_ref[i, 0], trig_ref[i, 1]
        return cosine * real - sine * imag, sine * real + cosine * imag

    def add(a, b):
        return a[0] + b[0], a[1] + b[1]

    sums = {}
    for low in range(2):
        for group in range(groups):
            source = (group * 2 + low) * 2
            stacked = jnp.concatenate(
                [
                    jnp.concatenate([data_ref[source + core, part] for part in range(2)], axis=1)
                    for core in range(2)
                ],
                axis=0,
            )
            product = jnp.dot(first_ref[...], stacked, preferred_element_type=jnp.float32)
            for half in range(2):
                terms = [
                    turn(half * 2 + child, product, (half * 2 + child) * beams, 0)
                    for child in range(2)
                ]
                level = tuple(
                    v.astype(jnp.bfloat16).astype(jnp.float32) for v in add(terms[0], terms[1])
                )
                sums[low, half] = level if group == 0 else add(sums[low, half], level)
    middle = {}
    for low in range(2):
        for half in range(2):
            parts = [halves_of(v) for v in sums[low, half]]
            stacked = jnp.concatenate(
                [jnp.concatenate([parts[0][i], parts[1][i]], axis=1) for i in range(2)], axis=0
            )
            product = jnp.dot(second_ref[...], stacked, preferred_element_type=jnp.float32)
            for next_half in range(2):
                middle[low, half, next_half] = turn(4 + next_half, product, next_half * beams, 0)
    merged = 8 * beams
    padding = padded_ref.shape[1] - HALO - merged
    for part in range(2):
        padded_ref[part, 0:HALO, :] = jnp.zeros((HALO, width), jnp.float32)
        padded_ref[part, HALO + merged :, :] = jnp.zeros((padding, width), jnp.float32)
    for half in range(2):
        for next_half in range(2):
            rows = []
            for low in range(2):
                parts = [halves_of(v) for v in middle[low, half, next_half]]
                rows += [jnp.concatenate([parts[0][i], parts[1][i]], axis=1) for i in range(2)]
            product = jnp.dot(
                third_ref[...], jnp.concatenate(rows, axis=0), preferred_element_type=jnp.float32
            )
            for last in range(2):
                terms = [
                    turn(6 + last * 2 + child, product, (last * 2 + child) * beams, 0)
                    for child in range(2)
                ]
                start = HALO + (half * 4 + next_half * 2 + last) * beams
                for part, value in enumerate(add(terms[0], terms[1])):
                    padded_ref[part, start : start + beams, :] = value
    for block in range(out_ref.shape[0]):
        for part in range(2):
            rows = padded_ref[part, 8 * block : 8 * block + WINDOW, :]
            out_ref[block, part] = rows.astype(jnp.bfloat16)


def sample_kernel(
    table_ref, whole_ref, real_ref, pixel_ref, out_ref, pair_ref, lhs_ref, cart_ref
):
    blocks, parts, _, width = table_ref.shape
    rows = 2 * parts * QUARTER
    lane = lax.broadcasted_iota(jnp.int32, (WINDOW, width), 1)
    for part in range(parts):
        values = [table_ref[i, part].astype(jnp.float32) for i in range(blocks)]
        rolled = [pltpu.roll(v, width - 1, 1) for v in values]
        for i in range(blocks):
            pair_ref[0, i, part] = values[i]
            pair_ref[1, i, part] = jnp.where(
                lane < width - 1, rolled[i], rolled[(i + 1) % blocks]
            )
    for quarter in range(4):
        low = 2 * quarter + 2
        for i in range(blocks):
            for tap in range(2):
                pair = [pair_ref[tap, i, part, low : low + QUARTER, :] for part in range(parts)]
                row = i * rows + tap * parts * QUARTER
                lhs_ref[quarter, row : row + parts * QUARTER, :] = jnp.concatenate(
                    pair, axis=0
                ).astype(jnp.bfloat16)
    pixels = 4 * LANES
    row_ids = lax.broadcasted_iota(jnp.int32, (width, pixels), 0)
    beam_ids = lax.broadcasted_iota(jnp.int32, (QUARTER, pixels), 0)

    def flat(value):
        return jnp.concatenate([value[i : i + 1, :] for i in range(4)], axis=1)

    def chunk(step, carry):
        place = pl.ds(step * 4, 4)
        inner, outer, beam = (flat(whole_ref[i, place, :]) for i in range(3))
        frac0, frac1 = (flat(real_ref[i, place, :]) for i in range(2))
        hot = jnp.where(row_ids == inner, 1.0, 0.0).astype(jnp.bfloat16)
        product = jnp.dot(lhs_ref[step >> 2], hot, preferred_element_type=jnp.float32)
        picked = product[0:rows]
        for k in range(1, blocks):
            picked = jnp.where(outer == k, product[k * rows : (k + 1) * rows], picked)
        weights = jnp.where(
            beam_ids == beam, 1.0 - frac0, jnp.where(beam_ids == beam + 1, frac0, 0.0)
        )
        low_weights = weights * (1.0 - frac1)
        high_weights = weights * frac1
        for part in range(parts):
            low = picked[part * QUARTER : (part + 1) * QUARTER]
            high = picked[(parts + part) * QUARTER : (parts + part + 1) * QUARTER]
            summed = jnp.sum(low_weights * low + high_weights * high, axis=0, keepdims=True)
            for i in range(4):
                cart_ref[part, pl.ds(step * 4 + i, 1), :] = summed[:, i * LANES : (i + 1) * LANES]
        return carry

    lax.fori_loop(0, whole_ref.shape[1] // 4, chunk, 0)
    for group in range(ROWS // 32):
        ordered = [
            swap_quarters(
                [
                    cart_ref[part, quarter * 16 + group * 8 : quarter * 16 + group * 8 + 8, :]
                    for quarter in range(4)
                ]
            )
            for part in range(parts)
        ]
        for j in range(4):
            start = group * 32 + 8 * j
            cosine = pixel_ref[0, start : start + 8, :]
            sine = pixel_ref[1, start : start + 8, :]
            real, imag = ordered[0][j], ordered[1][j]
            out_ref[pl.ds(2 * start, 8, stride=2), :] = cosine * real - sine * imag
            out_ref[pl.ds(2 * start + 1, 8, stride=2), :] = sine * real + cosine * imag


def body(
    polar_beams,
    band_start,
    band_weight,
    phase_rate,
    layer_wave,
    beam_map,
    range_map,
    pixel_frac,
    *,
    interpret=False,
):
    sub_index = lax.axis_index("sub")
    sub_count = lax.axis_size("sub")
    layers = lax.axis_size("hgt")
    beams = polar_beams.shape[2]
    range_count = polar_beams.shape[3]
    levels = band_start.shape[0]
    taps = band_weight.shape[-1]
    row_count, column_count = beam_map.shape
    matrices = levels * 4
    members = sub_count // 2
    width = range_count // members
    column_block = (sub_index >> 2) * 2 + (sub_index & 1)
    row_half = sub_index >> 1 & 1
    halves = [[s for s in range(sub_count) if s >> 1 & 1 == half] for half in range(2)]
    place = jnp.stack([column_block, row_half, column_block]).astype(jnp.int32)
    params = jnp.concatenate(
        [
            phase_rate.reshape(matrices, beams),
            band_start.reshape(matrices, beams).astype(jnp.float32),
            band_weight.reshape(matrices, beams, taps)
            .transpose(0, 2, 1)
            .reshape(matrices * taps, beams)
            .astype(jnp.float32),
        ],
        axis=0,
    ).T
    smem = pl.BlockSpec(memory_space=pltpu.SMEM)
    vmem = pl.BlockSpec(memory_space=pltpu.VMEM)
    shape = jax.ShapeDtypeStruct
    f32, bf16 = jnp.float32, jnp.bfloat16

    slices = pl.pallas_call(
        split_kernel,
        out_shape=shape((members, 2, beams, width), bf16),
        in_specs=[vmem],
        out_specs=vmem,
        interpret=interpret,
        name="split",
    )(polar_beams)
    slices = lax.all_to_all(slices, "sub", 0, 0, axis_index_groups=halves, tiled=True)
    trig, first, second, third, whole, real, pixel = pl.pallas_call(
        functools.partial(prepare_kernel, range_count=range_count),
        out_shape=[
            shape((10, 2, beams, width), f32),
            shape((4 * beams, 2 * beams), bf16),
            shape((2 * beams, 2 * beams), bf16),
            shape((4 * beams, 4 * beams), bf16),
            shape((3, row_count, LANES), jnp.int32),
            shape((2, row_count, LANES), f32),
            shape((3, row_count, LANES), f32),
        ],
        grid_spec=pltpu.PrefetchScalarGridSpec(
            num_scalar_prefetch=1,
            grid=(1,),
            in_specs=[
                smem,
                pl.BlockSpec((beams, params.shape[1]), lambda i, p: (0, 0)),
                pl.BlockSpec((row_count, LANES), lambda i, p: (0, p[0])),
                pl.BlockSpec((row_count, LANES), lambda i, p: (0, p[0])),
                pl.BlockSpec((3, row_count, LANES), lambda i, p: (0, 0, p[0])),
            ],
            out_specs=[
                pl.BlockSpec((10, 2, beams, width), lambda i, p: (0, 0, 0, 0)),
                pl.BlockSpec((4 * beams, 2 * beams), lambda i, p: (0, 0)),
                pl.BlockSpec((2 * beams, 2 * beams), lambda i, p: (0, 0)),
                pl.BlockSpec((4 * beams, 4 * beams), lambda i, p: (0, 0)),
                pl.BlockSpec((3, row_count, LANES), lambda i, p: (0, 0, 0)),
                pl.BlockSpec((2, row_count, LANES), lambda i, p: (0, 0, 0)),
                pl.BlockSpec((3, row_count, LANES), lambda i, p: (0, 0, 0)),
            ],
        ),
        interpret=interpret,
        name="prepare",
    )(place, layer_wave, params, beam_map, range_map, pixel_frac)
    windows = pl.pallas_call(
        functools.partial(merge_kernel, groups=sub_count // 2**levels),
        out_shape=shape((members, 2, WINDOW, width), bf16),
        in_specs=[vmem] * 5,
        out_specs=vmem,
        scratch_shapes=[pltpu.VMEM((2, 144, width), f32)],
        interpret=interpret,
        name="merge",
    )(slices, trig, first, second, third)
    table = lax.all_to_all(windows, "sub", 0, 0, axis_index_groups=halves, tiled=True)
    cart = pl.pallas_call(
        sample_kernel,
        out_shape=shape((2 * row_count, LANES), f32),
        in_specs=[vmem] * 4,
        out_specs=vmem,
        scratch_shapes=[
            pltpu.VMEM((2, members, 2, WINDOW, width), f32),
            pltpu.VMEM((4, members * 4 * QUARTER, width), bf16),
            pltpu.VMEM((2, row_count, LANES), f32),
        ],
        interpret=interpret,
        name="sample",
    )(table, whole, real, pixel)
    above = lax.ppermute(cart, "hgt", [(i, i - 1) for i in range(1, layers)])
    height_frac = pixel[2][:, None, :]
    blended = (1.0 - height_frac) * cart.reshape(row_count, 2, LANES) + (
        height_frac * above.reshape(row_count, 2, LANES)
    )
    tile_rows = row_count // sub_count
    blended = blended.reshape(sub_count, tile_rows * 2, LANES)
    tiles = lax.all_to_all(blended, "sub", 0, 0, tiled=True)
    tiles = tiles.reshape(sub_count // 4, 2, 2, tile_rows * 2, LANES)
    tiles = (tiles[:, 0] + tiles[:, 1]).reshape(members, tile_rows * 2, LANES)
    return tiles.transpose(1, 0, 2).reshape(tile_rows, 1, 2, column_count)


def solution(mesh):
    in_specs = (P("hgt", None, "sub", None), P(), P(), P(), P("hgt"), P(), P(), P())
    out_specs = P("sub", "hgt", None, None)
    return jax.shard_map(body, mesh=mesh, in_specs=in_specs, out_specs=out_specs, check_vma=False)
```

time: 85.1 us -> 80.9 us (0.951)
  the two profiles are of different devices: /device:TPU:14 before, /device:TPU:6 now
where the time goes in v2:
time: 80.9 us; the launch traced here: 79.9 us
  waiting for transfers between devices  20.6 us (25%)
  blocking collectives  20.5 us (25%)
  starting transfers between devices  16.7 us (21%)
  Pallas kernels  14.8 us (18%)
  local copies, waits for them, and re-layouts  4.52 us (6%)
  other arithmetic  2.04 us (3%)
    all_to_all x1, blocking collectives, body(): tiles = lax.all_to_all(blended, 'sub', 0, 0, tiled=True)  20.5 us
    all_to_all x1, waiting for transfers between devices, body(): lax.all_to_all(windows, 'sub', 0, 0, axis_index_groups=halves, tiled=True)  10.6 us
    all_to_all x1, starting transfers between devices, body(): lax.all_to_all(slices, 'sub', 0, 0, axis_index_groups=halves, tiled=True)  10.4 us
    pallas_call x1, Pallas kernels, body(): pl.pallas_call(sample_kernel, out_shape=shape((2 * row_count, LANES), f32...  7.13 us
    ppermute x1, waiting for transfers between devices, body(): above = lax.ppermute(cart, 'hgt', [(i, i - 1) for i in range(1, layers)])  5.27 us
    all_to_all x1, waiting for transfers between devices, body(): lax.all_to_all(slices, 'sub', 0, 0, axis_index_groups=halves, tiled=True)  4.79 us
    pallas_call x1, Pallas kernels, body(): pl.pallas_call(functools.partial(prepare_kernel, range_count=range_count)...  3.55 us
    all_to_all x1, starting transfers between devices, body(): lax.all_to_all(windows, 'sub', 0, 0, axis_index_groups=halves, tiled=True)  3.53 us
  transfers between devices with their start and end apart: 3, of which 3 were waited for; matrix products, arithmetic and copies ran while one was open for 4% of the time, Pallas kernels for 4%

profile of v2, /device:TPU:6, one launch (start us, length us, event | category | flops | bytes accessed | tf_op | source)
XLA Modules:
  0.0 79.9 jit_solution(14207255629941204793)
XLA Ops:
  0.0 1.7 %split.1 = bf16[16,2,16,256]{3,2,1,0:T(8,128)(2,1)} custom-call(bf16[1,2,16,4096]{3,2,1,0:T(8,128)(2,1)} %source_ref.1), custom_call_target="tpu_custom_call" | custom-call | tf_op jit(solution)/shard_map/split/pallas_call | solution.py:339
  1.7 10.4 %all-to-all-start = ((bf16[16,2,16,256]{3,2,1,0:T(8,128)(2,1)}), bf16[16,2,16,256]{3,2,1,0:T(8,128)(2,1)S(1)}, u32[]{:S(2)}, u32[]{:S(2)}) async-start(bf16[16,2,16,256]{3,2,1,0:T(8,128)(2,1)} %split.1), calls=%async_computation | async-start | bytes 524288 | tf_op jit(solution)/shard_map/all_to_all | solution.py:347
  12.1 0.0 copy-start.5
  12.8 0.0 copy-done.5
  12.8 0.0 copy-start.4
  12.8 0.0 copy-start.3
  12.8 0.1 copy.14
  12.9 0.6 copy-done.4
  13.5 0.1 copy.13
  13.6 0.0 copy-done.3
  13.6 0.1 copy.15
  13.7 0.6 pad_add_fusion.place_ref
  14.2 0.7 maximum_bitcast_fusion.params_ref
  14.9 3.6 %prepare.1 = (f32[10,2,16,256]{3,2,1,0:T(8,128)}, bf16[64,32]{1,0:T(8,128)(2,1)}, bf16[32,32]{1,0:T(8,128)(2,1)}, bf16[64,64]{1,0:T(8,128)(2,1)}, s32[3,64,128]{...) custom-call(s32[3]{0:T(128)} %pad_add_fusion.place_ref, f32[1]{0:T(128)S(6)} %copy.17.wave_ref, ...), custom_call_target="tpu_custom_call" | custom-call | tf_op jit(solution)/shard_map/prepare/pallas_call | solution.py:348
  18.5 4.8 %all-to-all-done.data_ref = bf16[16,2,16,256]{3,2,1,0:T(8,128)(2,1)S(1)} async-done(((bf16[16,2,16,256]{3,2,1,0:T(8,128)(2,1)}), bf16[16,2,16,256]{3,2,1,0:T(8,128)(2,1)S(1)}, u32[]{:S(2)}, u32[]{:S(2)}) %all-to-all-start) | async-done | bytes 262176 | tf_op jit(solution)/shard_map/all_to_all | solution.py:347
  23.2 0.0 copy-start
  23.2 0.7 copy-done
  23.9 2.5 %merge.1 = bf16[16,2,16,256]{3,2,1,0:T(8,128)(2,1)} custom-call(bf16[16,2,16,256]{3,2,1,0:T(8,128)(2,1)} %copy-done, f32[10,2,16,256]{3,2,1,0:T(8,128)} %get-tuple-element.13.trig_ref, bf16[64,32]{1,0:T(8,128)(2,1)} %get-tuple-element.14.first_ref, bf16[32,32]{1,0:T(8,128)(2,1)} %get-tuple-element.15.second_ref, bf16[64,64]{1,0:T(8,128)(2,1)} %get-tuple-element.16.third_ref), custom_call_target="tpu_custom_call" | custom-call | tf_op jit(solution)/shard_map/merge/pallas_call | solution.py:382
  26.4 3.5 %all-to-all-start.1 = ((bf16[16,2,16,256]{3,2,1,0:T(8,128)(2,1)}), bf16[16,2,16,256]{3,2,1,0:T(8,128)(2,1)S(1)}, u32[]{:S(2)}, u32[]{:S(2)}) async-start(bf16[16,2,16,256]{3,2,1,0:T(8,128)(2,1)} %merge.1), calls=%async_computation.1 | async-start | bytes 524288 | tf_op jit(solution)/shard_map/all_to_all | solution.py:391
  29.9 0.8 broadcast_subtract_fusion
  30.7 10.6 %all-to-all-done.1.table_ref = bf16[16,2,16,256]{3,2,1,0:T(8,128)(2,1)S(1)} async-done(((bf16[16,2,16,256]{3,2,1,0:T(8,128)(2,1)}), bf16[16,2,16,256]{3,2,1,0:T(8,128)(2,1)S(1)}, u32[]{:S(2)}, u32[]{:S(2)}) %all-to-all-start.1) | async-done | bytes 262176 | tf_op jit(solution)/shard_map/all_to_all | solution.py:391
  41.3 0.0 copy-start.1
  41.3 0.7 copy-done.1
  42.0 7.1 %sample.1 = f32[128,128]{1,0:T(8,128)} custom-call(bf16[16,2,16,256]{3,2,1,0:T(8,128)(2,1)} %copy-done.1, s32[3,64,128]{2,1,0:T(8,128)} %get-tuple-element.17.whole_ref, f32[2,64,128]{2,1,0:T(8,128)} %get-tuple-element.18.real_ref, f32[3,64,128]{2,1,0:T(8,128)} %get-tuple-element.12.pixel_ref), custom_call_target="tpu_custom_call" | custom-call | tf_op jit(solution)/shard_map/sample/pallas_call | solution.py:392
  49.1 2.7 %collective-permute-start = (f32[128,128]{1,0:T(8,128)}, f32[128,128]{1,0:T(8,128)S(1)}, u32[]{:S(2)}, u32[]{:S(2)}) collective-permute-start(f32[128,128]{1,0:T(8,128)} %sample.1), channel_id=1, source_target_pairs={{1,0},{2,1},{3,2},{4,3},{5,4},{6,5},{7,6},{8,7},{9,8},{10,9},{11,1... | collective-permute-start | bytes 196616 | tf_op jit(solution)/shard_map/ppermute | solution.py:405
  51.8 0.8 slice_bitcast_fusion
  52.6 5.3 %collective-permute-done = f32[128,128]{1,0:T(8,128)S(1)} collective-permute-done((f32[128,128]{1,0:T(8,128)}, f32[128,128]{1,0:T(8,128)S(1)}, u32[]{:S(2)}, u32[]{:S(2)}) %collective-permute-start) | collective-permute-done | bytes 65568 | tf_op jit(solution)/shard_map/ppermute | solution.py:405
  57.9 0.0 copy-start.2
  58.0 0.8 copy-done.2
  58.8 20.5 %all_to_all.15 = f32[32,4,128]{2,1,0:T(4,128)S(1)} all-to-all(f32[32,4,128]{2,1,0:T(4,128)S(1)} %bitcast.31), channel_id=1, replica_groups=mesh['sub'=32,'hgt'=16] {'sub'}, dimensions={0} | all-to-all | bytes 131072 | tf_op jit(solution)/shard_map/all_to_all | solution.py:412
  79.3 0.6 reshape.44
  (9 shorter events, 0.1 us)
Async XLA Ops:
  1.7 21.6 %all-to-all-start = ((bf16[16,2,16,256]{3,2,1,0:T(8,128)(2,1)}), bf16[16,2,16,256]{3,2,1,0:T(8,128)(2,1)S(1)}, u32[]{:S(2)}, u32[]{:S(2)}) async-start(bf16[16,2,16,256]{3,2,1,0:T(8,128)(2,1)} %split.1), calls=%async_computation | async-start | bytes 524288 | tf_op jit(solution)/shard_map/all_to_all | solution.py:347
  12.1 0.7 copy-start.5
  12.8 0.7 copy-start.4
  12.8 0.8 copy-start.3
  23.2 0.7 copy-start
  26.4 14.9 %all-to-all-start.1 = ((bf16[16,2,16,256]{3,2,1,0:T(8,128)(2,1)}), bf16[16,2,16,256]{3,2,1,0:T(8,128)(2,1)S(1)}, u32[]{:S(2)}, u32[]{:S(2)}) async-start(bf16[16,2,16,256]{3,2,1,0:T(8,128)(2,1)} %merge.1), calls=%async_computation.1 | async-start | bytes 524288 | tf_op jit(solution)/shard_map/all_to_all | solution.py:391
  41.3 0.7 copy-start.1
  49.1 8.8 %collective-permute-start = (f32[128,128]{1,0:T(8,128)}, f32[128,128]{1,0:T(8,128)S(1)}, u32[]{:S(2)}, u32[]{:S(2)}) collective-permute-start(f32[128,128]{1,0:T(8,128)} %sample.1), channel_id=1, source_target_pairs={{1,0},{2,1},{3,2},{4,3},{5,4},{6,5},{7,6},{8,7},{9,8},{10,9},{11,1... | collective-permute-start | bytes 196616 | tf_op jit(solution)/shard_map/ppermute | solution.py:405
  57.9 0.8 %copy-start.2 = (f32[128,128]{1,0:T(8,128)S(1)}, f32[128,128]{1,0:T(8,128)}, u32[]{:S(2)}) copy-start(f32[128,128]{1,0:T(8,128)} %sample.1) | copy-start | bytes 196612

commit v3 on v2

--- a/solution.py
+++ b/solution.py
@@ -51,6 +51,7 @@
     whole_ref,
     real_ref,
     pixel_ref,
+    height_ref,
     *,
     range_count,
 ):
@@ -127,7 +128,8 @@
     angles = (wave * range_phase) * (samples.astype(jnp.float32) + fracs[1])
     pixel_ref[0] = jnp.cos(angles)
     pixel_ref[1] = jnp.sin(angles)
-    pixel_ref[2] = fracs[2]
+    for part in range(2):
+        height_ref[pl.ds(part, ROWS, stride=2), :] = fracs[2]
     first_beam = place_ref[2] * 8 - HALO
     for group in range(ROWS // 32):
         rows = [slice(group * 32 + 8 * j, group * 32 + 8 * j + 8) for j in range(4)]
@@ -251,12 +253,12 @@
     def flat(value):
         return jnp.concatenate([value[i : i + 1, :] for i in range(4)], axis=1)
 
-    def chunk(step, carry):
+    def chunk(quarter, step):
         place = pl.ds(step * 4, 4)
         inner, outer, beam = (flat(whole_ref[i, place, :]) for i in range(3))
         frac0, frac1 = (flat(real_ref[i, place, :]) for i in range(2))
         hot = jnp.where(row_ids == inner, 1.0, 0.0).astype(jnp.bfloat16)
-        product = jnp.dot(lhs_ref[step >> 2], hot, preferred_element_type=jnp.float32)
+        product = jnp.dot(lhs_ref[quarter], hot, preferred_element_type=jnp.float32)
         picked = product[0:rows]
         for k in range(1, blocks):
             picked = jnp.where(outer == k, product[k * rows : (k + 1) * rows], picked)
@@ -271,9 +273,13 @@
             summed = jnp.sum(low_weights * low + high_weights * high, axis=0, keepdims=True)
             for i in range(4):
                 cart_ref[part, pl.ds(step * 4 + i, 1), :] = summed[:, i * LANES : (i + 1) * LANES]
+
+    def window(quarter, carry):
+        for i in range(4):
+            chunk(quarter, quarter * 4 + i)
         return carry
 
-    lax.fori_loop(0, whole_ref.shape[1] // 4, chunk, 0)
+    lax.fori_loop(0, 4, window, 0)
     for group in range(ROWS // 32):
         ordered = [
             swap_quarters(
@@ -336,6 +342,11 @@
     shape = jax.ShapeDtypeStruct
     f32, bf16 = jnp.float32, jnp.bfloat16
 
+    kept = shape if interpret else pltpu.VMEM
+
+    def local(value):
+        return value if interpret else pltpu.with_memory_space_constraint(value, pltpu.VMEM)
+
     slices = pl.pallas_call(
         split_kernel,
         out_shape=shape((members, 2, beams, width), bf16),
@@ -344,17 +355,18 @@
         interpret=interpret,
         name="split",
     )(polar_beams)
-    slices = lax.all_to_all(slices, "sub", 0, 0, axis_index_groups=halves, tiled=True)
-    trig, first, second, third, whole, real, pixel = pl.pallas_call(
+    slices = local(lax.all_to_all(slices, "sub", 0, 0, axis_index_groups=halves, tiled=True))
+    trig, first, second, third, whole, real, pixel, height = pl.pallas_call(
         functools.partial(prepare_kernel, range_count=range_count),
         out_shape=[
-            shape((10, 2, beams, width), f32),
-            shape((4 * beams, 2 * beams), bf16),
-            shape((2 * beams, 2 * beams), bf16),
-            shape((4 * beams, 4 * beams), bf16),
-            shape((3, row_count, LANES), jnp.int32),
-            shape((2, row_count, LANES), f32),
-            shape((3, row_count, LANES), f32),
+            kept((10, 2, beams, width), f32),
+            kept((4 * beams, 2 * beams), bf16),
+            kept((2 * beams, 2 * beams), bf16),
+            kept((4 * beams, 4 * beams), bf16),
+            kept((3, row_count, LANES), jnp.int32),
+            kept((2, row_count, LANES), f32),
+            kept((2, row_count, LANES), f32),
+            shape((2 * row_count, LANES), f32),
         ],
         grid_spec=pltpu.PrefetchScalarGridSpec(
             num_scalar_prefetch=1,
@@ -373,7 +385,8 @@
                 pl.BlockSpec((4 * beams, 4 * beams), lambda i, p: (0, 0)),
                 pl.BlockSpec((3, row_count, LANES), lambda i, p: (0, 0, 0)),
                 pl.BlockSpec((2, row_count, LANES), lambda i, p: (0, 0, 0)),
-                pl.BlockSpec((3, row_count, LANES), lambda i, p: (0, 0, 0)),
+                pl.BlockSpec((2, row_count, LANES), lambda i, p: (0, 0, 0)),
+                pl.BlockSpec((2 * row_count, LANES), lambda i, p: (0, 0)),
             ],
         ),
         interpret=interpret,
@@ -387,8 +400,8 @@
         scratch_shapes=[pltpu.VMEM((2, 144, width), f32)],
         interpret=interpret,
         name="merge",
-    )(slices, trig, first, second, third)
-    table = lax.all_to_all(windows, "sub", 0, 0, axis_index_groups=halves, tiled=True)
+    )(slices, local(trig), local(first), local(second), local(third))
+    table = local(lax.all_to_all(windows, "sub", 0, 0, axis_index_groups=halves, tiled=True))
     cart = pl.pallas_call(
         sample_kernel,
         out_shape=shape((2 * row_count, LANES), f32),
@@ -401,15 +414,12 @@
         ],
         interpret=interpret,
         name="sample",
-    )(table, whole, real, pixel)
+    )(table, local(whole), local(real), local(pixel))
     above = lax.ppermute(cart, "hgt", [(i, i - 1) for i in range(1, layers)])
-    height_frac = pixel[2][:, None, :]
-    blended = (1.0 - height_frac) * cart.reshape(row_count, 2, LANES) + (
-        height_frac * above.reshape(row_count, 2, LANES)
-    )
+    blended = (1.0 - height) * cart + height * above
     tile_rows = row_count // sub_count
-    blended = blended.reshape(sub_count, tile_rows * 2, LANES)
-    tiles = lax.all_to_all(blended, "sub", 0, 0, tiled=True)
+    blended = blended.astype(bf16).reshape(sub_count, tile_rows * 2, LANES)
+    tiles = lax.all_to_all(blended, "sub", 0, 0, tiled=True).astype(f32)
     tiles = tiles.reshape(sub_count // 4, 2, 2, tile_rows * 2, LANES)
     tiles = (tiles[:, 0] + tiles[:, 1]).reshape(members, tile_rows * 2, LANES)
     return tiles.transpose(1, 0, 2).reshape(tile_rows, 1, 2, column_count)

time: 80.9 us -> 75.4 us (0.932)
  blocking collectives: 20.5 us -> 35.3 us
  waiting for transfers between devices: 20.6 us -> 10.8 us
  Pallas kernels: 14.8 us -> 10.8 us
  starting transfers between devices: 16.7 us -> 13.1 us
  local copies, waits for them, and re-layouts: 4.52 us -> 1.51 us
    all_to_all x1 -> x2, blocking collectives: 20.5 us -> 35.3 us  [the longest x1 20.5 us: body(): tiles = lax.all_to_all(blended, 'sub', 0, 0, tiled=True).astype(f32)]
    all_to_all x1 -> x0, waiting for transfers between devices: 10.6 us -> none  [body(): lax.all_to_all(windows, 'sub', 0, 0, axis_index_groups=halves, tiled=True)]
    all_to_all x1 -> x0, starting transfers between devices: 3.53 us -> none  [body(): lax.all_to_all(windows, 'sub', 0, 0, axis_index_groups=halves, tiled=True)]
    pallas_call x1, Pallas kernels: 7.13 us -> 4.34 us  [body(): pl.pallas_call(sample_kernel, out_shape=shape((2 * row_count, LANES), f32...]
    unnamed x12 -> x8, local copies, waits for them, and re-layouts: 2.82 us -> 0.62 us
    pallas_call x1, Pallas kernels: 2.46 us -> 1.38 us  [body(): pl.pallas_call(functools.partial(merge_kernel, groups=sub_count // 2 ** l...]
    convert_element_type x0 -> x1, other arithmetic: none -> 0.86 us  [body(): blended = blended.astype(bf16).reshape(sub_count, tile_rows * 2, LANES)]
  transfers between devices with their start and end apart: 3 -> 2, of which waited for: 3 -> 2; matrix products, arithmetic and copies ran while one was open for 4% -> 2% of each run, Pallas kernels for 4% -> 5%
where the time goes in v3:
time: 75.4 us; the launch traced here: 74.5 us
  blocking collectives  35.3 us (47%)
  starting transfers between devices  13.1 us (17%)
  Pallas kernels  10.8 us (14%)
  waiting for transfers between devices  10.8 us (14%)
  other arithmetic  2.23 us (3%)
  local copies, waits for them, and re-layouts  1.51 us (2%)
    all_to_all x1, blocking collectives, body(): tiles = lax.all_to_all(blended, 'sub', 0, 0, tiled=True).astype(f32)  20.5 us
    all_to_all x1, blocking collectives, body(): lax.all_to_all(windows, 'sub', 0, 0, axis_index_groups=halves, tiled=True)  14.8 us
    all_to_all x1, starting transfers between devices, body(): lax.all_to_all(slices, 'sub', 0, 0, axis_index_groups=halves, tiled=True)  10.4 us
    ppermute x1, waiting for transfers between devices, body(): above = lax.ppermute(cart, 'hgt', [(i, i - 1) for i in range(1, layers)])  6 us
    all_to_all x1, waiting for transfers between devices, body(): lax.all_to_all(slices, 'sub', 0, 0, axis_index_groups=halves, tiled=True)  4.81 us
    pallas_call x1, Pallas kernels, body(): pl.pallas_call(sample_kernel, out_shape=shape((2 * row_count, LANES), f32...  4.34 us
    pallas_call x1, Pallas kernels, body(): pl.pallas_call(functools.partial(prepare_kernel, range_count=range_count)...  3.43 us
    ppermute x1, starting transfers between devices, body(): above = lax.ppermute(cart, 'hgt', [(i, i - 1) for i in range(1, layers)])  2.72 us
  transfers between devices with their start and end apart: 2, of which 2 were waited for; matrix products, arithmetic and copies ran while one was open for 2% of the time, Pallas kernels for 5%

profile of v3, /device:TPU:6, one launch (start us, length us, event | category | flops | bytes accessed | tf_op | source)
XLA Modules:
  0.0 74.5 jit_solution(11032977945797439213)
XLA Ops:
  0.0 1.7 %split.1 = bf16[16,2,16,256]{3,2,1,0:T(8,128)(2,1)} custom-call(bf16[1,2,16,4096]{3,2,1,0:T(8,128)(2,1)} %source_ref.1), custom_call_target="tpu_custom_call" | custom-call | tf_op jit(solution)/shard_map/split/pallas_call | solution.py:350
  1.7 10.4 %all-to-all-start = ((bf16[16,2,16,256]{3,2,1,0:T(8,128)(2,1)}), bf16[16,2,16,256]{3,2,1,0:T(8,128)(2,1)S(1)}, u32[]{:S(2)}, u32[]{:S(2)}) async-start(bf16[16,2,16,256]{3,2,1,0:T(8,128)(2,1)} %split.1), calls=%async_computation | async-start | bytes 524288 | tf_op jit(solution)/shard_map/all_to_all | solution.py:358
  12.1 0.0 copy-start.3
  12.8 0.0 copy-done.3
  12.8 0.0 copy-start.2
  12.8 0.0 copy-start.1
  12.8 0.1 copy.14
  12.9 0.6 copy-done.2
  13.5 0.1 copy.13
  13.6 0.0 copy-done.1
  13.6 0.1 copy.15
  13.7 0.7 pad_add_fusion.place_ref
  14.3 0.7 maximum_bitcast_fusion.params_ref
  15.0 3.4 %prepare.1 = (f32[10,2,16,256]{3,2,1,0:T(8,128)S(1)}, bf16[64,32]{1,0:T(8,128)(2,1)S(1)}, bf16[32,32]{1,0:T(8,128)(2,1)S(1)}, bf16[64,64]{1,0:T(8,128)(2,1)S(1)}...) custom-call(s32[3]{0:T(128)} %pad_add_fusion.place_ref, ...), custom_call_target="tpu_custom_call" | custom-call | tf_op jit(solution)/shard_map/prepare/pallas_call | solution.py:359
  18.4 4.8 %all-to-all-done.data_ref = bf16[16,2,16,256]{3,2,1,0:T(8,128)(2,1)S(1)} async-done(((bf16[16,2,16,256]{3,2,1,0:T(8,128)(2,1)}), bf16[16,2,16,256]{3,2,1,0:T(8,128)(2,1)S(1)}, u32[]{:S(2)}, u32[]{:S(2)}) %all-to-all-start) | async-done | bytes 262176 | tf_op jit(solution)/shard_map/all_to_all | solution.py:358
  23.2 1.4 %merge.1 = bf16[16,2,16,256]{3,2,1,0:T(8,128)(2,1)} custom-call(bf16[16,2,16,256]{3,2,1,0:T(8,128)(2,1)S(1)} %all-to-all-done.data_ref, f32[10,2,16,256]{3,2,1,0:T(8,128)S(1)} %get-tuple-element.14.trig_ref, bf16[64,32]{1,0:T(8,128)(2,1)S(1)} %get-tuple-element.15.first_ref, bf16[32,32]{1,0:T(8,128)(2,1)S(1)} %get-tuple-element.16.second_ref, ...), custom_call_target="tpu_custom_call" | custom-call | tf_op jit(solution)/shard_map/merge/pallas_call | solution.py:395
  24.6 14.8 %all_to_all.15.table_ref = bf16[16,2,16,256]{3,2,1,0:T(8,128)(2,1)S(1)} all-to-all(bf16[16,2,16,256]{3,2,1,0:T(8,128)(2,1)} %merge.1), channel_id=1, replica_groups={{0,16,64,80,128,144,192,208,256,272,320,336,384,400,448,464},{32,48,96,..., dimensions={0} | all-to-all | bytes 524288 | tf_op jit(solution)/shard_map/all_to_all | solution.py:404
  39.5 0.0 copy-start
  39.5 4.3 %sample.1 = f32[128,128]{1,0:T(8,128)} custom-call(bf16[16,2,16,256]{3,2,1,0:T(8,128)(2,1)S(1)} %all_to_all.15.table_ref, s32[3,64,128]{2,1,0:T(8,128)S(1)} %get-tuple-element.18.whole_ref, f32[2,64,128]{2,1,0:T(8,128)S(1)} %get-tuple-element.19.real_ref, f32[2,64,128]{2,1,0:T(8,128)S(1)} %get-tuple-element.20.pixel_ref), custom_call_target="tpu_custom_call" | custom-call | tf_op jit(solution)/shard_map/sample/pallas_call | solution.py:405
  43.8 2.7 %collective-permute-start = (f32[128,128]{1,0:T(8,128)}, f32[128,128]{1,0:T(8,128)S(1)}, u32[]{:S(2)}, u32[]{:S(2)}) collective-permute-start(f32[128,128]{1,0:T(8,128)} %sample.1), channel_id=1, source_target_pairs={{1,0},{2,1},{3,2},{4,3},{5,4},{6,5},{7,6},{8,7},{9,8},{10,9},{11,1... | collective-permute-start | bytes 196616 | tf_op jit(solution)/shard_map/ppermute | solution.py:418
  46.5 6.0 %collective-permute-done = f32[128,128]{1,0:T(8,128)S(1)} collective-permute-done((f32[128,128]{1,0:T(8,128)}, f32[128,128]{1,0:T(8,128)S(1)}, u32[]{:S(2)}, u32[]{:S(2)}) %collective-permute-start) | collective-permute-done | bytes 65568 | tf_op jit(solution)/shard_map/ppermute | solution.py:418
  52.5 0.0 copy-done
  52.5 0.9 %add_convert_fusion = bf16[128,128]{1,0:T(8,128)(2,1)S(1)} fusion(f32[128,128]{1,0:T(8,128)S(1)} %copy-done, f32[128,128]{1,0:T(8,128)S(1)} %collective-permute-done, f32[128,128]{1,0:T(8,128)} %sample.1), kind=kLoop, calls=%fused_computation | loop fusion | flops 81920 | bytes 229376 | tf_op jit(solution)/shard_map/convert_element_type | solution.py:421
  53.4 20.5 %all_to_all.16 = bf16[32,4,128]{2,1,0:T(4,128)(2,1)S(1)} all-to-all(bf16[32,4,128]{2,1,0:T(4,128)(2,1)S(1)} %bitcast.17), channel_id=1, replica_groups=mesh['sub'=32,'hgt'=16] {'sub'}, dimensions={0} | all-to-all | bytes 65536 | tf_op jit(solution)/shard_map/all_to_all | solution.py:422
  73.9 0.6 reshape.31
  (7 shorter events, 0.1 us)
Async XLA Ops:
  1.7 21.6 %all-to-all-start = ((bf16[16,2,16,256]{3,2,1,0:T(8,128)(2,1)}), bf16[16,2,16,256]{3,2,1,0:T(8,128)(2,1)S(1)}, u32[]{:S(2)}, u32[]{:S(2)}) async-start(bf16[16,2,16,256]{3,2,1,0:T(8,128)(2,1)} %split.1), calls=%async_computation | async-start | bytes 524288 | tf_op jit(solution)/shard_map/all_to_all | solution.py:358
  12.1 0.7 copy-start.3
  12.8 0.7 copy-start.2
  12.8 0.8 %copy-start.1 = (bf16[3,2,2,16,8]{3,4,2,1,0:T(8,128)(2,1)S(1)}, bf16[3,2,2,16,8]{3,4,2,1,0:T(8,128)(2,1)}, u32[]{:S(2)}) copy-start(bf16[3,2,2,16,8]{3,4,2,1,0:T(8,128)(2,1)} %param.10) | copy-start | bytes 9220
  39.5 13.1 %copy-start = (f32[128,128]{1,0:T(8,128)S(1)}, f32[128,128]{1,0:T(8,128)}, u32[]{:S(2)}) copy-start(f32[128,128]{1,0:T(8,128)} %get-tuple-element.13) | copy-start | bytes 196612
  43.8 8.7 %collective-permute-start = (f32[128,128]{1,0:T(8,128)}, f32[128,128]{1,0:T(8,128)S(1)}, u32[]{:S(2)}, u32[]{:S(2)}) collective-permute-start(f32[128,128]{1,0:T(8,128)} %sample.1), channel_id=1, source_target_pairs={{1,0},{2,1},{3,2},{4,3},{5,4},{6,5},{7,6},{8,7},{9,8},{10,9},{11,1... | collective-permute-start | bytes 196616 | tf_op jit(solution)/shard_map/ppermute | solution.py:418

commit v4 on v3

--- a/solution.py
+++ b/solution.py
@@ -15,11 +15,18 @@
 ROWS = 64
 
 
-def split_kernel(source_ref, out_ref):
+def split_kernel(source_ref, out_ref, semaphores):
     width = out_ref.shape[3]
-    for i in range(out_ref.shape[0]):
-        for part in range(out_ref.shape[1]):
-            out_ref[i, part] = source_ref[0, part, :, i * width : (i + 1) * width]
+    copies = [
+        pltpu.make_async_copy(
+            source_ref.at[0, :, :, pl.ds(i * width, width)], out_ref.at[i], semaphores.at[i]
+        )
+        for i in range(out_ref.shape[0])
+    ]
+    for copy in copies:
+        copy.start()
+    for copy in copies:
+        copy.wait()
 
 
 def swap_quarters(values):
@@ -51,7 +58,6 @@
     whole_ref,
     real_ref,
     pixel_ref,
-    height_ref,
     *,
     range_count,
 ):
@@ -124,12 +130,10 @@
     second_ref[...] = jnp.concatenate(rows, axis=0).astype(jnp.bfloat16)
 
     samples = range_ref[...]
-    fracs = [frac_ref[i].astype(jnp.float32) for i in range(3)]
+    fracs = [frac_ref[i].astype(jnp.float32) for i in range(2)]
     angles = (wave * range_phase) * (samples.astype(jnp.float32) + fracs[1])
     pixel_ref[0] = jnp.cos(angles)
     pixel_ref[1] = jnp.sin(angles)
-    for part in range(2):
-        height_ref[pl.ds(part, ROWS, stride=2), :] = fracs[2]
     first_beam = place_ref[2] * 8 - HALO
     for group in range(ROWS // 32):
         rows = [slice(group * 32 + 8 * j, group * 32 + 8 * j + 8) for j in range(4)]
@@ -138,8 +142,10 @@
         frac_parts = [swap_quarters([fracs[i][r] for r in rows]) for i in range(2)]
         for quarter in range(4):
             place = slice(quarter * 16 + group * 8, quarter * 16 + group * 8 + 8)
-            whole_ref[0, place, :] = sample_parts[quarter] & (width - 1)
-            whole_ref[1, place, :] = sample_parts[quarter] >> (width.bit_length() - 1)
+            sample = sample_parts[quarter]
+            block = (sample + 1 + (sample >> 8)) >> 8
+            whole_ref[0, place, :] = sample - block * (width - 1)
+            whole_ref[1, place, :] = block
             whole_ref[2, place, :] = beam_parts[quarter] - (2 * quarter + 2)
             for i in range(2):
                 real_ref[i, place, :] = frac_parts[i][quarter]
@@ -223,60 +229,84 @@
             out_ref[block, part] = rows.astype(jnp.bfloat16)
 
 
+def flat(value):
+    return jnp.concatenate([value[i : i + 1, :] for i in range(4)], axis=1)
+
+
+def range_columns(whole_ref, real_ref, step, width):
+    place = pl.ds(step * 4, 4)
+    row_ids = lax.broadcasted_iota(jnp.int32, (width, 4 * LANES), 0)
+    offset = row_ids - flat(whole_ref[0, place, :])
+    frac = flat(real_ref[1, place, :])
+    column = jnp.where(offset == 0, 1.0 - frac, jnp.where(offset == 1, frac, 0.0))
+    return column.astype(jnp.bfloat16)
+
+
+def weights_kernel(after_ref, whole_ref, real_ref, out_ref):
+    del after_ref
+
+    def chunk(step, carry):
+        out_ref[step] = range_columns(whole_ref, real_ref, 2 * step, out_ref.shape[1])
+        return carry
+
+    lax.fori_loop(0, out_ref.shape[0], chunk, 0)
+
+
 def sample_kernel(
-    table_ref, whole_ref, real_ref, pixel_ref, out_ref, pair_ref, lhs_ref, cart_ref
+    table_ref,
+    column_ref,
+    whole_ref,
+    real_ref,
+    pixel_ref,
+    out_ref,
+    block_ref,
+    lhs_ref,
+    cart_ref,
+    order_ref,
 ):
-    blocks, parts, _, width = table_ref.shape
-    rows = 2 * parts * QUARTER
+    slices, parts, _, width = table_ref.shape
+    blocks = slices + 1
+    rows = parts * QUARTER
     lane = lax.broadcasted_iota(jnp.int32, (WINDOW, width), 1)
     for part in range(parts):
-        values = [table_ref[i, part].astype(jnp.float32) for i in range(blocks)]
-        rolled = [pltpu.roll(v, width - 1, 1) for v in values]
-        for i in range(blocks):
-            pair_ref[0, i, part] = values[i]
-            pair_ref[1, i, part] = jnp.where(
-                lane < width - 1, rolled[i], rolled[(i + 1) % blocks]
-            )
+        values = [table_ref[i, part].astype(jnp.float32) for i in range(slices)]
+        block_ref[0, part] = values[0]
+        for k in range(1, blocks):
+            before = pltpu.roll(values[k - 1], k, 1)
+            after = pltpu.roll(values[k], k, 1) if k < slices else before
+            block_ref[k, part] = jnp.where(lane < k, before, after)
     for quarter in range(4):
         low = 2 * quarter + 2
-        for i in range(blocks):
-            for tap in range(2):
-                pair = [pair_ref[tap, i, part, low : low + QUARTER, :] for part in range(parts)]
-                row = i * rows + tap * parts * QUARTER
-                lhs_ref[quarter, row : row + parts * QUARTER, :] = jnp.concatenate(
-                    pair, axis=0
-                ).astype(jnp.bfloat16)
-    pixels = 4 * LANES
-    row_ids = lax.broadcasted_iota(jnp.int32, (width, pixels), 0)
-    beam_ids = lax.broadcasted_iota(jnp.int32, (QUARTER, pixels), 0)
-
-    def flat(value):
-        return jnp.concatenate([value[i : i + 1, :] for i in range(4)], axis=1)
-
-    def chunk(quarter, step):
+        for k in range(blocks):
+            pair = [block_ref[k, part, low : low + QUARTER, :] for part in range(parts)]
+            lhs_ref[quarter, k * rows : (k + 1) * rows, :] = jnp.concatenate(pair, axis=0).astype(
+                jnp.bfloat16
+            )
+    beam_ids = lax.broadcasted_iota(jnp.int32, (QUARTER, column_ref.shape[2]), 0)
+
+    def chunk(quarter, step, columns):
         place = pl.ds(step * 4, 4)
-        inner, outer, beam = (flat(whole_ref[i, place, :]) for i in range(3))
-        frac0, frac1 = (flat(real_ref[i, place, :]) for i in range(2))
-        hot = jnp.where(row_ids == inner, 1.0, 0.0).astype(jnp.bfloat16)
-        product = jnp.dot(lhs_ref[quarter], hot, preferred_element_type=jnp.float32)
+        outer, beam = flat(whole_ref[1, place, :]), flat(whole_ref[2, place, :])
+        frac = flat(real_ref[0, place, :])
+        product = jnp.dot(lhs_ref[quarter], columns, preferred_element_type=jnp.float32)
         picked = product[0:rows]
         for k in range(1, blocks):
             picked = jnp.where(outer == k, product[k * rows : (k + 1) * rows], picked)
         weights = jnp.where(
-            beam_ids == beam, 1.0 - frac0, jnp.where(beam_ids == beam + 1, frac0, 0.0)
+            beam_ids == beam, 1.0 - frac, jnp.where(beam_ids == beam + 1, frac, 0.0)
         )
-        low_weights = weights * (1.0 - frac1)
-        high_weights = weights * frac1
         for part in range(parts):
-            low = picked[part * QUARTER : (part + 1) * QUARTER]
-            high = picked[(parts + part) * QUARTER : (parts + part + 1) * QUARTER]
-            summed = jnp.sum(low_weights * low + high_weights * high, axis=0, keepdims=True)
+            summed = jnp.sum(
+                weights * picked[part * QUARTER : (part + 1) * QUARTER], axis=0, keepdims=True
+            )
             for i in range(4):
                 cart_ref[part, pl.ds(step * 4 + i, 1), :] = summed[:, i * LANES : (i + 1) * LANES]
 
     def window(quarter, carry):
-        for i in range(4):
-            chunk(quarter, quarter * 4 + i)
+        for i in range(2):
+            step = quarter * 4 + 2 * i
+            chunk(quarter, step, column_ref[quarter * 2 + i])
+            chunk(quarter, step + 1, range_columns(whole_ref, real_ref, step + 1, width))
         return carry
 
     lax.fori_loop(0, 4, window, 0)
@@ -295,8 +325,9 @@
             cosine = pixel_ref[0, start : start + 8, :]
             sine = pixel_ref[1, start : start + 8, :]
             real, imag = ordered[0][j], ordered[1][j]
-            out_ref[pl.ds(2 * start, 8, stride=2), :] = cosine * real - sine * imag
-            out_ref[pl.ds(2 * start + 1, 8, stride=2), :] = sine * real + cosine * imag
+            order_ref[pl.ds(2 * start, 8, stride=2), :] = cosine * real - sine * imag
+            order_ref[pl.ds(2 * start + 1, 8, stride=2), :] = sine * real + cosine * imag
+    out_ref[...] = order_ref[...].astype(jnp.bfloat16)
 
 
 def body(
@@ -339,7 +370,9 @@
     ).T
     smem = pl.BlockSpec(memory_space=pltpu.SMEM)
     vmem = pl.BlockSpec(memory_space=pltpu.VMEM)
+    far = pl.BlockSpec(memory_space=pl.ANY if interpret else pltpu.HBM)
     shape = jax.ShapeDtypeStruct
+    limit = pltpu.CompilerParams(vmem_limit_bytes=24 * 2**20)
     f32, bf16 = jnp.float32, jnp.bfloat16
 
     kept = shape if interpret else pltpu.VMEM
@@ -350,13 +383,14 @@
     slices = pl.pallas_call(
         split_kernel,
         out_shape=shape((members, 2, beams, width), bf16),
-        in_specs=[vmem],
-        out_specs=vmem,
+        in_specs=[far],
+        out_specs=far,
+        scratch_shapes=[pltpu.SemaphoreType.DMA((members,))],
         interpret=interpret,
         name="split",
     )(polar_beams)
     slices = local(lax.all_to_all(slices, "sub", 0, 0, axis_index_groups=halves, tiled=True))
-    trig, first, second, third, whole, real, pixel, height = pl.pallas_call(
+    trig, first, second, third, whole, real, pixel = pl.pallas_call(
         functools.partial(prepare_kernel, range_count=range_count),
         out_shape=[
             kept((10, 2, beams, width), f32),
@@ -366,7 +400,6 @@
             kept((3, row_count, LANES), jnp.int32),
             kept((2, row_count, LANES), f32),
             kept((2, row_count, LANES), f32),
-            shape((2 * row_count, LANES), f32),
         ],
         grid_spec=pltpu.PrefetchScalarGridSpec(
             num_scalar_prefetch=1,
@@ -376,7 +409,7 @@
                 pl.BlockSpec((beams, params.shape[1]), lambda i, p: (0, 0)),
                 pl.BlockSpec((row_count, LANES), lambda i, p: (0, p[0])),
                 pl.BlockSpec((row_count, LANES), lambda i, p: (0, p[0])),
-                pl.BlockSpec((3, row_count, LANES), lambda i, p: (0, 0, p[0])),
+                pl.BlockSpec((2, row_count, LANES), lambda i, p: (0, 0, p[0])),
             ],
             out_specs=[
                 pl.BlockSpec((10, 2, beams, width), lambda i, p: (0, 0, 0, 0)),
@@ -386,7 +419,6 @@
                 pl.BlockSpec((3, row_count, LANES), lambda i, p: (0, 0, 0)),
                 pl.BlockSpec((2, row_count, LANES), lambda i, p: (0, 0, 0)),
                 pl.BlockSpec((2, row_count, LANES), lambda i, p: (0, 0, 0)),
-                pl.BlockSpec((2 * row_count, LANES), lambda i, p: (0, 0)),
             ],
         ),
         interpret=interpret,
@@ -394,35 +426,50 @@
     )(place, layer_wave, params, beam_map, range_map, pixel_frac)
     windows = pl.pallas_call(
         functools.partial(merge_kernel, groups=sub_count // 2**levels),
-        out_shape=shape((members, 2, WINDOW, width), bf16),
+        out_shape=kept((members, 2, WINDOW, width), bf16),
         in_specs=[vmem] * 5,
         out_specs=vmem,
         scratch_shapes=[pltpu.VMEM((2, 144, width), f32)],
+        compiler_params=limit,
         interpret=interpret,
         name="merge",
     )(slices, local(trig), local(first), local(second), local(third))
     table = local(lax.all_to_all(windows, "sub", 0, 0, axis_index_groups=halves, tiled=True))
+    columns = pl.pallas_call(
+        weights_kernel,
+        out_shape=kept((row_count // 8, width, 4 * LANES), bf16),
+        in_specs=[pl.BlockSpec(memory_space=pl.ANY), vmem, vmem],
+        out_specs=vmem,
+        compiler_params=limit,
+        interpret=interpret,
+        name="weights",
+    )(windows, local(whole), local(real))
     cart = pl.pallas_call(
         sample_kernel,
-        out_shape=shape((2 * row_count, LANES), f32),
-        in_specs=[vmem] * 4,
+        out_shape=shape((2 * row_count, LANES), bf16),
+        in_specs=[vmem] * 5,
         out_specs=vmem,
         scratch_shapes=[
-            pltpu.VMEM((2, members, 2, WINDOW, width), f32),
-            pltpu.VMEM((4, members * 4 * QUARTER, width), bf16),
+            pltpu.VMEM((members + 1, 2, WINDOW, width), f32),
+            pltpu.VMEM((4, (members + 1) * 2 * QUARTER, width), bf16),
             pltpu.VMEM((2, row_count, LANES), f32),
+            pltpu.VMEM((2 * row_count, LANES), f32),
         ],
+        compiler_params=limit,
         interpret=interpret,
         name="sample",
-    )(table, local(whole), local(real), local(pixel))
-    above = lax.ppermute(cart, "hgt", [(i, i - 1) for i in range(1, layers)])
-    blended = (1.0 - height) * cart + height * above
+    )(table, local(columns), local(whole), local(real), local(pixel))
     tile_rows = row_count // sub_count
-    blended = blended.astype(bf16).reshape(sub_count, tile_rows * 2, LANES)
-    tiles = lax.all_to_all(blended, "sub", 0, 0, tiled=True).astype(f32)
+    tiles = cart.reshape(sub_count, tile_rows * 2, LANES)
+    tiles = lax.all_to_all(tiles, "sub", 0, 0, tiled=True).astype(f32)
     tiles = tiles.reshape(sub_count // 4, 2, 2, tile_rows * 2, LANES)
-    tiles = (tiles[:, 0] + tiles[:, 1]).reshape(members, tile_rows * 2, LANES)
-    return tiles.transpose(1, 0, 2).reshape(tile_rows, 1, 2, column_count)
+    tile = (tiles[:, 0] + tiles[:, 1]).reshape(members, tile_rows, 2, LANES)
+    above = lax.ppermute(tile, "hgt", [(i, i - 1) for i in range(1, layers)])
+    height = lax.dynamic_slice_in_dim(pixel_frac[2], sub_index * tile_rows, tile_rows, 0)
+    height = height.astype(f32).reshape(tile_rows, members, LANES).transpose(1, 0, 2)
+    height = height[:, :, None, :]
+    blended = (1.0 - height) * tile + height * above
+    return blended.transpose(1, 2, 0, 3).reshape(tile_rows, 1, 2, column_count)
 
 
 def solution(mesh):

time: 75.4 us -> 80.6 us (1.069)
  blocking collectives: 35.3 us -> 0 us
  waiting for transfers between devices: 10.8 us -> 31.8 us
  starting transfers between devices: 13.1 us -> 25.4 us
  Pallas kernels: 10.8 us -> 17.7 us
    all_to_all x2 -> x0, blocking collectives: 35.3 us -> none  [the longest x1 20.5 us: body(): tiles = lax.all_to_all(blended, 'sub', 0, 0, tiled=True).astype(f32)]
    all_to_all x0 -> x2, waiting for transfers between devices: none -> 22.6 us  [the longest x1 12.2 us: body(): tiles = lax.all_to_all(tiles, 'sub', 0, 0, tiled=True).astype(f32)]
    all_to_all x0 -> x2, starting transfers between devices: none -> 12.2 us  [the longest x1 8.7 us: body(): tiles = lax.all_to_all(tiles, 'sub', 0, 0, tiled=True).astype(f32)]
    pallas_call x1, Pallas kernels: 1.66 us -> 9.18 us  [body(): pl.pallas_call(split_kernel, out_shape=shape((members, 2, beams, width),...]
    convert_element_type x1 -> x0, other arithmetic: 0.86 us -> none  [body(): blended = blended.astype(bf16).reshape(sub_count, tile_rows * 2, LANES)]
    ppermute x1, waiting for transfers between devices: 6 us -> 5.15 us  [body(): above = lax.ppermute(tile, 'hgt', [(i, i - 1) for i in range(1, layers)])]
    pallas_call x1 -> x2, Pallas kernels: 4.34 us -> 4.32 us  [the longest x1 3.49 us: body(): pl.pallas_call(sample_kernel, out_shape=shape((2 * row_count, LANES), bf1...]
  transfers between devices with their start and end apart: 2 -> 4, of which waited for: 2 -> 4; matrix products, arithmetic and copies ran while one was open for 2% -> 5% of each run, Pallas kernels for 5% -> 5%
where the time goes in v4:
time: 80.6 us; the launch traced here: 80.1 us
  waiting for transfers between devices  31.8 us (39%)
  starting transfers between devices  25.4 us (32%)
  Pallas kernels  17.7 us (22%)
  other arithmetic  2.77 us (3%)
  local copies, waits for them, and re-layouts  1.6 us (2%)
    all_to_all x1, waiting for transfers between devices, body(): tiles = lax.all_to_all(tiles, 'sub', 0, 0, tiled=True).astype(f32)  12.2 us
    all_to_all x1, waiting for transfers between devices, body(): lax.all_to_all(windows, 'sub', 0, 0, axis_index_groups=halves, tiled=True)  10.5 us
    all_to_all x1, starting transfers between devices, body(): lax.all_to_all(slices, 'sub', 0, 0, axis_index_groups=halves, tiled=True)  10.4 us
    pallas_call x1, Pallas kernels, body(): pl.pallas_call(split_kernel, out_shape=shape((members, 2, beams, width),...  9.18 us
    all_to_all x1, starting transfers between devices, body(): tiles = lax.all_to_all(tiles, 'sub', 0, 0, tiled=True).astype(f32)  8.7 us
    ppermute x1, waiting for transfers between devices, body(): above = lax.ppermute(tile, 'hgt', [(i, i - 1) for i in range(1, layers)])  5.15 us
    all_to_all x1, waiting for transfers between devices, body(): lax.all_to_all(slices, 'sub', 0, 0, axis_index_groups=halves, tiled=True)  4.02 us
    all_to_all x1, starting transfers between devices, body(): lax.all_to_all(windows, 'sub', 0, 0, axis_index_groups=halves, tiled=True)  3.53 us
  transfers between devices with their start and end apart: 4, of which 4 were waited for; matrix products, arithmetic and copies ran while one was open for 5% of the time, Pallas kernels for 5%

profile of v4, /device:TPU:6, one launch (start us, length us, event | category | flops | bytes accessed | tf_op | source)
XLA Modules:
  0.0 80.1 jit_solution(7775658113125058517)
XLA Ops:
  0.0 9.2 %split.1 = bf16[16,2,16,256]{3,2,1,0:T(8,128)(2,1)} custom-call(bf16[1,2,16,4096]{3,2,1,0:T(8,128)(2,1)} %source_ref.1), custom_call_target="tpu_custom_call" | custom-call | tf_op jit(solution)/shard_map/split/pallas_call | solution.py:383
  9.2 10.4 %all-to-all-start = ((bf16[16,2,16,256]{3,2,1,0:T(8,128)(2,1)}), bf16[16,2,16,256]{3,2,1,0:T(8,128)(2,1)S(1)}, u32[]{:S(2)}, u32[]{:S(2)}) async-start(bf16[16,2,16,256]{3,2,1,0:T(8,128)(2,1)} %split.1), calls=%async_computation | async-start | bytes 524288 | tf_op jit(solution)/shard_map/all_to_all | solution.py:392
  20.3 0.7 convert_bitcast_fusion
  21.0 0.1 copy.15
  21.1 0.7 convert_element_type.25
  21.8 0.1 copy.14
  21.9 0.7 reshape.35
  22.6 0.1 copy.13
  22.7 0.6 pad_add_fusion.place_ref
  23.3 0.7 maximum_bitcast_fusion.params_ref
  23.9 2.8 %prepare.1 = (f32[10,2,16,256]{3,2,1,0:T(8,128)S(1)}, bf16[64,32]{1,0:T(8,128)(2,1)S(1)}, bf16[32,32]{1,0:T(8,128)(2,1)S(1)}, bf16[64,64]{1,0:T(8,128)(2,1)S(1)}...) custom-call(s32[3]{0:T(128)} %pad_add_fusion.place_ref, f32[1]{0:T(128)S(6)} %copy.22.wave_ref, ...), custom_call_target="tpu_custom_call" | custom-call | tf_op jit(solution)/shard_map/prepare/pallas_call | solution.py:393
  26.8 4.0 %all-to-all-done.data_ref = bf16[16,2,16,256]{3,2,1,0:T(8,128)(2,1)S(1)} async-done(((bf16[16,2,16,256]{3,2,1,0:T(8,128)(2,1)}), bf16[16,2,16,256]{3,2,1,0:T(8,128)(2,1)S(1)}, u32[]{:S(2)}, u32[]{:S(2)}) %all-to-all-start) | async-done | bytes 262176 | tf_op jit(solution)/shard_map/all_to_all | solution.py:392
  30.8 1.4 %merge.1.after_ref = bf16[16,2,16,256]{3,2,1,0:T(8,128)(2,1)} custom-call(bf16[16,2,16,256]{3,2,1,0:T(8,128)(2,1)S(1)} %all-to-all-done.data_ref, f32[10,2,16,256]{3,2,1,0:T(8,128)S(1)} %get-tuple-element.12.trig_ref, bf16[64,32]{1,0:T(8,128)(2,1)S(1)} %get-tuple-element.13.first_ref, bf16[32,32]{1,0:T(8,128)(2,1)S(1)} %get-tuple-element.14.second_ref, ...), custom_call_target="tpu_custom_call" | custom-call | tf_op jit(solution)/shard_map/merge/pallas_call | solution.py:427
  32.2 3.5 %all-to-all-start.1 = ((bf16[16,2,16,256]{3,2,1,0:T(8,128)(2,1)}), bf16[16,2,16,256]{3,2,1,0:T(8,128)(2,1)S(1)}, u32[]{:S(2)}, u32[]{:S(2)}) async-start(bf16[16,2,16,256]{3,2,1,0:T(8,128)(2,1)} %merge.1.after_ref), calls=%async_computation.1 | async-start | bytes 524288 | tf_op jit(solution)/shard_map/all_to_all | solution.py:437
  35.7 0.0 slice-start
  35.7 0.8 %weights.1.column_ref = bf16[8,256,512]{2,1,0:T(8,128)(2,1)S(1)} custom-call(bf16[16,2,16,256]{3,2,1,0:T(8,128)(2,1)} %merge.1.after_ref, s32[3,64,128]{2,1,0:T(8,128)S(1)} %get-tuple-element.16.whole_ref, f32[2,64,128]{2,1,0:T(8,128)S(1)} %get-tuple-element.17.real_ref), custom_call_target="tpu_custom_call" | custom-call | tf_op jit(solution)/shard_map/weights/pallas_call | solution.py:438
  36.6 10.5 %all-to-all-done.1.table_ref = bf16[16,2,16,256]{3,2,1,0:T(8,128)(2,1)S(1)} async-done(((bf16[16,2,16,256]{3,2,1,0:T(8,128)(2,1)}), bf16[16,2,16,256]{3,2,1,0:T(8,128)(2,1)S(1)}, u32[]{:S(2)}, u32[]{:S(2)}) %all-to-all-start.1) | async-done | bytes 262176 | tf_op jit(solution)/shard_map/all_to_all | solution.py:437
  47.0 3.5 %sample.1 = bf16[128,128]{1,0:T(8,128)(2,1)} custom-call(bf16[16,2,16,256]{3,2,1,0:T(8,128)(2,1)S(1)} %all-to-all-done.1.table_ref, bf16[8,256,512]{2,1,0:T(8,128)(2,1)S(1)} %weights.1.column_ref, s32[3,64,128]{2,1,0:T(8,128)S(1)} %get-tuple-element.16.whole_ref, f32[2,64,128]{2,1,0:T(8,128)S(1)} %get-tuple-element.17.real_ref, ...), custom_call_target="tpu_custom_call" | custom-call | tf_op jit(solution)/shard_map/sample/pallas_call | solution.py:447
  50.5 8.7 %all-to-all-start.2 = ((bf16[32,4,128]{2,1,0:T(4,128)(2,1)}), bf16[32,4,128]{2,1,0:T(4,128)(2,1)S(1)}, u32[]{:S(2)}, u32[]{:S(2)}) async-start(bf16[32,4,128]{2,1,0:T(4,128)(2,1)} %bitcast.7), calls=%async_computation.2 | async-start | bytes 65536 | tf_op jit(solution)/shard_map/all_to_all | solution.py:464
  59.2 0.0 slice-done
  59.3 12.2 %all-to-all-done.2 = bf16[32,4,128]{2,1,0:T(4,128)(2,1)S(1)} async-done(((bf16[32,4,128]{2,1,0:T(4,128)(2,1)}), bf16[32,4,128]{2,1,0:T(4,128)(2,1)S(1)}, u32[]{:S(2)}, u32[]{:S(2)}) %all-to-all-start.2) | async-done | bytes 32800 | tf_op jit(solution)/shard_map/all_to_all | solution.py:464
  71.5 2.7 %collective-permute-start = (f32[16,2,2,128]{3,0,2,1:T(8,128)S(1)}, f32[16,2,2,128]{3,0,2,1:T(8,128)S(1)}, u32[]{:S(2)}, u32[]{:S(2)}) collective-permute-start(f32[16,2,2,128]{3,0,2,1:T(8,128)S(1)} %bitcast.33), channel_id=1, source_target_pairs={{1,0},{2,1},{3,2},{4,3},{5,4},{6,5},{7,6},{8,7},{9,8},{10,9},{11,1... | collective-permute-start | bytes 98312 | tf_op jit(solution)/shard_map/ppermute | solution.py:467
  74.3 5.1 %collective-permute-done = f32[16,2,2,128]{3,0,2,1:T(8,128)S(1)} collective-permute-done((f32[16,2,2,128]{3,0,2,1:T(8,128)S(1)}, f32[16,2,2,128]{3,0,2,1:T(8,128)S(1)}, u32[]{:S(2)}, u32[]{:S(2)}) %collective-permute-start) | collective-permute-done | bytes 32800 | tf_op jit(solution)/shard_map/ppermute | solution.py:467
  79.4 0.6 reshape.39
  (8 shorter events, 0.1 us)
Async XLA Ops:
  9.2 21.6 %all-to-all-start = ((bf16[16,2,16,256]{3,2,1,0:T(8,128)(2,1)}), bf16[16,2,16,256]{3,2,1,0:T(8,128)(2,1)S(1)}, u32[]{:S(2)}, u32[]{:S(2)}) async-start(bf16[16,2,16,256]{3,2,1,0:T(8,128)(2,1)} %split.1), calls=%async_computation | async-start | bytes 524288 | tf_op jit(solution)/shard_map/all_to_all | solution.py:392
  32.2 14.9 %all-to-all-start.1 = ((bf16[16,2,16,256]{3,2,1,0:T(8,128)(2,1)}), bf16[16,2,16,256]{3,2,1,0:T(8,128)(2,1)S(1)}, u32[]{:S(2)}, u32[]{:S(2)}) async-start(bf16[16,2,16,256]{3,2,1,0:T(8,128)(2,1)} %merge.1.after_ref), calls=%async_computation.1 | async-start | bytes 524288 | tf_op jit(solution)/shard_map/all_to_all | solution.py:437
  35.7 23.5 %slice-start = ((bf16[3,64,2048]{2,1,0:T(8,128)(2,1)}), bf16[1,64,2048]{2,1,0:T(8,128)(2,1)S(1)}, s32[]{:S(2)}) async-start(bf16[3,64,2048]{2,1,0:T(8,128)(2,1)} %frac_ref.1), calls=%async_computation.3 | async-start | bytes 524288 | tf_op jit(solution)/shard_map/slice | solution.py:468
  50.5 20.9 %all-to-all-start.2 = ((bf16[32,4,128]{2,1,0:T(4,128)(2,1)}), bf16[32,4,128]{2,1,0:T(4,128)(2,1)S(1)}, u32[]{:S(2)}, u32[]{:S(2)}) async-start(bf16[32,4,128]{2,1,0:T(4,128)(2,1)} %bitcast.7), calls=%async_computation.2 | async-start | bytes 65536 | tf_op jit(solution)/shard_map/all_to_all | solution.py:464
  71.5 7.9 %collective-permute-start = (f32[16,2,2,128]{3,0,2,1:T(8,128)S(1)}, f32[16,2,2,128]{3,0,2,1:T(8,128)S(1)}, u32[]{:S(2)}, u32[]{:S(2)}) collective-permute-start(f32[16,2,2,128]{3,0,2,1:T(8,128)S(1)} %bitcast.33), channel_id=1, source_target_pairs={{1,0},{2,1},{3,2},{4,3},{5,4},{6,5},{7,6},{8,7},{9,8},{10,9},{11,1... | collective-permute-start | bytes 98312 | tf_op jit(solution)/shard_map/ppermute | solution.py:467

commit v5 on v4

--- a/solution.py
+++ b/solution.py
@@ -13,20 +13,6 @@
 HALO = 4
 QUARTER = 8
 ROWS = 64
-
-
-def split_kernel(source_ref, out_ref, semaphores):
-    width = out_ref.shape[3]
-    copies = [
-        pltpu.make_async_copy(
-            source_ref.at[0, :, :, pl.ds(i * width, width)], out_ref.at[i], semaphores.at[i]
-        )
-        for i in range(out_ref.shape[0])
-    ]
-    for copy in copies:
-        copy.start()
-    for copy in copies:
-        copy.wait()
 
 
 def swap_quarters(values):
@@ -236,9 +222,9 @@
 def range_columns(whole_ref, real_ref, step, width):
     place = pl.ds(step * 4, 4)
     row_ids = lax.broadcasted_iota(jnp.int32, (width, 4 * LANES), 0)
-    offset = row_ids - flat(whole_ref[0, place, :])
+    inner = flat(whole_ref[0, place, :])
     frac = flat(real_ref[1, place, :])
-    column = jnp.where(offset == 0, 1.0 - frac, jnp.where(offset == 1, frac, 0.0))
+    column = jnp.where(row_ids == inner, 1.0 - frac, jnp.where(row_ids == inner + 1, frac, 0.0))
     return column.astype(jnp.bfloat16)
 
 
@@ -289,16 +275,18 @@
         outer, beam = flat(whole_ref[1, place, :]), flat(whole_ref[2, place, :])
         frac = flat(real_ref[0, place, :])
         product = jnp.dot(lhs_ref[quarter], columns, preferred_element_type=jnp.float32)
-        picked = product[0:rows]
+        outer = jnp.broadcast_to(outer, (QUARTER, outer.shape[1]))
+        picked = [product[part * QUARTER : (part + 1) * QUARTER] for part in range(parts)]
         for k in range(1, blocks):
-            picked = jnp.where(outer == k, product[k * rows : (k + 1) * rows], picked)
+            here = outer == k
+            for part in range(parts):
+                row = k * rows + part * QUARTER
+                picked[part] = jnp.where(here, product[row : row + QUARTER], picked[part])
         weights = jnp.where(
             beam_ids == beam, 1.0 - frac, jnp.where(beam_ids == beam + 1, frac, 0.0)
         )
         for part in range(parts):
-            summed = jnp.sum(
-                weights * picked[part * QUARTER : (part + 1) * QUARTER], axis=0, keepdims=True
-            )
+            summed = jnp.sum(weights * picked[part], axis=0, keepdims=True)
             for i in range(4):
                 cart_ref[part, pl.ds(step * 4 + i, 1), :] = summed[:, i * LANES : (i + 1) * LANES]
 
@@ -370,7 +358,6 @@
     ).T
     smem = pl.BlockSpec(memory_space=pltpu.SMEM)
     vmem = pl.BlockSpec(memory_space=pltpu.VMEM)
-    far = pl.BlockSpec(memory_space=pl.ANY if interpret else pltpu.HBM)
     shape = jax.ShapeDtypeStruct
     limit = pltpu.CompilerParams(vmem_limit_bytes=24 * 2**20)
     f32, bf16 = jnp.float32, jnp.bfloat16
@@ -380,16 +367,11 @@
     def local(value):
         return value if interpret else pltpu.with_memory_space_constraint(value, pltpu.VMEM)
 
-    slices = pl.pallas_call(
-        split_kernel,
-        out_shape=shape((members, 2, beams, width), bf16),
-        in_specs=[far],
-        out_specs=far,
-        scratch_shapes=[pltpu.SemaphoreType.DMA((members,))],
-        interpret=interpret,
-        name="split",
-    )(polar_beams)
-    slices = local(lax.all_to_all(slices, "sub", 0, 0, axis_index_groups=halves, tiled=True))
+    slices = polar_beams.reshape(2, beams // 8, 8, members, width // LANES, LANES)
+    slices = slices.transpose(3, 0, 1, 4, 2, 5)
+    slices = lax.all_to_all(slices, "sub", 0, 0, axis_index_groups=halves, tiled=True)
+    slices = slices.transpose(0, 1, 2, 4, 3, 5).reshape(members, 2, beams, width)
+    slices = local(slices)
     trig, first, second, third, whole, real, pixel = pl.pallas_call(
         functools.partial(prepare_kernel, range_count=range_count),
         out_shape=[

time: 80.6 us -> 72.8 us (0.903)
  Pallas kernels: 17.7 us -> 8.04 us
  local copies, waits for them, and re-layouts: 1.6 us -> 3.27 us
    pallas_call x1 -> x0, Pallas kernels: 9.18 us -> none  [body(): pl.pallas_call(split_kernel, out_shape=shape((members, 2, beams, width),...]
    reshape x0 -> x1, local copies, waits for them, and re-layouts: none -> 1.67 us  [body(): polar_beams.reshape(2, beams // 8, 8, members, width // LANES, LANES)]
where the time goes in v5:
time: 72.8 us; the launch traced here: 72.2 us
  waiting for transfers between devices  31.9 us (44%)
  starting transfers between devices  25.4 us (35%)
  Pallas kernels  8.04 us (11%)
  local copies, waits for them, and re-layouts  3.27 us (4%)
  other arithmetic  2.77 us (4%)
  between operations  0.76 us (1%)
    all_to_all x1, waiting for transfers between devices, body(): tiles = lax.all_to_all(tiles, 'sub', 0, 0, tiled=True).astype(f32)  12.2 us
    all_to_all x1, waiting for transfers between devices, body(): lax.all_to_all(windows, 'sub', 0, 0, axis_index_groups=halves, tiled=True)  10.6 us
    all_to_all x1, starting transfers between devices, body(): lax.all_to_all(slices, 'sub', 0, 0, axis_index_groups=halves, tiled=True)  10.4 us
    all_to_all x1, starting transfers between devices, body(): tiles = lax.all_to_all(tiles, 'sub', 0, 0, tiled=True).astype(f32)  8.71 us
    ppermute x1, waiting for transfers between devices, body(): above = lax.ppermute(tile, 'hgt', [(i, i - 1) for i in range(1, layers)])  5.15 us
    all_to_all x1, waiting for transfers between devices, body(): lax.all_to_all(slices, 'sub', 0, 0, axis_index_groups=halves, tiled=True)  4.02 us
    all_to_all x1, starting transfers between devices, body(): lax.all_to_all(windows, 'sub', 0, 0, axis_index_groups=halves, tiled=True)  3.53 us
    pallas_call x1, Pallas kernels, body(): pl.pallas_call(sample_kernel, out_shape=shape((2 * row_count, LANES), bf1...  3.14 us
  transfers between devices with their start and end apart: 4, of which 4 were waited for; matrix products, arithmetic and copies ran while one was open for 5% of the time, Pallas kernels for 5%

profile of v5, /device:TPU:6, one launch (start us, length us, event | category | flops | bytes accessed | tf_op | source)
XLA Modules:
  0.0 72.2 jit_solution(2679441455140791261)
XLA Ops:
  0.0 1.7 %copy.24 = bf16[2,2,8,16,2,128]{5,2,4,1,0,3:T(8,128)(2,1)} copy(bf16[2,2,8,16,2,128]{5,2,4,3,1,0:T(8,128)(2,1)} %bitcast.40) | data formatting | bytes 524288 | tf_op jit(solution)/shard_map/reshape | solution.py:370
  1.7 10.4 %all-to-all-start = ((bf16[16,2,2,2,8,128]{5,4,3,2,1,0:T(8,128)(2,1)}), bf16[16,2,2,2,8,128]{5,4,3,2,1,0:T(8,128)(2,1)S(1)}, u32[]{:S(2)}, u32[]{:S(2)}) async-start(bf16[16,2,2,2,8,128]{5,4,3,2,1,0:T(8,128)(2,1)} %bitcast.36), calls=%async_computation | async-start | bytes 524288 | tf_op jit(solution)/shard_map/all_to_all | solution.py:372
  12.8 0.7 %convert_bitcast_fusion = f32[96,16]{1,0:T(8,128)S(1)} fusion(bf16[3,2,2,16,8]{3,4,2,1,0:T(8,128)(2,1)} %param.10), kind=kLoop, calls=%fused_computation.1 | loop fusion | flops 1536 | bytes 9216 | tf_op jit(solution)/shard_map/convert_element_type | solution.py:355
  13.5 0.1 copy.17
  13.6 0.7 convert_element_type.25
  14.3 0.1 copy.16
  14.4 0.7 reshape.43
  15.1 0.1 copy.15
  15.2 0.6 pad_add_fusion.place_ref
  15.7 0.7 maximum_bitcast_fusion.params_ref
  16.4 2.8 %prepare.1 = (f32[10,2,16,256]{3,2,1,0:T(8,128)S(1)}, bf16[64,32]{1,0:T(8,128)(2,1)S(1)}, bf16[32,32]{1,0:T(8,128)(2,1)S(1)}, bf16[64,64]{1,0:T(8,128)(2,1)S(1)}...) custom-call(s32[3]{0:T(128)} %pad_add_fusion.place_ref, f32[1]{0:T(128)S(6)} %copy.26.wave_ref, ...), custom_call_target="tpu_custom_call" | custom-call | tf_op jit(solution)/shard_map/prepare/pallas_call | solution.py:375
  19.2 4.0 %all-to-all-done = bf16[16,2,2,2,8,128]{5,4,3,2,1,0:T(8,128)(2,1)S(1)} async-done(((bf16[16,2,2,2,8,128]{5,4,3,2,1,0:T(8,128)(2,1)}), bf16[16,2,2,2,8,128]{5,4,3,2,1,0:T(8,128)(2,1)S(1)}, u32[]{:S(2)}, u32[]{:S(2)}) %all-to-all-start) | async-done | bytes 262176 | tf_op jit(solution)/shard_map/all_to_all | solution.py:372
  23.2 1.4 %merge.1.after_ref = bf16[16,2,16,256]{3,2,1,0:T(8,128)(2,1)} custom-call(bf16[16,2,16,256]{3,2,1,0:T(8,128)(2,1)S(1)} %bitcast.39, f32[10,2,16,256]{3,2,1,0:T(8,128)S(1)} %get-tuple-element.12.trig_ref, bf16[64,32]{1,0:T(8,128)(2,1)S(1)} %get-tuple-element.13.first_ref, bf16[32,32]{1,0:T(8,128)(2,1)S(1)} %get-tuple-element.14.second_ref, ...), custom_call_target="tpu_custom_call" | custom-call | tf_op jit(solution)/shard_map/merge/pallas_call | solution.py:409
  24.6 3.5 %all-to-all-start.1 = ((bf16[16,2,16,256]{3,2,1,0:T(8,128)(2,1)}), bf16[16,2,16,256]{3,2,1,0:T(8,128)(2,1)S(1)}, u32[]{:S(2)}, u32[]{:S(2)}) async-start(bf16[16,2,16,256]{3,2,1,0:T(8,128)(2,1)} %merge.1.after_ref), calls=%async_computation.1 | async-start | bytes 524288 | tf_op jit(solution)/shard_map/all_to_all | solution.py:419
  28.2 0.0 slice-start
  28.2 0.7 weights.1.column_ref
  28.9 10.6 %all-to-all-done.1.table_ref = bf16[16,2,16,256]{3,2,1,0:T(8,128)(2,1)S(1)} async-done(((bf16[16,2,16,256]{3,2,1,0:T(8,128)(2,1)}), bf16[16,2,16,256]{3,2,1,0:T(8,128)(2,1)S(1)}, u32[]{:S(2)}, u32[]{:S(2)}) %all-to-all-start.1) | async-done | bytes 262176 | tf_op jit(solution)/shard_map/all_to_all | solution.py:419
  39.5 3.1 %sample.1 = bf16[128,128]{1,0:T(8,128)(2,1)} custom-call(bf16[16,2,16,256]{3,2,1,0:T(8,128)(2,1)S(1)} %all-to-all-done.1.table_ref, bf16[8,256,512]{2,1,0:T(8,128)(2,1)S(1)} %weights.1.column_ref, s32[3,64,128]{2,1,0:T(8,128)S(1)} %get-tuple-element.16.whole_ref, f32[2,64,128]{2,1,0:T(8,128)S(1)} %get-tuple-element.17.real_ref, ...), custom_call_target="tpu_custom_call" | custom-call | tf_op jit(solution)/shard_map/sample/pallas_call | solution.py:429
  42.6 8.7 %all-to-all-start.2 = ((bf16[32,4,128]{2,1,0:T(4,128)(2,1)}), bf16[32,4,128]{2,1,0:T(4,128)(2,1)S(1)}, u32[]{:S(2)}, u32[]{:S(2)}) async-start(bf16[32,4,128]{2,1,0:T(4,128)(2,1)} %bitcast.11), calls=%async_computation.2 | async-start | bytes 65536 | tf_op jit(solution)/shard_map/all_to_all | solution.py:446
  51.4 0.0 slice-done
  51.4 12.2 %all-to-all-done.2 = bf16[32,4,128]{2,1,0:T(4,128)(2,1)S(1)} async-done(((bf16[32,4,128]{2,1,0:T(4,128)(2,1)}), bf16[32,4,128]{2,1,0:T(4,128)(2,1)S(1)}, u32[]{:S(2)}, u32[]{:S(2)}) %all-to-all-start.2) | async-done | bytes 32800 | tf_op jit(solution)/shard_map/all_to_all | solution.py:446
  63.6 2.7 %collective-permute-start = (f32[16,2,2,128]{3,0,2,1:T(8,128)S(1)}, f32[16,2,2,128]{3,0,2,1:T(8,128)S(1)}, u32[]{:S(2)}, u32[]{:S(2)}) collective-permute-start(f32[16,2,2,128]{3,0,2,1:T(8,128)S(1)} %bitcast.42), channel_id=1, source_target_pairs={{1,0},{2,1},{3,2},{4,3},{5,4},{6,5},{7,6},{8,7},{9,8},{10,9},{11,1... | collective-permute-start | bytes 98312 | tf_op jit(solution)/shard_map/ppermute | solution.py:449
  66.4 5.1 %collective-permute-done = f32[16,2,2,128]{3,0,2,1:T(8,128)S(1)} collective-permute-done((f32[16,2,2,128]{3,0,2,1:T(8,128)S(1)}, f32[16,2,2,128]{3,0,2,1:T(8,128)S(1)}, u32[]{:S(2)}, u32[]{:S(2)}) %collective-permute-start) | collective-permute-done | bytes 32800 | tf_op jit(solution)/shard_map/ppermute | solution.py:449
  71.6 0.6 reshape.47
  (8 shorter events, 0.1 us)
Async XLA Ops:
  1.7 21.6 %all-to-all-start = ((bf16[16,2,2,2,8,128]{5,4,3,2,1,0:T(8,128)(2,1)}), bf16[16,2,2,2,8,128]{5,4,3,2,1,0:T(8,128)(2,1)S(1)}, u32[]{:S(2)}, u32[]{:S(2)}) async-start(bf16[16,2,2,2,8,128]{5,4,3,2,1,0:T(8,128)(2,1)} %bitcast.36), calls=%async_computation | async-start | bytes 524288 | tf_op jit(solution)/shard_map/all_to_all | solution.py:372
  24.6 14.9 %all-to-all-start.1 = ((bf16[16,2,16,256]{3,2,1,0:T(8,128)(2,1)}), bf16[16,2,16,256]{3,2,1,0:T(8,128)(2,1)S(1)}, u32[]{:S(2)}, u32[]{:S(2)}) async-start(bf16[16,2,16,256]{3,2,1,0:T(8,128)(2,1)} %merge.1.after_ref), calls=%async_computation.1 | async-start | bytes 524288 | tf_op jit(solution)/shard_map/all_to_all | solution.py:419
  28.2 23.2 %slice-start = ((bf16[3,64,2048]{2,1,0:T(8,128)(2,1)}), bf16[1,64,2048]{2,1,0:T(8,128)(2,1)S(1)}, s32[]{:S(2)}) async-start(bf16[3,64,2048]{2,1,0:T(8,128)(2,1)} %frac_ref.1), calls=%async_computation.3 | async-start | bytes 524288 | tf_op jit(solution)/shard_map/slice | solution.py:450
  42.6 20.9 %all-to-all-start.2 = ((bf16[32,4,128]{2,1,0:T(4,128)(2,1)}), bf16[32,4,128]{2,1,0:T(4,128)(2,1)S(1)}, u32[]{:S(2)}, u32[]{:S(2)}) async-start(bf16[32,4,128]{2,1,0:T(4,128)(2,1)} %bitcast.11), calls=%async_computation.2 | async-start | bytes 65536 | tf_op jit(solution)/shard_map/all_to_all | solution.py:446
  63.6 7.9 %collective-permute-start = (f32[16,2,2,128]{3,0,2,1:T(8,128)S(1)}, f32[16,2,2,128]{3,0,2,1:T(8,128)S(1)}, u32[]{:S(2)}, u32[]{:S(2)}) collective-permute-start(f32[16,2,2,128]{3,0,2,1:T(8,128)S(1)} %bitcast.42), channel_id=1, source_target_pairs={{1,0},{2,1},{3,2},{4,3},{5,4},{6,5},{7,6},{8,7},{9,8},{10,9},{11,1... | collective-permute-start | bytes 98312 | tf_op jit(solution)/shard_map/ppermute | solution.py:449

commit v6 on v5

--- a/solution.py
+++ b/solution.py
@@ -30,13 +30,20 @@
     return values
 
 
+def block_of(sub_index):
+    return (sub_index >> 2) * 2 + (sub_index & 1)
+
+
 def prepare_kernel(
     place_ref,
     wave_ref,
-    params_ref,
+    start_ref,
+    weight_ref,
+    rate_ref,
     beam_ref,
     range_ref,
     frac_ref,
+    tall_ref,
     trig_ref,
     first_ref,
     second_ref,
@@ -44,19 +51,34 @@
     whole_ref,
     real_ref,
     pixel_ref,
+    height_ref,
+    params_ref,
+    tall_scratch,
     *,
     range_count,
 ):
     wave = wave_ref[0]
-    params = params_ref[...]
-    beams = params.shape[0]
-    matrices = 12
-    taps = (params.shape[1] - 2 * matrices) // matrices
+    levels, children, halves, taps, beams = weight_ref.shape
+    matrices = levels * children * halves
+    params_ref[...] = jnp.zeros_like(params_ref)
+    for level in range(levels):
+        for child in range(children):
+            i = (level * children + child) * halves
+            params_ref[i : i + halves, 0:beams] = rate_ref[level, child]
+            row = matrices + i
+            params_ref[row : row + halves, 0:beams] = start_ref[level, child].astype(jnp.float32)
+            for half in range(halves):
+                row = 2 * matrices + (i + half) * taps
+                params_ref[row : row + taps, 0:beams] = weight_ref[level, child, half].astype(
+                    jnp.float32
+                )
+    params = params_ref[...].T[0:beams]
     width = trig_ref.shape[3]
     lane = lax.broadcasted_iota(jnp.int32, (1, width), 1)
-    position = ((place_ref[0] * width + lane).astype(jnp.float32) + 0.5) / range_count
-    row_half = place_ref[1]
-    upper = row_half == 1
+    sub_index = place_ref[0]
+    column_block = block_of(sub_index)
+    position = ((column_block * width + lane).astype(jnp.float32) + 0.5) / range_count
+    upper = sub_index >> 1 & 1 == 1
 
     def column(offset, level, child, half):
         i = offset + (level * 2 + child) * 2 + half
@@ -115,12 +137,19 @@
         rows.append(jnp.concatenate([block, block], axis=1))
     second_ref[...] = jnp.concatenate(rows, axis=0).astype(jnp.bfloat16)
 
+    for block in range(height_ref.shape[0] // 4):
+        tall_scratch[block] = tall_ref[0, :, block * LANES : (block + 1) * LANES].astype(
+            jnp.float32
+        )
+        tall = tall_scratch[block, pl.ds((sub_index & 7) * 2, 2), :]
+        for row in range(4):
+            height_ref[pl.ds(block * 4 + row, 1), :] = tall[row // 2 : row // 2 + 1]
     samples = range_ref[...]
     fracs = [frac_ref[i].astype(jnp.float32) for i in range(2)]
     angles = (wave * range_phase) * (samples.astype(jnp.float32) + fracs[1])
     pixel_ref[0] = jnp.cos(angles)
     pixel_ref[1] = jnp.sin(angles)
-    first_beam = place_ref[2] * 8 - HALO
+    first_beam = column_block * 8 - HALO
     for group in range(ROWS // 32):
         rows = [slice(group * 32 + 8 * j, group * 32 + 8 * j + 8) for j in range(4)]
         sample_parts = swap_quarters([samples[r] for r in rows])
@@ -143,8 +172,9 @@
 
 
 def merge_kernel(
-    data_ref, trig_ref, first_ref, second_ref, third_ref, out_ref, padded_ref, *, groups
+    data_ref, trig_ref, first_ref, second_ref, third_ref, before_ref, out_ref, padded_ref, *, groups
 ):
+    del before_ref
     beams, width = data_ref.shape[2], data_ref.shape[3]
 
     def turn(i, product, row, col):
@@ -228,9 +258,7 @@
     return column.astype(jnp.bfloat16)
 
 
-def weights_kernel(after_ref, whole_ref, real_ref, out_ref):
-    del after_ref
-
+def weights_kernel(whole_ref, real_ref, out_ref):
     def chunk(step, carry):
         out_ref[step] = range_columns(whole_ref, real_ref, 2 * step, out_ref.shape[1])
         return carry
@@ -338,24 +366,10 @@
     levels = band_start.shape[0]
     taps = band_weight.shape[-1]
     row_count, column_count = beam_map.shape
-    matrices = levels * 4
     members = sub_count // 2
     width = range_count // members
-    column_block = (sub_index >> 2) * 2 + (sub_index & 1)
-    row_half = sub_index >> 1 & 1
     halves = [[s for s in range(sub_count) if s >> 1 & 1 == half] for half in range(2)]
-    place = jnp.stack([column_block, row_half, column_block]).astype(jnp.int32)
-    params = jnp.concatenate(
-        [
-            phase_rate.reshape(matrices, beams),
-            band_start.reshape(matrices, beams).astype(jnp.float32),
-            band_weight.reshape(matrices, beams, taps)
-            .transpose(0, 2, 1)
-            .reshape(matrices * taps, beams)
-            .astype(jnp.float32),
-        ],
-        axis=0,
-    ).T
+    place = sub_index.astype(jnp.int32).reshape(1)
     smem = pl.BlockSpec(memory_space=pltpu.SMEM)
     vmem = pl.BlockSpec(memory_space=pltpu.VMEM)
     shape = jax.ShapeDtypeStruct
@@ -372,7 +386,7 @@
     slices = lax.all_to_all(slices, "sub", 0, 0, axis_index_groups=halves, tiled=True)
     slices = slices.transpose(0, 1, 2, 4, 3, 5).reshape(members, 2, beams, width)
     slices = local(slices)
-    trig, first, second, third, whole, real, pixel = pl.pallas_call(
+    trig, first, second, third, whole, real, pixel, height = pl.pallas_call(
         functools.partial(prepare_kernel, range_count=range_count),
         out_shape=[
             kept((10, 2, beams, width), f32),
@@ -382,16 +396,20 @@
             kept((3, row_count, LANES), jnp.int32),
             kept((2, row_count, LANES), f32),
             kept((2, row_count, LANES), f32),
+            shape((4 * members, LANES), f32),
         ],
         grid_spec=pltpu.PrefetchScalarGridSpec(
             num_scalar_prefetch=1,
             grid=(1,),
             in_specs=[
                 smem,
-                pl.BlockSpec((beams, params.shape[1]), lambda i, p: (0, 0)),
-                pl.BlockSpec((row_count, LANES), lambda i, p: (0, p[0])),
-                pl.BlockSpec((row_count, LANES), lambda i, p: (0, p[0])),
-                pl.BlockSpec((2, row_count, LANES), lambda i, p: (0, 0, p[0])),
+                pl.BlockSpec(band_start.shape, lambda i, p: (0, 0, 0, 0)),
+                pl.BlockSpec((levels, 2, 2, taps, beams), lambda i, p: (0, 0, 0, 0, 0)),
+                pl.BlockSpec(phase_rate.shape, lambda i, p: (0, 0, 0, 0)),
+                pl.BlockSpec((row_count, LANES), lambda i, p: (0, block_of(p[0]))),
+                pl.BlockSpec((row_count, LANES), lambda i, p: (0, block_of(p[0]))),
+                pl.BlockSpec((2, row_count, LANES), lambda i, p: (0, 0, block_of(p[0]))),
+                pl.BlockSpec((1, 16, column_count), lambda i, p: (2, p[0] >> 3, 0)),
             ],
             out_specs=[
                 pl.BlockSpec((10, 2, beams, width), lambda i, p: (0, 0, 0, 0)),
@@ -401,34 +419,49 @@
                 pl.BlockSpec((3, row_count, LANES), lambda i, p: (0, 0, 0)),
                 pl.BlockSpec((2, row_count, LANES), lambda i, p: (0, 0, 0)),
                 pl.BlockSpec((2, row_count, LANES), lambda i, p: (0, 0, 0)),
+                pl.BlockSpec((4 * members, LANES), lambda i, p: (0, 0)),
+            ],
+            scratch_shapes=[
+                pltpu.VMEM((LANES, LANES), f32),
+                pltpu.VMEM((members, 16, LANES), f32),
             ],
         ),
         interpret=interpret,
         name="prepare",
-    )(place, layer_wave, params, beam_map, range_map, pixel_frac)
+    )(
+        place,
+        layer_wave,
+        band_start,
+        band_weight.transpose(0, 1, 2, 4, 3),
+        phase_rate,
+        beam_map,
+        range_map,
+        pixel_frac,
+        pixel_frac,
+    )
+    columns = pl.pallas_call(
+        weights_kernel,
+        out_shape=kept((row_count // 8, width, 4 * LANES), bf16),
+        in_specs=[vmem, vmem],
+        out_specs=vmem,
+        compiler_params=limit,
+        interpret=interpret,
+        name="weights",
+    )(local(whole), local(real))
     windows = pl.pallas_call(
         functools.partial(merge_kernel, groups=sub_count // 2**levels),
         out_shape=kept((members, 2, WINDOW, width), bf16),
-        in_specs=[vmem] * 5,
+        in_specs=[vmem] * 5 + [pl.BlockSpec(memory_space=pl.ANY)],
         out_specs=vmem,
         scratch_shapes=[pltpu.VMEM((2, 144, width), f32)],
         compiler_params=limit,
         interpret=interpret,
         name="merge",
-    )(slices, local(trig), local(first), local(second), local(third))
+    )(slices, local(trig), local(first), local(second), local(third), local(columns))
     table = local(lax.all_to_all(windows, "sub", 0, 0, axis_index_groups=halves, tiled=True))
-    columns = pl.pallas_call(
-        weights_kernel,
-        out_shape=kept((row_count // 8, width, 4 * LANES), bf16),
-        in_specs=[pl.BlockSpec(memory_space=pl.ANY), vmem, vmem],
-        out_specs=vmem,
-        compiler_params=limit,
-        interpret=interpret,
-        name="weights",
-    )(windows, local(whole), local(real))
     cart = pl.pallas_call(
         sample_kernel,
-        out_shape=shape((2 * row_count, LANES), bf16),
+        out_shape=kept((2 * row_count, LANES), bf16),
         in_specs=[vmem] * 5,
         out_specs=vmem,
         scratch_shapes=[
@@ -447,9 +480,7 @@
     tiles = tiles.reshape(sub_count // 4, 2, 2, tile_rows * 2, LANES)
     tile = (tiles[:, 0] + tiles[:, 1]).reshape(members, tile_rows, 2, LANES)
     above = lax.ppermute(tile, "hgt", [(i, i - 1) for i in range(1, layers)])
-    height = lax.dynamic_slice_in_dim(pixel_frac[2], sub_index * tile_rows, tile_rows, 0)
-    height = height.astype(f32).reshape(tile_rows, members, LANES).transpose(1, 0, 2)
-    height = height[:, :, None, :]
+    height = height.reshape(members, tile_rows, 2, LANES)
     blended = (1.0 - height) * tile + height * above
     return blended.transpose(1, 2, 0, 3).reshape(tile_rows, 1, 2, column_count)
 

time: 72.8 us -> 70.9 us (0.974)
  blocking collectives: 0 us -> 35.3 us
  waiting for transfers between devices: 31.9 us -> 12.2 us
  starting transfers between devices: 25.4 us -> 13.2 us
  other arithmetic: 2.77 us -> 0.05 us
  Pallas kernels: 8.04 us -> 6.67 us
  local copies, waits for them, and re-layouts: 3.27 us -> 2.31 us
    all_to_all x0 -> x2, blocking collectives: none -> 35.3 us  [the longest x1 21 us: body(): tiles = lax.all_to_all(tiles, 'sub', 0, 0, tiled=True).astype(f32)]
    all_to_all x2 -> x0, waiting for transfers between devices: 22.8 us -> none  [the longest x1 12.2 us: body(): tiles = lax.all_to_all(tiles, 'sub', 0, 0, tiled=True).astype(f32)]
    all_to_all x2 -> x0, starting transfers between devices: 12.2 us -> none  [the longest x1 8.71 us: body(): tiles = lax.all_to_all(tiles, 'sub', 0, 0, tiled=True).astype(f32)]
    all_to_all x1, waiting for transfers between devices: 4.02 us -> 7.04 us  [body(): lax.all_to_all(slices, 'sub', 0, 0, axis_index_groups=halves, tiled=True)]
    convert_element_type x2 -> x0, other arithmetic: 1.46 us -> none  [the longest x1 0.74 us: body(): params = jnp.concatenate([phase_rate.reshape(matrices, beams), band_start...]
    reshape x2 -> x0, local copies, waits for them, and re-layouts: 0.78 us -> none  [body(): phase_rate.reshape(matrices, beams)]
  transfers between devices with their start and end apart: 4 -> 2, of which waited for: 4 -> 2; matrix products, arithmetic and copies ran while one was open for 5% -> 0% of each run, Pallas kernels for 5% -> 5%
where the time goes in v6:
time: 70.9 us; the launch traced here: 70.4 us
  blocking collectives  35.3 us (50%)
  starting transfers between devices  13.2 us (19%)
  waiting for transfers between devices  12.2 us (17%)
  Pallas kernels  6.67 us (9%)
  local copies, waits for them, and re-layouts  2.31 us (3%)
  between operations  0.71 us (1%)
    all_to_all x1, blocking collectives, body(): tiles = lax.all_to_all(tiles, 'sub', 0, 0, tiled=True).astype(f32)  21 us
    all_to_all x1, blocking collectives, body(): lax.all_to_all(windows, 'sub', 0, 0, axis_index_groups=halves, tiled=True)  14.4 us
    all_to_all x1, starting transfers between devices, body(): lax.all_to_all(slices, 'sub', 0, 0, axis_index_groups=halves, tiled=True)  10.4 us
    all_to_all x1, waiting for transfers between devices, body(): lax.all_to_all(slices, 'sub', 0, 0, axis_index_groups=halves, tiled=True)  7.04 us
    ppermute x1, waiting for transfers between devices, body(): above = lax.ppermute(tile, 'hgt', [(i, i - 1) for i in range(1, layers)])  5.17 us
    pallas_call x1, Pallas kernels, body(): pl.pallas_call(functools.partial(prepare_kernel, range_count=range_count)...  2.75 us
    ppermute x1, starting transfers between devices, body(): above = lax.ppermute(tile, 'hgt', [(i, i - 1) for i in range(1, layers)])  2.74 us
    pallas_call x1, Pallas kernels, body(): pl.pallas_call(sample_kernel, out_shape=kept((2 * row_count, LANES), bf16...  2.53 us
  transfers between devices with their start and end apart: 2, of which 2 were waited for; matrix products, arithmetic and copies ran while one was open for 0% of the time, Pallas kernels for 5%

profile of v6, /device:TPU:6, one launch (start us, length us, event | category | flops | bytes accessed | tf_op | source)
XLA Modules:
  0.0 70.4 jit_solution(13768820924321360785)
XLA Ops:
  0.0 1.7 %copy.12 = bf16[2,2,8,16,2,128]{5,2,4,1,0,3:T(8,128)(2,1)} copy(bf16[2,2,8,16,2,128]{5,2,4,3,1,0:T(8,128)(2,1)} %bitcast.20) | data formatting | bytes 524288 | tf_op jit(solution)/shard_map/reshape | solution.py:384
  1.7 10.4 %all-to-all-start = ((bf16[16,2,2,2,8,128]{5,4,3,2,1,0:T(8,128)(2,1)}), bf16[16,2,2,2,8,128]{5,4,3,2,1,0:T(8,128)(2,1)S(1)}, u32[]{:S(2)}, u32[]{:S(2)}) async-start(bf16[16,2,2,2,8,128]{5,4,3,2,1,0:T(8,128)(2,1)} %bitcast.17), calls=%async_computation | async-start | bytes 524288 | tf_op jit(solution)/shard_map/all_to_all | solution.py:386
  12.7 2.8 %prepare.1 = (f32[10,2,16,256]{3,2,1,0:T(8,128)S(1)}, bf16[64,32]{1,0:T(8,128)(2,1)S(1)}, bf16[32,32]{1,0:T(8,128)(2,1)S(1)}, bf16[64,64]{1,0:T(8,128)(2,1)S(1)}...) custom-call(s32[1]{0:T(128)} %bitcast.place_ref, ...), custom_call_target="tpu_custom_call" | custom-call | tf_op jit(solution)/shard_map/prepare/pallas_call | solution.py:389
  15.5 0.7 weights.1.before_ref.column_ref
  16.2 7.0 %all-to-all-done = bf16[16,2,2,2,8,128]{5,4,3,2,1,0:T(8,128)(2,1)S(1)} async-done(((bf16[16,2,2,2,8,128]{5,4,3,2,1,0:T(8,128)(2,1)}), bf16[16,2,2,2,8,128]{5,4,3,2,1,0:T(8,128)(2,1)S(1)}, u32[]{:S(2)}, u32[]{:S(2)}) %all-to-all-start) | async-done | bytes 262176 | tf_op jit(solution)/shard_map/all_to_all | solution.py:386
  23.2 0.7 merge.1
  23.9 0.0 copy-start
  23.9 14.4 %all_to_all.15.table_ref = bf16[16,2,16,256]{3,2,1,0:T(8,128)(2,1)S(1)} all-to-all(bf16[16,2,16,256]{3,2,1,0:T(8,128)(2,1)S(1)} %merge.1), channel_id=1, replica_groups={{0,16,64,80,128,144,192,208,256,272,320,336,384,400,448,464},{32,48,96,..., dimensions={0} | all-to-all | bytes 524288 | tf_op jit(solution)/shard_map/all_to_all | solution.py:461
  38.3 2.5 %sample.1 = bf16[128,128]{1,0:T(8,128)(2,1)S(1)} custom-call(bf16[16,2,16,256]{3,2,1,0:T(8,128)(2,1)S(1)} %all_to_all.15.table_ref, bf16[8,256,512]{2,1,0:T(8,128)(2,1)S(1)} %weights.1.before_ref.column_ref, s32[3,64,128]{2,1,0:T(8,128)S(1)} %get-tuple-element.18.whole_ref, f32[2,64,128]{2,1,0:T(8,128)S(1)} %get-tuple-element.19.real_ref, ...), custom_call_target="tpu_custom_call" | custom-call | tf_op jit(solution)/shard_map/sample/pallas_call | solution.py:462
  40.8 21.0 %all_to_all.16 = bf16[32,4,128]{2,1,0:T(4,128)(2,1)S(1)} all-to-all(bf16[32,4,128]{2,1,0:T(4,128)(2,1)S(1)} %bitcast.19), channel_id=1, replica_groups=mesh['sub'=32,'hgt'=16] {'sub'}, dimensions={0} | all-to-all | bytes 65536 | tf_op jit(solution)/shard_map/all_to_all | solution.py:479
  61.8 2.7 %collective-permute-start = (f32[16,2,2,128]{3,2,1,0:T(2,128)S(1)}, f32[16,2,2,128]{3,2,1,0:T(2,128)S(1)}, u32[]{:S(2)}, u32[]{:S(2)}) collective-permute-start(f32[16,2,2,128]{3,2,1,0:T(2,128)S(1)} %bitcast.22), channel_id=1, source_target_pairs={{1,0},{2,1},{3,2},{4,3},{5,4},{6,5},{7,6},{8,7},{9,8},{10,9},{11,1... | collective-permute-start | bytes 98312 | tf_op jit(solution)/shard_map/ppermute | solution.py:482
  64.6 5.2 %collective-permute-done = f32[16,2,2,128]{3,2,1,0:T(2,128)S(1)} collective-permute-done((f32[16,2,2,128]{3,2,1,0:T(2,128)S(1)}, f32[16,2,2,128]{3,2,1,0:T(2,128)S(1)}, u32[]{:S(2)}, u32[]{:S(2)}) %collective-permute-start) | collective-permute-done | bytes 32800 | tf_op jit(solution)/shard_map/ppermute | solution.py:482
  69.8 0.0 copy-done
  69.8 0.6 reshape.35
  (4 shorter events, 0.1 us)
Async XLA Ops:
  1.7 21.6 %all-to-all-start = ((bf16[16,2,2,2,8,128]{5,4,3,2,1,0:T(8,128)(2,1)}), bf16[16,2,2,2,8,128]{5,4,3,2,1,0:T(8,128)(2,1)S(1)}, u32[]{:S(2)}, u32[]{:S(2)}) async-start(bf16[16,2,2,2,8,128]{5,4,3,2,1,0:T(8,128)(2,1)} %bitcast.17), calls=%async_computation | async-start | bytes 524288 | tf_op jit(solution)/shard_map/all_to_all | solution.py:386
  23.9 45.8 %copy-start = (f32[64,128]{1,0:T(8,128)S(1)}, f32[64,128]{1,0:T(8,128)}, u32[]{:S(2)}) copy-start(f32[64,128]{1,0:T(8,128)} %get-tuple-element.13) | copy-start | bytes 98308
  61.8 7.9 %collective-permute-start = (f32[16,2,2,128]{3,2,1,0:T(2,128)S(1)}, f32[16,2,2,128]{3,2,1,0:T(2,128)S(1)}, u32[]{:S(2)}, u32[]{:S(2)}) collective-permute-start(f32[16,2,2,128]{3,2,1,0:T(2,128)S(1)} %bitcast.22), channel_id=1, source_target_pairs={{1,0},{2,1},{3,2},{4,3},{5,4},{6,5},{7,6},{8,7},{9,8},{10,9},{11,1... | collective-permute-start | bytes 98312 | tf_op jit(solution)/shard_map/ppermute | solution.py:482

commit v7 on v6

--- a/solution.py
+++ b/solution.py
@@ -251,11 +251,12 @@
 
 def range_columns(whole_ref, real_ref, step, width):
     place = pl.ds(step * 4, 4)
-    row_ids = lax.broadcasted_iota(jnp.int32, (width, 4 * LANES), 0)
+    row_ids = lax.broadcasted_iota(jnp.int16, (width, 4 * LANES), 0)
     inner = flat(whole_ref[0, place, :])
     frac = flat(real_ref[1, place, :])
-    column = jnp.where(row_ids == inner, 1.0 - frac, jnp.where(row_ids == inner + 1, frac, 0.0))
-    return column.astype(jnp.bfloat16)
+    low, high = (1.0 - frac).astype(jnp.bfloat16), frac.astype(jnp.bfloat16)
+    first, second = inner.astype(jnp.int16), (inner + 1).astype(jnp.int16)
+    return jnp.where(row_ids == first, low, jnp.where(row_ids == second, high, jnp.bfloat16(0)))
 
 
 def weights_kernel(whole_ref, real_ref, out_ref):
@@ -346,6 +347,14 @@
     out_ref[...] = order_ref[...].astype(jnp.bfloat16)
 
 
+def blend_kernel(tile_ref, above_ref, height_ref, out_ref):
+    for block in range(tile_ref.shape[0]):
+        height = height_ref[block * 4 : block * 4 + 4, :]
+        value = (1.0 - height) * tile_ref[block] + height * above_ref[block]
+        for row in range(out_ref.shape[0]):
+            out_ref[row, 0, :, block * LANES : (block + 1) * LANES] = value[2 * row : 2 * row + 2]
+
+
 def body(
     polar_beams,
     band_start,
@@ -396,7 +405,7 @@
             kept((3, row_count, LANES), jnp.int32),
             kept((2, row_count, LANES), f32),
             kept((2, row_count, LANES), f32),
-            shape((4 * members, LANES), f32),
+            kept((4 * members, LANES), f32),
         ],
         grid_spec=pltpu.PrefetchScalarGridSpec(
             num_scalar_prefetch=1,
@@ -477,12 +486,17 @@
     tile_rows = row_count // sub_count
     tiles = cart.reshape(sub_count, tile_rows * 2, LANES)
     tiles = lax.all_to_all(tiles, "sub", 0, 0, tiled=True).astype(f32)
-    tiles = tiles.reshape(sub_count // 4, 2, 2, tile_rows * 2, LANES)
-    tile = (tiles[:, 0] + tiles[:, 1]).reshape(members, tile_rows, 2, LANES)
+    tiles = tiles.reshape(sub_count // 4, 2, 2 * tile_rows * 2, LANES)
+    tile = (tiles[:, 0] + tiles[:, 1]).reshape(members, tile_rows * 2, LANES)
     above = lax.ppermute(tile, "hgt", [(i, i - 1) for i in range(1, layers)])
-    height = height.reshape(members, tile_rows, 2, LANES)
-    blended = (1.0 - height) * tile + height * above
-    return blended.transpose(1, 2, 0, 3).reshape(tile_rows, 1, 2, column_count)
+    return pl.pallas_call(
+        blend_kernel,
+        out_shape=shape((tile_rows, 1, 2, column_count), f32),
+        in_specs=[vmem] * 3,
+        out_specs=vmem,
+        interpret=interpret,
+        name="blend",
+    )(local(tile), local(above), local(height))
 
 
 def solution(mesh):

time: 70.9 us -> 70.5 us (level)
  waiting for transfers between devices: 12.2 us -> 13 us
    all_to_all x1, waiting for transfers between devices: 7.04 us -> 7.87 us  [body(): lax.all_to_all(slices, 'sub', 0, 0, axis_index_groups=halves, tiled=True)]
  transfers between devices with their start and end apart: 2 -> 2, of which waited for: 2 -> 2; matrix products, arithmetic and copies ran while one was open for 0% -> 0% of each run, Pallas kernels for 5% -> 4%
where the time goes in v7:
time: 70.5 us; the launch traced here: 70.2 us
  blocking collectives  35.3 us (50%)
  starting transfers between devices  13.2 us (19%)
  waiting for transfers between devices  13 us (18%)
  Pallas kernels  6.27 us (9%)
  local copies, waits for them, and re-layouts  1.67 us (2%)
    all_to_all x1, blocking collectives, body(): tiles = lax.all_to_all(tiles, 'sub', 0, 0, tiled=True).astype(f32)  21 us
    all_to_all x1, blocking collectives, body(): lax.all_to_all(windows, 'sub', 0, 0, axis_index_groups=halves, tiled=True)  14.4 us
    all_to_all x1, starting transfers between devices, body(): lax.all_to_all(slices, 'sub', 0, 0, axis_index_groups=halves, tiled=True)  10.4 us
    all_to_all x1, waiting for transfers between devices, body(): lax.all_to_all(slices, 'sub', 0, 0, axis_index_groups=halves, tiled=True)  7.87 us
    ppermute x1, waiting for transfers between devices, body(): above = lax.ppermute(tile, 'hgt', [(i, i - 1) for i in range(1, layers)])  5.17 us
    ppermute x1, starting transfers between devices, body(): above = lax.ppermute(tile, 'hgt', [(i, i - 1) for i in range(1, layers)])  2.74 us
    pallas_call x1, Pallas kernels, body(): pl.pallas_call(sample_kernel, out_shape=kept((2 * row_count, LANES), bf16...  2.33 us
    pallas_call x1, Pallas kernels, body(): pl.pallas_call(functools.partial(prepare_kernel, range_count=range_count)...  2.17 us
  transfers between devices with their start and end apart: 2, of which 2 were waited for; matrix products, arithmetic and copies ran while one was open for 0% of the time, Pallas kernels for 4%

profile of v7, /device:TPU:6, one launch (start us, length us, event | category | flops | bytes accessed | tf_op | source)
XLA Modules:
  0.0 70.2 jit_solution(1641627161800809237)
XLA Ops:
  0.0 1.7 %copy.12 = bf16[2,2,8,16,2,128]{5,2,4,1,0,3:T(8,128)(2,1)} copy(bf16[2,2,8,16,2,128]{5,2,4,3,1,0:T(8,128)(2,1)} %bitcast.17) | data formatting | bytes 524288 | tf_op jit(solution)/shard_map/reshape | solution.py:393
  1.7 10.4 %all-to-all-start = ((bf16[16,2,2,2,8,128]{5,4,3,2,1,0:T(8,128)(2,1)}), bf16[16,2,2,2,8,128]{5,4,3,2,1,0:T(8,128)(2,1)S(1)}, u32[]{:S(2)}, u32[]{:S(2)}) async-start(bf16[16,2,2,2,8,128]{5,4,3,2,1,0:T(8,128)(2,1)} %bitcast.12), calls=%async_computation | async-start | bytes 524288 | tf_op jit(solution)/shard_map/all_to_all | solution.py:395
  12.7 2.2 %prepare.1 = (f32[10,2,16,256]{3,2,1,0:T(8,128)S(1)}, bf16[64,32]{1,0:T(8,128)(2,1)S(1)}, bf16[32,32]{1,0:T(8,128)(2,1)S(1)}, bf16[64,64]{1,0:T(8,128)(2,1)S(1)}...) custom-call(s32[1]{0:T(128)} %bitcast.4.place_ref, ...), custom_call_target="tpu_custom_call" | custom-call | tf_op jit(solution)/shard_map/prepare/pallas_call | solution.py:398
  14.9 0.4 weights.1.before_ref.column_ref
  15.4 7.9 %all-to-all-done = bf16[16,2,2,2,8,128]{5,4,3,2,1,0:T(8,128)(2,1)S(1)} async-done(((bf16[16,2,2,2,8,128]{5,4,3,2,1,0:T(8,128)(2,1)}), bf16[16,2,2,2,8,128]{5,4,3,2,1,0:T(8,128)(2,1)S(1)}, u32[]{:S(2)}, u32[]{:S(2)}) %all-to-all-start) | async-done | bytes 262176 | tf_op jit(solution)/shard_map/all_to_all | solution.py:395
  23.2 0.7 merge.1
  23.9 14.4 %all_to_all.15.table_ref = bf16[16,2,16,256]{3,2,1,0:T(8,128)(2,1)S(1)} all-to-all(bf16[16,2,16,256]{3,2,1,0:T(8,128)(2,1)S(1)} %merge.1), channel_id=1, replica_groups={{0,16,64,80,128,144,192,208,256,272,320,336,384,400,448,464},{32,48,96,..., dimensions={0} | all-to-all | bytes 524288 | tf_op jit(solution)/shard_map/all_to_all | solution.py:470
  38.3 2.3 %sample.1 = bf16[128,128]{1,0:T(8,128)(2,1)S(1)} custom-call(bf16[16,2,16,256]{3,2,1,0:T(8,128)(2,1)S(1)} %all_to_all.15.table_ref, bf16[8,256,512]{2,1,0:T(8,128)(2,1)S(1)} %weights.1.before_ref.column_ref, s32[3,64,128]{2,1,0:T(8,128)S(1)} %get-tuple-element.17.whole_ref, f32[2,64,128]{2,1,0:T(8,128)S(1)} %get-tuple-element.18.real_ref, ...), custom_call_target="tpu_custom_call" | custom-call | tf_op jit(solution)/shard_map/sample/pallas_call | solution.py:471
  40.6 21.0 %all_to_all.16 = bf16[32,4,128]{2,1,0:T(4,128)(2,1)S(1)} all-to-all(bf16[32,4,128]{2,1,0:T(4,128)(2,1)S(1)} %bitcast.14), channel_id=1, replica_groups=mesh['sub'=32,'hgt'=16] {'sub'}, dimensions={0} | all-to-all | bytes 65536 | tf_op jit(solution)/shard_map/all_to_all | solution.py:488
  61.6 2.7 %collective-permute-start = (f32[16,4,128]{2,1,0:T(4,128)S(1)}, f32[16,4,128]{2,1,0:T(4,128)S(1)}, u32[]{:S(2)}, u32[]{:S(2)}) collective-permute-start(f32[16,4,128]{2,1,0:T(4,128)S(1)} %bitcast.15), channel_id=1, source_target_pairs={{1,0},{2,1},{3,2},{4,3},{5,4},{6,5},{7,6},{8,7},{9,8},{10,9},{11,1... | collective-permute-start | bytes 98312 | tf_op jit(solution)/shard_map/ppermute | solution.py:491
  64.4 5.2 %collective-permute-done.above_ref = f32[16,4,128]{2,1,0:T(4,128)S(1)} collective-permute-done((f32[16,4,128]{2,1,0:T(4,128)S(1)}, f32[16,4,128]{2,1,0:T(4,128)S(1)}, u32[]{:S(2)}, u32[]{:S(2)}) %collective-permute-start) | collective-permute-done | bytes 32800 | tf_op jit(solution)/shard_map/ppermute | solution.py:491
  69.5 0.6 blend.1
  (2 shorter events, 0.0 us)
Async XLA Ops:
  1.7 21.6 %all-to-all-start = ((bf16[16,2,2,2,8,128]{5,4,3,2,1,0:T(8,128)(2,1)}), bf16[16,2,2,2,8,128]{5,4,3,2,1,0:T(8,128)(2,1)S(1)}, u32[]{:S(2)}, u32[]{:S(2)}) async-start(bf16[16,2,2,2,8,128]{5,4,3,2,1,0:T(8,128)(2,1)} %bitcast.12), calls=%async_computation | async-start | bytes 524288 | tf_op jit(solution)/shard_map/all_to_all | solution.py:395
  61.6 7.9 %collective-permute-start = (f32[16,4,128]{2,1,0:T(4,128)S(1)}, f32[16,4,128]{2,1,0:T(4,128)S(1)}, u32[]{:S(2)}, u32[]{:S(2)}) collective-permute-start(f32[16,4,128]{2,1,0:T(4,128)S(1)} %bitcast.15), channel_id=1, source_target_pairs={{1,0},{2,1},{3,2},{4,3},{5,4},{6,5},{7,6},{8,7},{9,8},{10,9},{11,1... | collective-permute-start | bytes 98312 | tf_op jit(solution)/shard_map/ppermute | solution.py:491

commit v8 on v7

--- a/solution.py
+++ b/solution.py
@@ -290,13 +290,6 @@
             before = pltpu.roll(values[k - 1], k, 1)
             after = pltpu.roll(values[k], k, 1) if k < slices else before
             block_ref[k, part] = jnp.where(lane < k, before, after)
-    for quarter in range(4):
-        low = 2 * quarter + 2
-        for k in range(blocks):
-            pair = [block_ref[k, part, low : low + QUARTER, :] for part in range(parts)]
-            lhs_ref[quarter, k * rows : (k + 1) * rows, :] = jnp.concatenate(pair, axis=0).astype(
-                jnp.bfloat16
-            )
     beam_ids = lax.broadcasted_iota(jnp.int32, (QUARTER, column_ref.shape[2]), 0)
 
     def chunk(quarter, step, columns):
@@ -319,14 +312,17 @@
             for i in range(4):
                 cart_ref[part, pl.ds(step * 4 + i, 1), :] = summed[:, i * LANES : (i + 1) * LANES]
 
-    def window(quarter, carry):
+    for quarter in range(4):
+        low = 2 * quarter + 2
+        for k in range(blocks):
+            pair = [block_ref[k, part, low : low + QUARTER, :] for part in range(parts)]
+            lhs_ref[quarter, k * rows : (k + 1) * rows, :] = jnp.concatenate(pair, axis=0).astype(
+                jnp.bfloat16
+            )
         for i in range(2):
             step = quarter * 4 + 2 * i
             chunk(quarter, step, column_ref[quarter * 2 + i])
             chunk(quarter, step + 1, range_columns(whole_ref, real_ref, step + 1, width))
-        return carry
-
-    lax.fori_loop(0, 4, window, 0)
     for group in range(ROWS // 32):
         ordered = [
             swap_quarters(

time: 70.5 us -> 69.9 us (level)
  no operation moved by 1% of the time
where the time goes in v8:
time: 69.9 us; the launch traced here: 69.5 us
  blocking collectives  35.3 us (51%)
  starting transfers between devices  13.2 us (19%)
  waiting for transfers between devices  13 us (19%)
  Pallas kernels  5.61 us (8%)
  local copies, waits for them, and re-layouts  1.67 us (2%)
    all_to_all x1, blocking collectives, body(): tiles = lax.all_to_all(tiles, 'sub', 0, 0, tiled=True).astype(f32)  21 us
    all_to_all x1, blocking collectives, body(): lax.all_to_all(windows, 'sub', 0, 0, axis_index_groups=halves, tiled=True)  14.4 us
    all_to_all x1, starting transfers between devices, body(): lax.all_to_all(slices, 'sub', 0, 0, axis_index_groups=halves, tiled=True)  10.4 us
    all_to_all x1, waiting for transfers between devices, body(): lax.all_to_all(slices, 'sub', 0, 0, axis_index_groups=halves, tiled=True)  7.87 us
    ppermute x1, waiting for transfers between devices, body(): above = lax.ppermute(tile, 'hgt', [(i, i - 1) for i in range(1, layers)])  5.17 us
    ppermute x1, starting transfers between devices, body(): above = lax.ppermute(tile, 'hgt', [(i, i - 1) for i in range(1, layers)])  2.74 us
    pallas_call x1, Pallas kernels, body(): pl.pallas_call(functools.partial(prepare_kernel, range_count=range_count)...  2.17 us
    pallas_call x1, Pallas kernels, body(): pl.pallas_call(sample_kernel, out_shape=kept((2 * row_count, LANES), bf16...  1.67 us
  transfers between devices with their start and end apart: 2, of which 2 were waited for; matrix products, arithmetic and copies ran while one was open for 0% of the time, Pallas kernels for 4%

profile of v8, /device:TPU:6, one launch (start us, length us, event | category | flops | bytes accessed | tf_op | source)
XLA Modules:
  0.0 69.5 jit_solution(2914112557814525044)
XLA Ops:
  0.0 1.7 %copy.12 = bf16[2,2,8,16,2,128]{5,2,4,1,0,3:T(8,128)(2,1)} copy(bf16[2,2,8,16,2,128]{5,2,4,3,1,0:T(8,128)(2,1)} %bitcast.17) | data formatting | bytes 524288 | tf_op jit(solution)/shard_map/reshape | solution.py:389
  1.7 10.4 %all-to-all-start = ((bf16[16,2,2,2,8,128]{5,4,3,2,1,0:T(8,128)(2,1)}), bf16[16,2,2,2,8,128]{5,4,3,2,1,0:T(8,128)(2,1)S(1)}, u32[]{:S(2)}, u32[]{:S(2)}) async-start(bf16[16,2,2,2,8,128]{5,4,3,2,1,0:T(8,128)(2,1)} %bitcast.12), calls=%async_computation | async-start | bytes 524288 | tf_op jit(solution)/shard_map/all_to_all | solution.py:391
  12.7 2.2 %prepare.1 = (f32[10,2,16,256]{3,2,1,0:T(8,128)S(1)}, bf16[64,32]{1,0:T(8,128)(2,1)S(1)}, bf16[32,32]{1,0:T(8,128)(2,1)S(1)}, bf16[64,64]{1,0:T(8,128)(2,1)S(1)}...) custom-call(s32[1]{0:T(128)} %bitcast.4.place_ref, ...), custom_call_target="tpu_custom_call" | custom-call | tf_op jit(solution)/shard_map/prepare/pallas_call | solution.py:394
  14.9 0.4 weights.1.before_ref.column_ref
  15.4 7.9 %all-to-all-done = bf16[16,2,2,2,8,128]{5,4,3,2,1,0:T(8,128)(2,1)S(1)} async-done(((bf16[16,2,2,2,8,128]{5,4,3,2,1,0:T(8,128)(2,1)}), bf16[16,2,2,2,8,128]{5,4,3,2,1,0:T(8,128)(2,1)S(1)}, u32[]{:S(2)}, u32[]{:S(2)}) %all-to-all-start) | async-done | bytes 262176 | tf_op jit(solution)/shard_map/all_to_all | solution.py:391
  23.2 0.7 merge.1
  23.9 14.4 %all_to_all.15.table_ref = bf16[16,2,16,256]{3,2,1,0:T(8,128)(2,1)S(1)} all-to-all(bf16[16,2,16,256]{3,2,1,0:T(8,128)(2,1)S(1)} %merge.1), channel_id=1, replica_groups={{0,16,64,80,128,144,192,208,256,272,320,336,384,400,448,464},{32,48,96,..., dimensions={0} | all-to-all | bytes 524288 | tf_op jit(solution)/shard_map/all_to_all | solution.py:466
  38.3 1.7 %sample.1 = bf16[128,128]{1,0:T(8,128)(2,1)S(1)} custom-call(bf16[16,2,16,256]{3,2,1,0:T(8,128)(2,1)S(1)} %all_to_all.15.table_ref, bf16[8,256,512]{2,1,0:T(8,128)(2,1)S(1)} %weights.1.before_ref.column_ref, s32[3,64,128]{2,1,0:T(8,128)S(1)} %get-tuple-element.17.whole_ref, f32[2,64,128]{2,1,0:T(8,128)S(1)} %get-tuple-element.18.real_ref, ...), custom_call_target="tpu_custom_call" | custom-call | tf_op jit(solution)/shard_map/sample/pallas_call | solution.py:467
  40.0 21.0 %all_to_all.16 = bf16[32,4,128]{2,1,0:T(4,128)(2,1)S(1)} all-to-all(bf16[32,4,128]{2,1,0:T(4,128)(2,1)S(1)} %bitcast.14), channel_id=1, replica_groups=mesh['sub'=32,'hgt'=16] {'sub'}, dimensions={0} | all-to-all | bytes 65536 | tf_op jit(solution)/shard_map/all_to_all | solution.py:484
  61.0 2.7 %collective-permute-start = (f32[16,4,128]{2,1,0:T(4,128)S(1)}, f32[16,4,128]{2,1,0:T(4,128)S(1)}, u32[]{:S(2)}, u32[]{:S(2)}) collective-permute-start(f32[16,4,128]{2,1,0:T(4,128)S(1)} %bitcast.15), channel_id=1, source_target_pairs={{1,0},{2,1},{3,2},{4,3},{5,4},{6,5},{7,6},{8,7},{9,8},{10,9},{11,1... | collective-permute-start | bytes 98312 | tf_op jit(solution)/shard_map/ppermute | solution.py:487
  63.7 5.2 %collective-permute-done.above_ref = f32[16,4,128]{2,1,0:T(4,128)S(1)} collective-permute-done((f32[16,4,128]{2,1,0:T(4,128)S(1)}, f32[16,4,128]{2,1,0:T(4,128)S(1)}, u32[]{:S(2)}, u32[]{:S(2)}) %collective-permute-start) | collective-permute-done | bytes 32800 | tf_op jit(solution)/shard_map/ppermute | solution.py:487
  68.9 0.6 blend.1
  (2 shorter events, 0.0 us)
Async XLA Ops:
  1.7 21.6 %all-to-all-start = ((bf16[16,2,2,2,8,128]{5,4,3,2,1,0:T(8,128)(2,1)}), bf16[16,2,2,2,8,128]{5,4,3,2,1,0:T(8,128)(2,1)S(1)}, u32[]{:S(2)}, u32[]{:S(2)}) async-start(bf16[16,2,2,2,8,128]{5,4,3,2,1,0:T(8,128)(2,1)} %bitcast.12), calls=%async_computation | async-start | bytes 524288 | tf_op jit(solution)/shard_map/all_to_all | solution.py:391
  61.0 7.9 %collective-permute-start = (f32[16,4,128]{2,1,0:T(4,128)S(1)}, f32[16,4,128]{2,1,0:T(4,128)S(1)}, u32[]{:S(2)}, u32[]{:S(2)}) collective-permute-start(f32[16,4,128]{2,1,0:T(4,128)S(1)} %bitcast.15), channel_id=1, source_target_pairs={{1,0},{2,1},{3,2},{4,3},{5,4},{6,5},{7,6},{8,7},{9,8},{10,9},{11,1... | collective-permute-start | bytes 98312 | tf_op jit(solution)/shard_map/ppermute | solution.py:487

commit v9 on v8

--- a/solution.py
+++ b/solution.py
@@ -10,7 +10,9 @@
 range_phase = 0.003
 LANES = 128
 WINDOW = 16
-HALO = 4
+SENT = 13
+PACKED = 56
+HALO = 2
 QUARTER = 8
 ROWS = 64
 
@@ -161,7 +163,7 @@
             block = (sample + 1 + (sample >> 8)) >> 8
             whole_ref[0, place, :] = sample - block * (width - 1)
             whole_ref[1, place, :] = block
-            whole_ref[2, place, :] = beam_parts[quarter] - (2 * quarter + 2)
+            whole_ref[2, place, :] = beam_parts[quarter] - 2 * quarter
             for i in range(2):
                 real_ref[i, place, :] = frac_parts[i][quarter]
 
@@ -172,7 +174,7 @@
 
 
 def merge_kernel(
-    data_ref, trig_ref, first_ref, second_ref, third_ref, before_ref, out_ref, padded_ref, *, groups
+    data_ref, trig_ref, first_ref, second_ref, third_ref, before_ref, out_ref, padded_ref, stage_ref, *, groups
 ):
     del before_ref
     beams, width = data_ref.shape[2], data_ref.shape[3]
@@ -240,9 +242,15 @@
                 for part, value in enumerate(add(terms[0], terms[1])):
                     padded_ref[part, start : start + beams, :] = value
     for block in range(out_ref.shape[0]):
-        for part in range(2):
-            rows = padded_ref[part, 8 * block : 8 * block + WINDOW, :]
-            out_ref[block, part] = rows.astype(jnp.bfloat16)
+        for piece in range(width // LANES):
+            for part in range(2):
+                row = (piece * 2 + part) * SENT
+                stage_ref[block, row : row + SENT, :] = padded_ref[
+                    part, 8 * block : 8 * block + SENT, piece * LANES : (piece + 1) * LANES
+                ]
+        row = 2 * (width // LANES) * SENT
+        stage_ref[block, row:, :] = jnp.zeros((PACKED - row, LANES), jnp.float32)
+        out_ref[block] = stage_ref[block].astype(jnp.bfloat16)
 
 
 def flat(value):
@@ -274,17 +282,27 @@
     real_ref,
     pixel_ref,
     out_ref,
+    table_scratch,
     block_ref,
     lhs_ref,
     cart_ref,
     order_ref,
 ):
-    slices, parts, _, width = table_ref.shape
+    slices = table_ref.shape[0]
+    parts, width = block_ref.shape[1], block_ref.shape[3]
     blocks = slices + 1
+    for i in range(slices):
+        table_scratch[i] = table_ref[i].astype(jnp.float32)
     rows = parts * QUARTER
     lane = lax.broadcasted_iota(jnp.int32, (WINDOW, width), 1)
     for part in range(parts):
-        values = [table_ref[i, part].astype(jnp.float32) for i in range(slices)]
+        starts = [(piece * parts + part) * SENT for piece in range(width // LANES)]
+        values = [
+            jnp.concatenate(
+                [table_scratch[i, start : start + WINDOW, :] for start in starts], axis=1
+            )
+            for i in range(slices)
+        ]
         block_ref[0, part] = values[0]
         for k in range(1, blocks):
             before = pltpu.roll(values[k - 1], k, 1)
@@ -313,7 +331,7 @@
                 cart_ref[part, pl.ds(step * 4 + i, 1), :] = summed[:, i * LANES : (i + 1) * LANES]
 
     for quarter in range(4):
-        low = 2 * quarter + 2
+        low = 2 * quarter
         for k in range(blocks):
             pair = [block_ref[k, part, low : low + QUARTER, :] for part in range(parts)]
             lhs_ref[quarter, k * rows : (k + 1) * rows, :] = jnp.concatenate(pair, axis=0).astype(
@@ -455,10 +473,13 @@
     )(local(whole), local(real))
     windows = pl.pallas_call(
         functools.partial(merge_kernel, groups=sub_count // 2**levels),
-        out_shape=kept((members, 2, WINDOW, width), bf16),
+        out_shape=kept((members, PACKED, LANES), bf16),
         in_specs=[vmem] * 5 + [pl.BlockSpec(memory_space=pl.ANY)],
         out_specs=vmem,
-        scratch_shapes=[pltpu.VMEM((2, 144, width), f32)],
+        scratch_shapes=[
+            pltpu.VMEM((2, 144, width), f32),
+            pltpu.VMEM((members, PACKED, LANES), f32),
+        ],
         compiler_params=limit,
         interpret=interpret,
         name="merge",
@@ -470,6 +491,7 @@
         in_specs=[vmem] * 5,
         out_specs=vmem,
         scratch_shapes=[
+            pltpu.VMEM((members, PACKED, LANES), f32),
             pltpu.VMEM((members + 1, 2, WINDOW, width), f32),
             pltpu.VMEM((4, (members + 1) * 2 * QUARTER, width), bf16),
             pltpu.VMEM((2, row_count, LANES), f32),

time: 69.9 us -> 69.1 us (0.989)
  blocking collectives: 35.3 us -> 34.6 us
where the time goes in v9:
time: 69.1 us; the launch traced here: 68.8 us
  blocking collectives  34.6 us (50%)
  starting transfers between devices  13.2 us (19%)
  waiting for transfers between devices  13 us (19%)
  Pallas kernels  5.59 us (8%)
  local copies, waits for them, and re-layouts  1.67 us (2%)
    all_to_all x1, blocking collectives, body(): tiles = lax.all_to_all(tiles, 'sub', 0, 0, tiled=True).astype(f32)  20.9 us
    all_to_all x1, blocking collectives, body(): lax.all_to_all(windows, 'sub', 0, 0, axis_index_groups=halves, tiled=True)  13.7 us
    all_to_all x1, starting transfers between devices, body(): lax.all_to_all(slices, 'sub', 0, 0, axis_index_groups=halves, tiled=True)  10.4 us
    all_to_all x1, waiting for transfers between devices, body(): lax.all_to_all(slices, 'sub', 0, 0, axis_index_groups=halves, tiled=True)  7.87 us
    ppermute x1, waiting for transfers between devices, body(): above = lax.ppermute(tile, 'hgt', [(i, i - 1) for i in range(1, layers)])  5.16 us
    ppermute x1, starting transfers between devices, body(): above = lax.ppermute(tile, 'hgt', [(i, i - 1) for i in range(1, layers)])  2.75 us
    pallas_call x1, Pallas kernels, body(): pl.pallas_call(functools.partial(prepare_kernel, range_count=range_count)...  2.17 us
    reshape x1, local copies, waits for them, and re-layouts, body(): polar_beams.reshape(2, beams // 8, 8, members, width // LANES, LANES)  1.67 us
  transfers between devices with their start and end apart: 2, of which 2 were waited for; matrix products, arithmetic and copies ran while one was open for 0% of the time, Pallas kernels for 4%

profile of v9, /device:TPU:6, one launch (start us, length us, event | category | flops | bytes accessed | tf_op | source)
XLA Modules:
  0.0 68.8 jit_solution(3328250995188476887)
XLA Ops:
  0.0 1.7 %copy.12 = bf16[2,2,8,16,2,128]{5,2,4,1,0,3:T(8,128)(2,1)} copy(bf16[2,2,8,16,2,128]{5,2,4,3,1,0:T(8,128)(2,1)} %bitcast.17) | data formatting | bytes 524288 | tf_op jit(solution)/shard_map/reshape | solution.py:407
  1.7 10.4 %all-to-all-start = ((bf16[16,2,2,2,8,128]{5,4,3,2,1,0:T(8,128)(2,1)}), bf16[16,2,2,2,8,128]{5,4,3,2,1,0:T(8,128)(2,1)S(1)}, u32[]{:S(2)}, u32[]{:S(2)}) async-start(bf16[16,2,2,2,8,128]{5,4,3,2,1,0:T(8,128)(2,1)} %bitcast.12), calls=%async_computation | async-start | bytes 524288 | tf_op jit(solution)/shard_map/all_to_all | solution.py:409
  12.7 2.2 %prepare.1 = (f32[10,2,16,256]{3,2,1,0:T(8,128)S(1)}, bf16[64,32]{1,0:T(8,128)(2,1)S(1)}, bf16[32,32]{1,0:T(8,128)(2,1)S(1)}, bf16[64,64]{1,0:T(8,128)(2,1)S(1)}...) custom-call(s32[1]{0:T(128)} %bitcast.4.place_ref, ...), custom_call_target="tpu_custom_call" | custom-call | tf_op jit(solution)/shard_map/prepare/pallas_call | solution.py:412
  14.9 0.4 weights.1.before_ref.column_ref
  15.4 7.9 %all-to-all-done = bf16[16,2,2,2,8,128]{5,4,3,2,1,0:T(8,128)(2,1)S(1)} async-done(((bf16[16,2,2,2,8,128]{5,4,3,2,1,0:T(8,128)(2,1)}), bf16[16,2,2,2,8,128]{5,4,3,2,1,0:T(8,128)(2,1)S(1)}, u32[]{:S(2)}, u32[]{:S(2)}) %all-to-all-start) | async-done | bytes 262176 | tf_op jit(solution)/shard_map/all_to_all | solution.py:409
  23.2 0.7 %merge.1 = bf16[16,56,128]{2,1,0:T(8,128)(2,1)S(1)} custom-call(bf16[16,2,16,256]{3,2,1,0:T(8,128)(2,1)S(1)} %bitcast.13, f32[10,2,16,256]{3,2,1,0:T(8,128)S(1)} %get-tuple-element.13.trig_ref, bf16[64,32]{1,0:T(8,128)(2,1)S(1)} %get-tuple-element.14.first_ref, bf16[32,32]{1,0:T(8,128)(2,1)S(1)} %get-tuple-element.15.second_ref, ...), custom_call_target="tpu_custom_call" | custom-call | tf_op jit(solution)/shard_map/merge/pallas_call | solution.py:474
  24.0 13.7 %all_to_all.15.table_ref = bf16[16,56,128]{2,1,0:T(8,128)(2,1)S(1)} all-to-all(bf16[16,56,128]{2,1,0:T(8,128)(2,1)S(1)} %merge.1), channel_id=1, replica_groups={{0,16,64,80,128,144,192,208,256,272,320,336,384,400,448,464},{32,48,96,..., dimensions={0} | all-to-all | bytes 458752 | tf_op jit(solution)/shard_map/all_to_all | solution.py:487
  37.7 1.6 %sample.1 = bf16[128,128]{1,0:T(8,128)(2,1)S(1)} custom-call(bf16[16,56,128]{2,1,0:T(8,128)(2,1)S(1)} %all_to_all.15.table_ref, bf16[8,256,512]{2,1,0:T(8,128)(2,1)S(1)} %weights.1.before_ref.column_ref, s32[3,64,128]{2,1,0:T(8,128)S(1)} %get-tuple-element.17.whole_ref, f32[2,64,128]{2,1,0:T(8,128)S(1)} %get-tuple-element.18.real_ref, ...), custom_call_target="tpu_custom_call" | custom-call | tf_op jit(solution)/shard_map/sample/pallas_call | solution.py:488
  39.3 20.9 %all_to_all.16 = bf16[32,4,128]{2,1,0:T(4,128)(2,1)S(1)} all-to-all(bf16[32,4,128]{2,1,0:T(4,128)(2,1)S(1)} %bitcast.14), channel_id=1, replica_groups=mesh['sub'=32,'hgt'=16] {'sub'}, dimensions={0} | all-to-all | bytes 65536 | tf_op jit(solution)/shard_map/all_to_all | solution.py:506
  60.2 2.7 %collective-permute-start = (f32[16,4,128]{2,1,0:T(4,128)S(1)}, f32[16,4,128]{2,1,0:T(4,128)S(1)}, u32[]{:S(2)}, u32[]{:S(2)}) collective-permute-start(f32[16,4,128]{2,1,0:T(4,128)S(1)} %bitcast.15), channel_id=1, source_target_pairs={{1,0},{2,1},{3,2},{4,3},{5,4},{6,5},{7,6},{8,7},{9,8},{10,9},{11,1... | collective-permute-start | bytes 98312 | tf_op jit(solution)/shard_map/ppermute | solution.py:509
  63.0 5.2 %collective-permute-done.above_ref = f32[16,4,128]{2,1,0:T(4,128)S(1)} collective-permute-done((f32[16,4,128]{2,1,0:T(4,128)S(1)}, f32[16,4,128]{2,1,0:T(4,128)S(1)}, u32[]{:S(2)}, u32[]{:S(2)}) %collective-permute-start) | collective-permute-done | bytes 32800 | tf_op jit(solution)/shard_map/ppermute | solution.py:509
  68.2 0.6 blend.1
  (2 shorter events, 0.0 us)
Async XLA Ops:
  1.7 21.6 %all-to-all-start = ((bf16[16,2,2,2,8,128]{5,4,3,2,1,0:T(8,128)(2,1)}), bf16[16,2,2,2,8,128]{5,4,3,2,1,0:T(8,128)(2,1)S(1)}, u32[]{:S(2)}, u32[]{:S(2)}) async-start(bf16[16,2,2,2,8,128]{5,4,3,2,1,0:T(8,128)(2,1)} %bitcast.12), calls=%async_computation | async-start | bytes 524288 | tf_op jit(solution)/shard_map/all_to_all | solution.py:409
  60.2 7.9 %collective-permute-start = (f32[16,4,128]{2,1,0:T(4,128)S(1)}, f32[16,4,128]{2,1,0:T(4,128)S(1)}, u32[]{:S(2)}, u32[]{:S(2)}) collective-permute-start(f32[16,4,128]{2,1,0:T(4,128)S(1)} %bitcast.15), channel_id=1, source_target_pairs={{1,0},{2,1},{3,2},{4,3},{5,4},{6,5},{7,6},{8,7},{9,8},{10,9},{11,1... | collective-permute-start | bytes 98312 | tf_op jit(solution)/shard_map/ppermute | solution.py:509

commit v10 on v9

--- a/solution.py
+++ b/solution.py
@@ -362,11 +362,18 @@
 
 
 def blend_kernel(tile_ref, above_ref, height_ref, out_ref):
-    for block in range(tile_ref.shape[0]):
-        height = height_ref[block * 4 : block * 4 + 4, :]
-        value = (1.0 - height) * tile_ref[block] + height * above_ref[block]
-        for row in range(out_ref.shape[0]):
-            out_ref[row, 0, :, block * LANES : (block + 1) * LANES] = value[2 * row : 2 * row + 2]
+    def pair(ref, group):
+        rows = ref[group * 16 : group * 16 + 16, :].astype(jnp.float32)
+        return rows[0:8] + rows[8:16]
+
+    for group in range(tile_ref.shape[0] // 16):
+        height = height_ref[group * 8 : group * 8 + 8, :]
+        value = (1.0 - height) * pair(tile_ref, group) + height * pair(above_ref, group)
+        for core in range(2):
+            lanes = slice((group * 2 + core) * LANES, (group * 2 + core + 1) * LANES)
+            for row in range(out_ref.shape[0]):
+                start = core * 4 + 2 * row
+                out_ref[row, 0, :, lanes] = value[start : start + 2]
 
 
 def body(
@@ -503,10 +510,9 @@
     )(table, local(columns), local(whole), local(real), local(pixel))
     tile_rows = row_count // sub_count
     tiles = cart.reshape(sub_count, tile_rows * 2, LANES)
-    tiles = lax.all_to_all(tiles, "sub", 0, 0, tiled=True).astype(f32)
-    tiles = tiles.reshape(sub_count // 4, 2, 2 * tile_rows * 2, LANES)
-    tile = (tiles[:, 0] + tiles[:, 1]).reshape(members, tile_rows * 2, LANES)
-    above = lax.ppermute(tile, "hgt", [(i, i - 1) for i in range(1, layers)])
+    tiles = lax.all_to_all(tiles, "sub", 0, 0, tiled=True)
+    tiles = tiles.reshape(2 * row_count, LANES)
+    above = lax.ppermute(tiles, "hgt", [(i, i - 1) for i in range(1, layers)])
     return pl.pallas_call(
         blend_kernel,
         out_shape=shape((tile_rows, 1, 2, column_count), f32),
@@ -514,7 +520,7 @@
         out_specs=vmem,
         interpret=interpret,
         name="blend",
-    )(local(tile), local(above), local(height))
+    )(local(tiles), local(above), local(height))
 
 
 def solution(mesh):

time: 69.1 us -> 69.1 us (level)
  no operation moved by 1% of the time
where the time goes in v10:
time: 69.1 us; the launch traced here: 68.8 us
  blocking collectives  34.6 us (50%)
  starting transfers between devices  13.2 us (19%)
  waiting for transfers between devices  13 us (19%)
  Pallas kernels  5.59 us (8%)
  local copies, waits for them, and re-layouts  1.67 us (2%)
    all_to_all x1, blocking collectives, body(): tiles = lax.all_to_all(tiles, 'sub', 0, 0, tiled=True)  20.9 us
    all_to_all x1, blocking collectives, body(): lax.all_to_all(windows, 'sub', 0, 0, axis_index_groups=halves, tiled=True)  13.7 us
    all_to_all x1, starting transfers between devices, body(): lax.all_to_all(slices, 'sub', 0, 0, axis_index_groups=halves, tiled=True)  10.4 us
    all_to_all x1, waiting for transfers between devices, body(): lax.all_to_all(slices, 'sub', 0, 0, axis_index_groups=halves, tiled=True)  7.87 us
    ppermute x1, waiting for transfers between devices, body(): above = lax.ppermute(tiles, 'hgt', [(i, i - 1) for i in range(1, layers)])  5.16 us
    ppermute x1, starting transfers between devices, body(): above = lax.ppermute(tiles, 'hgt', [(i, i - 1) for i in range(1, layers)])  2.74 us
    pallas_call x1, Pallas kernels, body(): pl.pallas_call(functools.partial(prepare_kernel, range_count=range_count)...  2.17 us
    reshape x1, local copies, waits for them, and re-layouts, body(): polar_beams.reshape(2, beams // 8, 8, members, width // LANES, LANES)  1.67 us
  transfers between devices with their start and end apart: 2, of which 2 were waited for; matrix products, arithmetic and copies ran while one was open for 0% of the time, Pallas kernels for 4%

profile of v10, /device:TPU:6, one launch (start us, length us, event | category | flops | bytes accessed | tf_op | source)
XLA Modules:
  0.0 68.8 jit_solution(5286370759167113880)
XLA Ops:
  0.0 1.7 %copy.11 = bf16[2,2,8,16,2,128]{5,2,4,1,0,3:T(8,128)(2,1)} copy(bf16[2,2,8,16,2,128]{5,2,4,3,1,0:T(8,128)(2,1)} %bitcast.15) | data formatting | bytes 524288 | tf_op jit(solution)/shard_map/reshape | solution.py:414
  1.7 10.4 %all-to-all-start = ((bf16[16,2,2,2,8,128]{5,4,3,2,1,0:T(8,128)(2,1)}), bf16[16,2,2,2,8,128]{5,4,3,2,1,0:T(8,128)(2,1)S(1)}, u32[]{:S(2)}, u32[]{:S(2)}) async-start(bf16[16,2,2,2,8,128]{5,4,3,2,1,0:T(8,128)(2,1)} %bitcast.10), calls=%async_computation | async-start | bytes 524288 | tf_op jit(solution)/shard_map/all_to_all | solution.py:416
  12.7 2.2 %prepare.1 = (f32[10,2,16,256]{3,2,1,0:T(8,128)S(1)}, bf16[64,32]{1,0:T(8,128)(2,1)S(1)}, bf16[32,32]{1,0:T(8,128)(2,1)S(1)}, bf16[64,64]{1,0:T(8,128)(2,1)S(1)}...) custom-call(s32[1]{0:T(128)} %bitcast.4.place_ref, ...), custom_call_target="tpu_custom_call" | custom-call | tf_op jit(solution)/shard_map/prepare/pallas_call | solution.py:419
  14.9 0.4 weights.1.before_ref.column_ref
  15.4 7.9 %all-to-all-done = bf16[16,2,2,2,8,128]{5,4,3,2,1,0:T(8,128)(2,1)S(1)} async-done(((bf16[16,2,2,2,8,128]{5,4,3,2,1,0:T(8,128)(2,1)}), bf16[16,2,2,2,8,128]{5,4,3,2,1,0:T(8,128)(2,1)S(1)}, u32[]{:S(2)}, u32[]{:S(2)}) %all-to-all-start) | async-done | bytes 262176 | tf_op jit(solution)/shard_map/all_to_all | solution.py:416
  23.2 0.7 %merge.1 = bf16[16,56,128]{2,1,0:T(8,128)(2,1)S(1)} custom-call(bf16[16,2,16,256]{3,2,1,0:T(8,128)(2,1)S(1)} %bitcast.11, f32[10,2,16,256]{3,2,1,0:T(8,128)S(1)} %get-tuple-element.13.trig_ref, bf16[64,32]{1,0:T(8,128)(2,1)S(1)} %get-tuple-element.14.first_ref, bf16[32,32]{1,0:T(8,128)(2,1)S(1)} %get-tuple-element.15.second_ref, ...), custom_call_target="tpu_custom_call" | custom-call | tf_op jit(solution)/shard_map/merge/pallas_call | solution.py:481
  24.0 13.7 %all_to_all.15.table_ref = bf16[16,56,128]{2,1,0:T(8,128)(2,1)S(1)} all-to-all(bf16[16,56,128]{2,1,0:T(8,128)(2,1)S(1)} %merge.1), channel_id=1, replica_groups={{0,16,64,80,128,144,192,208,256,272,320,336,384,400,448,464},{32,48,96,..., dimensions={0} | all-to-all | bytes 458752 | tf_op jit(solution)/shard_map/all_to_all | solution.py:494
  37.7 1.6 %sample.1 = bf16[128,128]{1,0:T(8,128)(2,1)S(1)} custom-call(bf16[16,56,128]{2,1,0:T(8,128)(2,1)S(1)} %all_to_all.15.table_ref, bf16[8,256,512]{2,1,0:T(8,128)(2,1)S(1)} %weights.1.before_ref.column_ref, s32[3,64,128]{2,1,0:T(8,128)S(1)} %get-tuple-element.17.whole_ref, f32[2,64,128]{2,1,0:T(8,128)S(1)} %get-tuple-element.18.real_ref, ...), custom_call_target="tpu_custom_call" | custom-call | tf_op jit(solution)/shard_map/sample/pallas_call | solution.py:495
  39.3 20.9 %all_to_all.16 = bf16[32,4,128]{2,1,0:T(4,128)(2,1)S(1)} all-to-all(bf16[32,4,128]{2,1,0:T(4,128)(2,1)S(1)} %bitcast.12), channel_id=1, replica_groups=mesh['sub'=32,'hgt'=16] {'sub'}, dimensions={0} | all-to-all | bytes 65536 | tf_op jit(solution)/shard_map/all_to_all | solution.py:513
  60.2 2.7 %collective-permute-start = (bf16[128,128]{1,0:T(8,128)(2,1)S(1)}, bf16[128,128]{1,0:T(8,128)(2,1)S(1)}, u32[]{:S(2)}, u32[]{:S(2)}) collective-permute-start(bf16[128,128]{1,0:T(8,128)(2,1)S(1)} %bitcast.13), channel_id=1, source_target_pairs={{1,0},{2,1},{3,2},{4,3},{5,4},{6,5},{7,6},{8,7},{9,8},{10,9},{11,1... | collective-permute-start | bytes 98312 | tf_op jit(solution)/shard_map/ppermute | solution.py:515
  63.0 5.2 %collective-permute-done.above_ref = bf16[128,128]{1,0:T(8,128)(2,1)S(1)} collective-permute-done((bf16[128,128]{1,0:T(8,128)(2,1)S(1)}, bf16[128,128]{1,0:T(8,128)(2,1)S(1)}, u32[]{:S(2)}, u32[]{:S(2)}) %collective-permute-start) | collective-permute-done | bytes 32800 | tf_op jit(solution)/shard_map/ppermute | solution.py:515
  68.1 0.6 blend.1
Async XLA Ops:
  1.7 21.6 %all-to-all-start = ((bf16[16,2,2,2,8,128]{5,4,3,2,1,0:T(8,128)(2,1)}), bf16[16,2,2,2,8,128]{5,4,3,2,1,0:T(8,128)(2,1)S(1)}, u32[]{:S(2)}, u32[]{:S(2)}) async-start(bf16[16,2,2,2,8,128]{5,4,3,2,1,0:T(8,128)(2,1)} %bitcast.10), calls=%async_computation | async-start | bytes 524288 | tf_op jit(solution)/shard_map/all_to_all | solution.py:416
  60.2 7.9 %collective-permute-start = (bf16[128,128]{1,0:T(8,128)(2,1)S(1)}, bf16[128,128]{1,0:T(8,128)(2,1)S(1)}, u32[]{:S(2)}, u32[]{:S(2)}) collective-permute-start(bf16[128,128]{1,0:T(8,128)(2,1)S(1)} %bitcast.13), channel_id=1, source_target_pairs={{1,0},{2,1},{3,2},{4,3},{5,4},{6,5},{7,6},{8,7},{9,8},{10,9},{11,1... | collective-permute-start | bytes 98312 | tf_op jit(solution)/shard_map/ppermute | solution.py:515

commit v11 on v10

--- a/solution.py
+++ b/solution.py
@@ -269,7 +269,8 @@
 
 def weights_kernel(whole_ref, real_ref, out_ref):
     def chunk(step, carry):
-        out_ref[step] = range_columns(whole_ref, real_ref, 2 * step, out_ref.shape[1])
+        ahead = jnp.where(step < 8, 2 * step, 2 * step - 15)
+        out_ref[step] = range_columns(whole_ref, real_ref, ahead, out_ref.shape[1])
         return carry
 
     lax.fori_loop(0, out_ref.shape[0], chunk, 0)
@@ -340,7 +341,12 @@
         for i in range(2):
             step = quarter * 4 + 2 * i
             chunk(quarter, step, column_ref[quarter * 2 + i])
-            chunk(quarter, step + 1, range_columns(whole_ref, real_ref, step + 1, width))
+            columns = (
+                column_ref[8 + i]
+                if quarter == 0
+                else range_columns(whole_ref, real_ref, step + 1, width)
+            )
+            chunk(quarter, step + 1, columns)
     for group in range(ROWS // 32):
         ordered = [
             swap_quarters(
@@ -471,7 +477,7 @@
     )
     columns = pl.pallas_call(
         weights_kernel,
-        out_shape=kept((row_count // 8, width, 4 * LANES), bf16),
+        out_shape=kept((row_count // 8 + 2, width, 4 * LANES), bf16),
         in_specs=[vmem, vmem],
         out_specs=vmem,
         compiler_params=limit,

time: 69.1 us -> 69.1 us (level)
  no operation moved by 1% of the time
where the time goes in v11:
time: 69.1 us; the launch traced here: 68.7 us
  blocking collectives  34.6 us (50%)
  starting transfers between devices  13.1 us (19%)
  waiting for transfers between devices  12.9 us (19%)
  Pallas kernels  5.69 us (8%)
  local copies, waits for them, and re-layouts  1.67 us (2%)
    all_to_all x1, blocking collectives, body(): tiles = lax.all_to_all(tiles, 'sub', 0, 0, tiled=True)  20.9 us
    all_to_all x1, blocking collectives, body(): lax.all_to_all(windows, 'sub', 0, 0, axis_index_groups=halves, tiled=True)  13.7 us
    all_to_all x1, starting transfers between devices, body(): lax.all_to_all(slices, 'sub', 0, 0, axis_index_groups=halves, tiled=True)  10.4 us
    all_to_all x1, waiting for transfers between devices, body(): lax.all_to_all(slices, 'sub', 0, 0, axis_index_groups=halves, tiled=True)  7.74 us
    ppermute x1, waiting for transfers between devices, body(): above = lax.ppermute(tiles, 'hgt', [(i, i - 1) for i in range(1, layers)])  5.17 us
    ppermute x1, starting transfers between devices, body(): above = lax.ppermute(tiles, 'hgt', [(i, i - 1) for i in range(1, layers)])  2.73 us
    pallas_call x1, Pallas kernels, body(): pl.pallas_call(functools.partial(prepare_kernel, range_count=range_count)...  2.17 us
    reshape x1, local copies, waits for them, and re-layouts, body(): polar_beams.reshape(2, beams // 8, 8, members, width // LANES, LANES)  1.67 us
  transfers between devices with their start and end apart: 2, of which 2 were waited for; matrix products, arithmetic and copies ran while one was open for 0% of the time, Pallas kernels for 4%

profile of v11, /device:TPU:6, one launch (start us, length us, event | category | flops | bytes accessed | tf_op | source)
XLA Modules:
  0.0 68.7 jit_solution(100683326665932906)
XLA Ops:
  0.0 1.7 %copy.11 = bf16[2,2,8,16,2,128]{5,2,4,1,0,3:T(8,128)(2,1)} copy(bf16[2,2,8,16,2,128]{5,2,4,3,1,0:T(8,128)(2,1)} %bitcast.15) | data formatting | bytes 524288 | tf_op jit(solution)/shard_map/reshape | solution.py:420
  1.7 10.4 %all-to-all-start = ((bf16[16,2,2,2,8,128]{5,4,3,2,1,0:T(8,128)(2,1)}), bf16[16,2,2,2,8,128]{5,4,3,2,1,0:T(8,128)(2,1)S(1)}, u32[]{:S(2)}, u32[]{:S(2)}) async-start(bf16[16,2,2,2,8,128]{5,4,3,2,1,0:T(8,128)(2,1)} %bitcast.10), calls=%async_computation | async-start | bytes 524288 | tf_op jit(solution)/shard_map/all_to_all | solution.py:422
  12.7 2.2 %prepare.1 = (f32[10,2,16,256]{3,2,1,0:T(8,128)S(1)}, bf16[64,32]{1,0:T(8,128)(2,1)S(1)}, bf16[32,32]{1,0:T(8,128)(2,1)S(1)}, bf16[64,64]{1,0:T(8,128)(2,1)S(1)}...) custom-call(s32[1]{0:T(128)} %bitcast.4.place_ref, ...), custom_call_target="tpu_custom_call" | custom-call | tf_op jit(solution)/shard_map/prepare/pallas_call | solution.py:425
  14.9 0.6 weights.1.before_ref.column_ref
  15.5 7.7 %all-to-all-done = bf16[16,2,2,2,8,128]{5,4,3,2,1,0:T(8,128)(2,1)S(1)} async-done(((bf16[16,2,2,2,8,128]{5,4,3,2,1,0:T(8,128)(2,1)}), bf16[16,2,2,2,8,128]{5,4,3,2,1,0:T(8,128)(2,1)S(1)}, u32[]{:S(2)}, u32[]{:S(2)}) %all-to-all-start) | async-done | bytes 262176 | tf_op jit(solution)/shard_map/all_to_all | solution.py:422
  23.2 0.7 %merge.1 = bf16[16,56,128]{2,1,0:T(8,128)(2,1)S(1)} custom-call(bf16[16,2,16,256]{3,2,1,0:T(8,128)(2,1)S(1)} %bitcast.11, f32[10,2,16,256]{3,2,1,0:T(8,128)S(1)} %get-tuple-element.13.trig_ref, bf16[64,32]{1,0:T(8,128)(2,1)S(1)} %get-tuple-element.14.first_ref, bf16[32,32]{1,0:T(8,128)(2,1)S(1)} %get-tuple-element.15.second_ref, ...), custom_call_target="tpu_custom_call" | custom-call | tf_op jit(solution)/shard_map/merge/pallas_call | solution.py:487
  24.0 13.7 %all_to_all.15.table_ref = bf16[16,56,128]{2,1,0:T(8,128)(2,1)S(1)} all-to-all(bf16[16,56,128]{2,1,0:T(8,128)(2,1)S(1)} %merge.1), channel_id=1, replica_groups={{0,16,64,80,128,144,192,208,256,272,320,336,384,400,448,464},{32,48,96,..., dimensions={0} | all-to-all | bytes 458752 | tf_op jit(solution)/shard_map/all_to_all | solution.py:500
  37.7 1.6 %sample.1 = bf16[128,128]{1,0:T(8,128)(2,1)S(1)} custom-call(bf16[16,56,128]{2,1,0:T(8,128)(2,1)S(1)} %all_to_all.15.table_ref, bf16[10,256,512]{2,1,0:T(8,128)(2,1)S(1)} %weights.1.before_ref.column_ref, s32[3,64,128]{2,1,0:T(8,128)S(1)} %get-tuple-element.17.whole_ref, f32[2,64,128]{2,1,0:T(8,128)S(1)} %get-tuple-element.18.real_ref, ...), custom_call_target="tpu_custom_call" | custom-call | tf_op jit(solution)/shard_map/sample/pallas_call | solution.py:501
  39.3 20.9 %all_to_all.16 = bf16[32,4,128]{2,1,0:T(4,128)(2,1)S(1)} all-to-all(bf16[32,4,128]{2,1,0:T(4,128)(2,1)S(1)} %bitcast.12), channel_id=1, replica_groups=mesh['sub'=32,'hgt'=16] {'sub'}, dimensions={0} | all-to-all | bytes 65536 | tf_op jit(solution)/shard_map/all_to_all | solution.py:519
  60.2 2.7 %collective-permute-start = (bf16[128,128]{1,0:T(8,128)(2,1)S(1)}, bf16[128,128]{1,0:T(8,128)(2,1)S(1)}, u32[]{:S(2)}, u32[]{:S(2)}) collective-permute-start(bf16[128,128]{1,0:T(8,128)(2,1)S(1)} %bitcast.13), channel_id=1, source_target_pairs={{1,0},{2,1},{3,2},{4,3},{5,4},{6,5},{7,6},{8,7},{9,8},{10,9},{11,1... | collective-permute-start | bytes 98312 | tf_op jit(solution)/shard_map/ppermute | solution.py:521
  62.9 5.2 %collective-permute-done.above_ref = bf16[128,128]{1,0:T(8,128)(2,1)S(1)} collective-permute-done((bf16[128,128]{1,0:T(8,128)(2,1)S(1)}, bf16[128,128]{1,0:T(8,128)(2,1)S(1)}, u32[]{:S(2)}, u32[]{:S(2)}) %collective-permute-start) | collective-permute-done | bytes 32800 | tf_op jit(solution)/shard_map/ppermute | solution.py:521
  68.1 0.6 blend.1
Async XLA Ops:
  1.7 21.6 %all-to-all-start = ((bf16[16,2,2,2,8,128]{5,4,3,2,1,0:T(8,128)(2,1)}), bf16[16,2,2,2,8,128]{5,4,3,2,1,0:T(8,128)(2,1)S(1)}, u32[]{:S(2)}, u32[]{:S(2)}) async-start(bf16[16,2,2,2,8,128]{5,4,3,2,1,0:T(8,128)(2,1)} %bitcast.10), calls=%async_computation | async-start | bytes 524288 | tf_op jit(solution)/shard_map/all_to_all | solution.py:422
  60.2 7.9 %collective-permute-start = (bf16[128,128]{1,0:T(8,128)(2,1)S(1)}, bf16[128,128]{1,0:T(8,128)(2,1)S(1)}, u32[]{:S(2)}, u32[]{:S(2)}) collective-permute-start(bf16[128,128]{1,0:T(8,128)(2,1)S(1)} %bitcast.13), channel_id=1, source_target_pairs={{1,0},{2,1},{3,2},{4,3},{5,4},{6,5},{7,6},{8,7},{9,8},{10,9},{11,1... | collective-permute-start | bytes 98312 | tf_op jit(solution)/shard_map/ppermute | solution.py:521
